TPU v7x, 256 devices: a whole 4x4x8 slice. The times are simulated.
256 devices in a mesh: grp: 8 (over y, x_lo), brick: 32 (over z, x_hi, core).
Axes of the slice: x: 4 (x_hi: 2, x_lo: 2; x = x_hi * 2 + x_lo), y: 4, z: 8, core: 2. Of those that a mesh axis runs over, the one named last changes fastest.
Arguments:
- coeffs: bfloat16 [8, 16384, 1024], P(None, 'brick'), may hold values from -6 to 6
- tensor: bfloat16 [32, 1024, 1024], P('grp', 'brick'), may hold values from -0.005859375 to 0.005859375
- pairs: int32 [2, 2], replicated, may hold values from 0 to 7
- lateral: int32 [16384], P('brick'), may hold values from 0 to 511
- thermal: float32 [8], replicated, may hold values from 0.5 to 1
Outputs:
- updated: float32 [32, 8, 16384], P(None, None, 'brick')
Inputs may be any that keep to these rules, and one draw needn't show every extreme that they name: `pairs`: row p names the species that receives the collision term and the species it collides with. A cell's lateral partner, as an index within the same block of 512 cells.
All inputs are finite; a program needn't handle non-finite values.
Results may differ from a plain program's by a relative error of at most 0.0003.
Values may be sent and summed in bfloat16 or wider, within the bound.
No kernel may reach another device: no remote copies, remote signals or barrier semaphores. Data moves between devices by JAX's collectives and lax.ppermute only.
A program may use at most 128 MiB of HBM per device.

v0:
```python
import jax
import jax.numpy as jnp
from jax import lax
from jax.sharding import PartitionSpec as P

PLANE = 128


collision_update = 0.5
courant = 0.08
max_speed = 11.0
mixing = 0.2


def sent_to_all(array, axis):
    copies = jnp.broadcast_to(array, (lax.axis_size(axis), *array.shape))
    return lax.all_to_all(copies, axis, split_axis=0, concat_axis=0, tiled=True)


def in_order(parts, dim):
    shape = list(parts.shape[1:])
    shape[dim] *= parts.shape[0]
    return jnp.moveaxis(parts, 0, dim).reshape(shape)


def gather_directly(array, axis, dim):
    parts = sent_to_all(array, axis)
    return in_order(parts, dim)


def with_halo(cells, sides, width):
    for axis, dim in sides:
        count = lax.axis_size(axis)
        head = lax.slice_in_dim(cells, 0, width, axis=dim)
        tail = lax.slice_in_dim(cells, cells.shape[dim] - width, cells.shape[dim], axis=dim)
        cells = jnp.concatenate(
            [
                lax.ppermute(tail, axis, [(i, (i + 1) % count) for i in range(count)]),
                cells,
                lax.ppermute(head, axis, [((i + 1) % count, i) for i in range(count)]),
            ],
            axis=dim,
        )
    return cells


def advance(extended, thermal, partner):
    mode_count = extended.shape[0] - 2
    thermo = thermal[None, :, None, None]
    orders = jnp.arange(mode_count, dtype=jnp.int32).astype(jnp.float32)[:, None, None, None]
    speed = thermo * (
        jnp.sqrt(orders) * extended[:mode_count] + jnp.sqrt(orders + 1.0) * extended[2:]
    )
    middle = extended[1 : mode_count + 1]
    face = 0.5 * (speed[:, :, :-1] + speed[:, :, 1:]) - 0.5 * max_speed * thermo * (
        middle[:, :, 1:] - middle[:, :, :-1]
    )
    center = middle[:, :, 1:-1]
    shape_flat = (mode_count, center.shape[1], center.shape[2] * center.shape[3])
    center = center.reshape(shape_flat)
    divergence = (face[:, :, 1:] - face[:, :, :-1]).reshape(shape_flat)
    beside = jnp.take(center, partner, axis=2)
    return center - courant * divergence + mixing * (beside - center)


def local(coeffs, tensor, pairs, lateral, thermal):
    species, cells, width = coeffs.shape
    local_modes = tensor.shape[0]
    group_count = lax.axis_size("grp")
    modes = local_modes * group_count
    pair_count = pairs.shape[0]
    layers = cells // PLANE
    left_rows = jnp.transpose(coeffs[pairs[:, 0]], (2, 0, 1))
    right_flat = coeffs[pairs[:, 1]].reshape(pair_count * cells, width)
    brick_window = jnp.transpose(coeffs[:, :, :modes], (2, 0, 1))
    padded_state = jnp.pad(brick_window, ((1, 1), (0, 0), (0, 0)))
    indicator_matrix = (
        pairs[:, 0][:, None] == jnp.arange(species, dtype=jnp.int32)[None, :]
    ).astype(jnp.float32)
    piece = lax.all_gather(tensor, "brick", axis=1, tiled=True)
    rows_here = piece.shape[1]
    inner = lax.dot_general(
        piece.reshape(local_modes * rows_here, width),
        right_flat,
        (((1,), (1,)), ((), ())),
        preferred_element_type=jnp.float32,
    )
    inner = inner.reshape(local_modes, rows_here, pair_count, cells)
    factor = left_rows.astype(jnp.float32)
    collide = jnp.sum(inner * factor[None], axis=1)
    pair_all = gather_directly(collide, "grp", 0)
    pair_extended = jnp.pad(pair_all, ((1, 1), (0, 0), (0, 0)))
    span = pair_extended.shape[0]
    collision_extended = jnp.einsum(
        "quw,ut->qtw", pair_extended, indicator_matrix, precision=lax.Precision.HIGHEST
    )
    species_state = padded_state.astype(jnp.float32) + collision_update * collision_extended
    extended = with_halo(species_state.reshape(span, species, layers, PLANE), (("brick", 2),), 1)
    updated = advance(extended, thermal, lateral)
    return updated


def solution(mesh):
    in_specs = (P(None, "brick", None), P("grp", "brick", None), P(), P("brick"), P())
    out_specs = P(None, None, "brick")
    return jax.shard_map(local, mesh=mesh, in_specs=in_specs, out_specs=out_specs, check_vma=False)
```

profile of v0, /device:TPU:1, one launch (start us, length us, event | category | flops | bytes accessed | tf_op | source)
XLA Modules:
  0.0 193.7 jit_solution(13047162379919570659)
XLA Ops:
  6.5 0.0 all-gather.2.cloned.1.call-start
  6.5 0.7 all-gather.2.cloned.1.call-update
  7.3 1.0 slice_reduce_fusion
  8.2 0.0 slice-start
  8.3 0.0 copy-start
  8.3 5.5 %gather_fusion = bf16[2,512,1024]{2,1,0:T(8,128)(2,1)} fusion(bf16[8,512,1024]{2,1,0:T(8,128)(2,1)} %param.5, s32[1024]{0:T(1024)S(1)} %get-tuple-element.11), kind=kCustom, calls=%fused_computation | custom fusion | bytes 4194312 | tf_op jit(solution)/shard_map/gather | solution.py:74
  13.8 4.1 %gather_fusion.1 = bf16[2,512,1024]{2,1,0:T(8,128)(2,1)S(1)} fusion(bf16[8,512,1024]{2,1,0:T(8,128)(2,1)} %param.5, s32[1024]{0:T(1024)S(1)} %get-tuple-element.10), kind=kCustom, calls=%fused_computation.1 | custom fusion | bytes 4194312 | tf_op jit(solution)/shard_map/gather | solution.py:73
  17.8 0.0 slice-done
  17.8 0.5 copy.14
  18.4 2.5 %convert_bitcast_fusion = f32[1024,2,512]{0,2,1:T(8,128)} fusion(bf16[2,512,1024]{2,1,0:T(8,128)(2,1)S(1)} %gather_fusion.1), kind=kLoop, calls=%fused_computation.5 | loop fusion | flops 1048576 | bytes 6291456 | tf_op jit(solution)/shard_map/convert_element_type | solution.py:89
  20.9 94.9 %all-gather.2.cloned.1.call-done = bf16[4,1024,1024]{2,1,0:T(8,128)(2,1)} async-done(((bf16[4,32,1024]{2,1,0:T(8,128)(2,1)}), bf16[4,1024,1024]{2,1,0:T(8,128)(2,1)}) %all-gather.2.cloned.1.call-update) | async-done | bytes 8388624 | tf_op jit(solution)/shard_map/all_gather | solution.py:80
  115.8 16.0 %convolution_bitcast_fusion = f32[4096,1024]{0,1:T(8,128)} fusion(bf16[1024,1024]{1,0:T(8,128)(2,1)} %bitcast.35, bf16[4096,1024]{1,0:T(8,128)(2,1)} %bitcast.38), kind=kOutput, calls=%fused_computation.4 | convolution fusion | flops 8589934592 | bytes 27262976 | tf_op jit(solution)/shard_map/dot_general | solution.py:82
  131.9 20.4 %reshape.44 = f32[4,1024,2,512]{1,0,3,2:T(4,128)} reshape(f32[4096,1024]{0,1:T(8,128)} %convolution_bitcast_fusion) | data formatting | bytes 33554432 | tf_op jit(solution)/shard_map/reshape | solution.py:88
  152.3 10.5 %multiply_reduce_fusion = f32[4,2,512]{0,2,1:T(8,128)S(1)} fusion(f32[4,1024,2,512]{1,0,3,2:T(4,128)} %reshape.44, f32[1024,2,512]{0,2,1:T(8,128)} %convert_bitcast_fusion), kind=kLoop, calls=%fused_computation.3 | loop fusion | flops 8384512 | bytes 20987904 | tf_op jit(solution)/shard_map/reduce_sum | solution.py:90
  162.8 0.2 copy.11
  163.0 0.7 broadcast_in_dim.21
  163.7 4.0 %all-to-all-start = ((f32[8,4,2,512]{3,2,1,0:T(2,128)}), f32[8,4,2,512]{3,2,1,0:T(2,128)S(1)}, u32[]{:S(2)}, u32[]{:S(2)}) async-start(f32[8,4,2,512]{3,2,1,0:T(2,128)} %broadcast_in_dim.21), calls=%async_computation | async-start | bytes 262144 | tf_op jit(solution)/shard_map/all_to_all | solution.py:17
  167.8 0.0 copy-done.1
  167.8 5.7 %all-to-all-done = f32[8,4,2,512]{3,2,1,0:T(2,128)S(1)} async-done(((f32[8,4,2,512]{3,2,1,0:T(2,128)}), f32[8,4,2,512]{3,2,1,0:T(2,128)S(1)}, u32[]{:S(2)}, u32[]{:S(2)}) %all-to-all-start) | async-done | bytes 131104 | tf_op jit(solution)/shard_map/all_to_all | solution.py:17
  173.5 0.5 fusion.1
  174.0 0.7 fusion.21
  174.7 3.2 %collective-permute-start = (f32[34,8,1,128]{3,1,2,0:T(8,128)}, f32[34,8,1,128]{3,1,2,0:T(8,128)S(1)}, u32[]{:S(2)}, u32[]{:S(2)}) collective-permute-start(f32[34,8,1,128]{3,1,2,0:T(8,128)} %get-tuple-element.9), channel_id=1, source_target_pairs={{0,1},{1,2},{2,3},{3,4},{4,5},{5,6},{6,7},{7,8},{8,9},{9,10},{10,1... | collective-permute-start | bytes 417800 | tf_op jit(solution)/shard_map/ppermute | solution.py:38
  177.9 0.0 collective-permute-start.1
  178.0 0.8 copy.12
  178.8 2.7 %gather_fusion.2 = f32[512,32,8]{1,2,0:T(8,128)} fusion(f32[32,8,512]{0,1,2:T(8,128)S(1)} %copy.12, s32[1024]{0:T(1024)S(1)} %pad_clamp_fusion), kind=kCustom, calls=%fused_computation.2 | custom fusion | bytes 1050624 | tf_op jit(solution)/shard_map/jit(_take)/gather | solution.py:62
  181.5 2.4 %copy.13 = f32[512,32,8]{0,2,1:T(8,128)S(1)} copy(f32[512,32,8]{1,2,0:T(8,128)} %gather_fusion.2) | data formatting | bytes 1048576 | tf_op jit(solution)/shard_map/jit(_take)/gather | solution.py:62
  183.9 0.0 collective-permute-done
  184.0 1.4 collective-permute-done.1
  185.3 0.1 pad_maximum_fusion
  185.4 0.2 fusion.3
  185.6 0.3 fusion.6
  185.9 1.0 fusion.11
  (9 shorter events, 0.1 us)
Async XLA Ops:
  6.5 109.3 %all-gather.2.cloned.1.call-start = ((), (), s32[]{:S(2)}) async-start(), calls=%async_computation.1 | async-start | bytes 8650752 | tf_op jit(solution)/shard_map/all_gather | solution.py:80
  8.2 9.6 %slice-start = ((bf16[8,512,1024]{2,1,0:T(8,128)(2,1)}), bf16[8,512,32]{2,1,0:T(8,128)(2,1)S(1)}, s32[]{:S(2)}) async-start(bf16[8,512,1024]{2,1,0:T(8,128)(2,1)} %param.5), calls=%async_computation.2 | async-start | bytes 2097152 | tf_op jit(solution)/shard_map/slice | solution.py:75
  8.3 10.1 %copy-start = (s32[512]{0:T(512)S(1)}, s32[512]{0:T(512)}, u32[]{:S(2)}) copy-start(s32[512]{0:T(512)} %param.8) | copy-start | bytes 6148
  152.3 15.4 %copy-start.1 = (f32[8]{0:T(128)S(1)}, f32[8]{0:T(128)}, u32[]{:S(2)}) copy-start(f32[8]{0:T(128)} %param.9) | copy-start | bytes 100
  163.7 9.7 %all-to-all-start = ((f32[8,4,2,512]{3,2,1,0:T(2,128)}), f32[8,4,2,512]{3,2,1,0:T(2,128)S(1)}, u32[]{:S(2)}, u32[]{:S(2)}) async-start(f32[8,4,2,512]{3,2,1,0:T(2,128)} %broadcast_in_dim.21), calls=%async_computation | async-start | bytes 262144 | tf_op jit(solution)/shard_map/all_to_all | solution.py:17
  174.7 9.2 %collective-permute-start = (f32[34,8,1,128]{3,1,2,0:T(8,128)}, f32[34,8,1,128]{3,1,2,0:T(8,128)S(1)}, u32[]{:S(2)}, u32[]{:S(2)}) collective-permute-start(f32[34,8,1,128]{3,1,2,0:T(8,128)} %get-tuple-element.9), channel_id=1, source_target_pairs={{0,1},{1,2},{2,3},{3,4},{4,5},{5,6},{6,7},{7,8},{8,9},{9,10},{10,1... | collective-permute-start | bytes 417800 | tf_op jit(solution)/shard_map/ppermute | solution.py:38
  177.9 7.4 %collective-permute-start.1 = (f32[34,8,1,128]{3,1,2,0:T(8,128)}, f32[34,8,1,128]{3,1,2,0:T(8,128)S(1)}, u32[]{:S(2)}, u32[]{:S(2)}) collective-permute-start(f32[34,8,1,128]{3,1,2,0:T(8,128)} %get-tuple-element.8), channel_id=1, source_target_pairs={{1,0},{2,1},{3,2},{4,3},{5,4},{6,5},{7,6},{8,7},{9,8},{10,9},{11,1... | collective-permute-start | bytes 417800 | tf_op jit(solution)/shard_map/ppermute | solution.py:40
Sparse Core Ops, SparseCore 0:
  10.2 105.6 all-gather.1
where the time goes:
time: 195 us; the launch traced here: 194 us
  waiting for transfers between devices  103 us (53%)
  local copies, waits for them, and re-layouts  38.2 us (20%)
  matrix products  16.6 us (9%)
  other arithmetic  15.5 us (8%)
  between operations  13.5 us (7%)
  starting transfers between devices  7.19 us (4%)
    all_gather x1, waiting for transfers between devices, local(): piece = lax.all_gather(tensor, 'brick', axis=1, tiled=True)  94.9 us
    reshape x1, local copies, waits for them, and re-layouts, local(): inner = inner.reshape(local_modes, rows_here, pair_count, cells)  20.4 us
    dot_general x1, matrix products, local(): lax.dot_general(piece.reshape(local_modes * rows_here, width), right_flat...  16 us
    reduce_sum x1, other arithmetic, local(): collide = jnp.sum(inner * factor[None], axis=1)  10.5 us
    all_to_all x1, waiting for transfers between devices, sent_to_all(): return lax.all_to_all(copies, axis, split_axis=0, concat_axis=0, tiled=True)  5.71 us
    gather x1, local copies, waits for them, and re-layouts, local(): right_flat = coeffs[pairs[:, 1]].reshape(pair_count * cells, width)  5.5 us
    gather x2, local copies, waits for them, and re-layouts, advance(): beside = jnp.take(center, partner, axis=2)  5.12 us
    gather x1, local copies, waits for them, and re-layouts, local(): left_rows = jnp.transpose(coeffs[pairs[:, 0]], (2, 0, 1))  4.06 us
  transfers between devices with their start and end apart: 4, of which 3 were waited for; matrix products, arithmetic and copies ran while one was open for 10% of the time, Pallas kernels for 0%

commit v1 on v0

v1 whole, which is shorter than its diff:
```python
import functools

import jax
import jax.numpy as jnp
from jax import lax
from jax.experimental import pallas as pl
from jax.experimental.pallas import tpu as pltpu
from jax.sharding import Mesh, PartitionSpec as P

PLANE = 128
Y, XL, Z, XH, CORE = 4, 2, 8, 2, 2
FINE = ("y", "xl", "z", "xh", "core")
BRICK = ("z", "xh", "core")
MODES_HERE = 4
ROWS = 32

collision_update = 0.5
courant = 0.08
max_speed = 11.0
mixing = 0.2

UP = [(i, (i + 1) % Z) for i in range(Z)]
DOWN = [((i + 1) % Z, i) for i in range(Z)]
SWAP = [(0, 1), (1, 0)]


def prepare_kernel(place, pairs, left, right, right_out, keep, send):
    core = place[2]
    right_out[...] = right[...]
    turned = jnp.transpose(left[0]).reshape(Z * XH, CORE, ROWS, left.shape[1])

    @pl.when(core == 0)
    def _():
        keep[0] = turned[:, 0]
        send[0] = turned[:, 1]

    @pl.when(core == 1)
    def _():
        keep[0] = turned[:, 1]
        send[0] = turned[:, 0]


def prepare(place, pairs, coeffs):
    _, cells, width = coeffs.shape
    halves = jax.ShapeDtypeStruct((2, Z * XH, ROWS, cells), coeffs.dtype)
    half_spec = pl.BlockSpec((1, Z * XH, ROWS, cells), lambda p, place, pairs: (p, 0, 0, 0))
    return pl.pallas_call(
        prepare_kernel,
        grid_spec=pltpu.PrefetchScalarGridSpec(
            num_scalar_prefetch=2,
            grid=(2,),
            in_specs=[
                pl.BlockSpec((1, cells, width), lambda p, place, pairs: (pairs[p, 0], 0, 0)),
                pl.BlockSpec((1, cells, width), lambda p, place, pairs: (pairs[p, 1], 0, 0)),
            ],
            out_specs=[
                pl.BlockSpec((1, cells, width), lambda p, place, pairs: (p, 0, 0)),
                half_spec,
                half_spec,
            ],
        ),
        out_shape=[jax.ShapeDtypeStruct((2, cells, width), coeffs.dtype), halves, halves],
        compiler_params=pltpu.CompilerParams(vmem_limit_bytes=40 * 2**20),
        name="prepare",
    )(place, pairs, coeffs, coeffs)


TILE = 256


def collide_kernel(pieces, n_more, last, place, *refs):
    n = len(pieces)
    xs = refs[:n]
    right_own, right_sib, left_own, left_sib = refs[n : n + 4]
    more = refs[n + 4 : n + 4 + n_more]
    out, stacked = refs[n + 4 + n_more :]
    source = pl.program_id(0)
    z, xh = place[0], place[1]

    @pl.when(source == 0)
    def _():
        row = 0
        for x in xs:
            rows = x.shape[0] * x.shape[1] * x.shape[2]
            stacked[pl.ds(row, rows), :] = x[...].reshape(rows, x.shape[3])
            row += rows

    def work(right, left):
        cells = right.shape[1]
        for p in range(2):
            for t in range(cells // TILE):
                at = pl.ds(t * TILE, TILE)
                inner = lax.dot_general(
                    stacked[...],
                    right[p, at, :],
                    (((1,), (1,)), ((), ())),
                    preferred_element_type=jnp.float32,
                )
                sums = [None] * MODES_HERE
                row = 0
                for x, (first, blocks) in zip(xs, pieces):
                    for flip, offset, fixed in blocks:
                        here = fixed if offset is None else lax.rem(z + (offset + Z), Z)
                        column = xh if not flip else 1 - xh
                        factor = left[p, here * XH + column, :, at].astype(jnp.float32)
                        for k in range(x.shape[1]):
                            term = inner[row : row + ROWS] * factor
                            row += ROWS
                            term = (term[0:8] + term[8:16]) + (term[16:24] + term[24:32])
                            m = first + k
                            sums[m] = term if sums[m] is None else sums[m] + term
                done = jnp.concatenate([jnp.sum(s, axis=0, keepdims=True) for s in sums], axis=0)
                for m in more:
                    done = done + m[0, p * MODES_HERE : (p + 1) * MODES_HERE, at]
                if last:
                    for g in range(out.shape[0]):
                        out[g, 0, p * MODES_HERE : (p + 1) * MODES_HERE, at] = done
                else:
                    out[0, p * MODES_HERE : (p + 1) * MODES_HERE, at] = done

    @pl.when(source == 0)
    def _():
        work(right_own, left_own)

    @pl.when(source == 1)
    def _():
        work(right_sib, left_sib)


def collide_part(place, xs, pieces, right_own, right_sib, left_own, left_sib, more=(), last=False):
    _, cells, width = right_own.shape
    rows = sum(x.shape[0] * x.shape[1] * x.shape[2] for x in xs)
    whole = lambda a: pl.BlockSpec(a.shape, lambda s, place: (0,) * a.ndim)
    if last:
        groups = Y * XL
        out_spec = pl.BlockSpec(
            (groups, 1, 2 * MODES_HERE, cells),
            lambda s, place: (0, jnp.where(s == 0, place[2], 1 - place[2]), 0, 0),
        )
        out_shape = jax.ShapeDtypeStruct((groups, CORE, 2 * MODES_HERE, cells), jnp.float32)
    else:
        out_spec = pl.BlockSpec((1, 2 * MODES_HERE, cells), lambda s, place: (s, 0, 0))
        out_shape = jax.ShapeDtypeStruct((2, 2 * MODES_HERE, cells), jnp.float32)
    return pl.pallas_call(
        functools.partial(collide_kernel, pieces, len(more), last),
        grid_spec=pltpu.PrefetchScalarGridSpec(
            num_scalar_prefetch=1,
            grid=(2,),
            in_specs=[whole(a) for a in (*xs, right_own, right_sib, left_own, left_sib)]
            + [pl.BlockSpec((1, 2 * MODES_HERE, cells), lambda s, place: (s, 0, 0)) for _ in more],
            out_specs=out_spec,
            scratch_shapes=[pltpu.VMEM((rows, width), jnp.bfloat16)],
        ),
        out_shape=out_shape,
        compiler_params=pltpu.CompilerParams(vmem_limit_bytes=48 * 2**20),
        cost_estimate=pl.CostEstimate(
            flops=2 * rows * 4 * cells * width, transcendentals=0, bytes_accessed=8 * cells * width
        ),
        name="collide",
    )(place, *xs, right_own, right_sib, left_own, left_sib, *more)


def finish_kernel(pairs, thermal, parts, before, after, window, window_before, window_after, onehot, out, state):
    modes, species, cells = window.shape
    span = cells + 2 * PLANE
    row = lax.broadcasted_iota(jnp.int32, (species, span), 0)
    gain = [
        jnp.where(row == pairs[p, 0], jnp.float32(collision_update), jnp.float32(0.0)) for p in range(2)
    ]
    for g in range(Y * XL):
        own = parts[g, 0] + parts[g, 1]
        both = jnp.concatenate([before[g], own, after[g]], axis=1)
        for k in range(MODES_HERE):
            m = g * MODES_HERE + k
            kept = jnp.concatenate([window_before[m], window[m], window_after[m]], axis=1).astype(jnp.float32)
            for p in range(2):
                r = p * MODES_HERE + k
                kept = kept + gain[p] * both[r : r + 1]
            state[m] = kept
    srow = lax.broadcasted_iota(jnp.int32, (species, cells), 0)
    th = jnp.zeros((species, cells), jnp.float32)
    for s in range(species):
        th = jnp.where(srow == s, thermal[s], th)
    centre = state[:, :, PLANE : PLANE + cells]
    flat = centre.reshape(modes * species, cells)
    high = flat.astype(jnp.bfloat16)
    rest = flat - high.astype(jnp.float32)
    middle = rest.astype(jnp.bfloat16)
    low = (rest - middle.astype(jnp.float32)).astype(jnp.bfloat16)
    pick = onehot[...]
    beside = (
        jnp.dot(low, pick, preferred_element_type=jnp.float32)
        + jnp.dot(middle, pick, preferred_element_type=jnp.float32)
    ) + jnp.dot(high, pick, preferred_element_type=jnp.float32)
    beside = beside.reshape(modes, species, cells)
    for k in range(modes):
        here = state[k, :, PLANE : PLANE + cells]
        ahead = state[k, :, 2 * PLANE :]
        behind = state[k, :, :cells]
        drift = jnp.zeros((species, cells), jnp.float32)
        if k > 0:
            drift += (float(k) ** 0.5) * (state[k - 1, :, 2 * PLANE :] - state[k - 1, :, :cells])
        if k < modes - 1:
            drift += (float(k + 1) ** 0.5) * (state[k + 1, :, 2 * PLANE :] - state[k + 1, :, :cells])
        divergence = th * (0.5 * drift - (0.5 * max_speed) * ((ahead - here) - (here - behind)))
        out[k] = here - courant * divergence + mixing * (beside[k] - here)


def finish(pairs, thermal, parts, before, after, window, window_before, window_after, onehot):
    modes, species, cells = window.shape
    vmem = pl.BlockSpec(memory_space=pltpu.VMEM)
    smem = pl.BlockSpec(memory_space=pltpu.SMEM)
    return pl.pallas_call(
        finish_kernel,
        in_specs=[smem, smem] + [vmem] * 7,
        out_specs=vmem,
        out_shape=jax.ShapeDtypeStruct((modes, species, cells), jnp.float32),
        scratch_shapes=[pltpu.VMEM((modes, species, cells + 2 * PLANE), jnp.float32)],
        compiler_params=pltpu.CompilerParams(vmem_limit_bytes=40 * 2**20),
        name="finish",
    )(pairs, thermal, parts, before, after, window, window_before, window_after, onehot)


def local(coeffs, tensor, pairs, lateral, thermal):
    species, cells, width = coeffs.shape
    modes = tensor.shape[0] * Y * XL
    bricks = Z * XH * CORE
    place = jnp.stack([lax.axis_index("z"), lax.axis_index("xh"), lax.axis_index("core")]).astype(jnp.int32)
    onward = [(i, (i + 1) % bricks) for i in range(bricks)]
    backward = [((i + 1) % bricks, i) for i in range(bricks)]

    column = lax.all_gather(tensor, "z", axis=0, tiled=False)

    other = [lax.ppermute(tensor[2 * h : 2 * h + 2], "xh", SWAP)[None] for h in range(2)]
    right_own, left_own, left_send = prepare(place, pairs, coeffs)
    right_sib = lax.ppermute(right_own, "core", SWAP)
    left_sib = lax.ppermute(left_send, "core", SWAP)

    near, far = [], []
    for h in range(2):
        first = 2 * h
        near.append((other[h], (first, ((True, 0, None),))))
        up = down = other[h]
        for s in range(1, 4 + (h == 0)):
            up = lax.ppermute(up, "z", UP)
            (near if s <= 2 else far).append((up, (first, ((True, -s, None),))))
        for s in range(1, 4 + (h == 1)):
            down = lax.ppermute(down, "z", DOWN)
            (near if s <= 2 else far).append((down, (first, ((True, s, None),))))

    window = jnp.transpose(coeffs[:, :, :modes], (2, 0, 1))
    window_before = lax.ppermute(window[:, :, cells - PLANE :], BRICK, onward)
    window_after = lax.ppermute(window[:, :, :PLANE], BRICK, backward)
    onehot = (lax.broadcasted_iota(jnp.int32, (cells, cells), 0) == lateral[None, :]).astype(jnp.bfloat16)

    sides = (right_own, right_sib, left_own, left_sib)
    part1 = collide_part(place, [a for a, _ in near], tuple(d for _, d in near), *sides)
    part2 = collide_part(place, [a for a, _ in far], tuple(d for _, d in far), *sides)
    whole = (0, tuple((False, None, b) for b in range(Z)))
    parts = collide_part(place, [column], (whole,), *sides, more=(part1, part2), last=True)

    parts = parts.reshape(Y * XL * CORE, 2 * MODES_HERE, cells)
    parts = lax.all_to_all(parts, ("y", "xl", "core"), split_axis=0, concat_axis=0, tiled=True)
    parts = parts.reshape(Y * XL, CORE, 2 * MODES_HERE, cells)
    first = parts[:, 0, :, :PLANE] + parts[:, 1, :, :PLANE]
    final = parts[:, 0, :, cells - PLANE :] + parts[:, 1, :, cells - PLANE :]
    before = lax.ppermute(final, BRICK, onward)
    after = lax.ppermute(first, BRICK, backward)
    return finish(pairs, thermal, parts, before, after, window, window_before, window_after, onehot)


def solution(mesh):
    fine = Mesh(mesh.devices.reshape(Y, XL, Z, XH, CORE), FINE)
    in_specs = (P(None, BRICK, None), P(("y", "xl"), BRICK, None), P(), P(BRICK), P())
    out_specs = P(None, None, BRICK)
    return jax.shard_map(local, mesh=fine, in_specs=in_specs, out_specs=out_specs, check_vma=False)
```

time: 195 us -> 125 us (0.64)
  waiting for transfers between devices: 103 us -> 44.8 us
  local copies, waits for them, and re-layouts: 38.2 us -> 8.87 us
  starting transfers between devices: 7.19 us -> 35.2 us
  Pallas kernels: 0 us -> 21.4 us
  matrix products: 16.6 us -> 0 us
  other arithmetic: 15.5 us -> 0.22 us
    all_gather x1, waiting for transfers between devices: 94.9 us -> 0.02 us  [local(): column = lax.all_gather(tensor, 'z', axis=0, tiled=False)]
    ppermute x2 -> x22, waiting for transfers between devices: 1.39 us -> 39.9 us  [the longest x7 19.9 us: local(): up = lax.ppermute(up, 'z', UP)]
    ppermute x2 -> x22, starting transfers between devices: 3.17 us -> 26.6 us  [the longest x7 13.6 us: local(): down = lax.ppermute(down, 'z', DOWN)]
    pallas_call x0 -> x5, Pallas kernels: none -> 21.4 us  [the longest x3 17.8 us: collide_part(): pl.pallas_call(functools.partial(collide_kernel, pieces, len(more), last)...]
    reshape x1 -> x0, local copies, waits for them, and re-layouts: 20.4 us -> none  [local(): inner = inner.reshape(local_modes, rows_here, pair_count, cells)]
    dot_general x2 -> x0, matrix products: 16.6 us -> none  [the longest x1 16 us: local(): lax.dot_general(piece.reshape(local_modes * rows_here, width), right_flat...]
    gather x4 -> x0, local copies, waits for them, and re-layouts: 14.7 us -> none  [the longest x1 5.5 us: local(): right_flat = coeffs[pairs[:, 1]].reshape(pair_count * cells, width)]
    reduce_sum x1 -> x0, other arithmetic: 10.5 us -> none  [local(): collide = jnp.sum(inner * factor[None], axis=1)]
  transfers between devices with their start and end apart: 4 -> 24, of which waited for: 3 -> 15; matrix products, arithmetic and copies ran while one was open for 10% -> 1% of each run, Pallas kernels for 0% -> 9%
where the time goes in v1:
time: 125 us; the launch traced here: 124 us
  waiting for transfers between devices  44.8 us (36%)
  starting transfers between devices  35.2 us (28%)
  Pallas kernels  21.4 us (17%)
  between operations  13.6 us (11%)
  local copies, waits for them, and re-layouts  8.87 us (7%)
    ppermute x7, waiting for transfers between devices, local(): up = lax.ppermute(up, 'z', UP)  19.9 us
    pallas_call x3, Pallas kernels, collide_part(): pl.pallas_call(functools.partial(collide_kernel, pieces, len(more), last)...  17.8 us
    ppermute x7, starting transfers between devices, local(): down = lax.ppermute(down, 'z', DOWN)  13.6 us
    ppermute x7, waiting for transfers between devices, local(): down = lax.ppermute(down, 'z', DOWN)  9.31 us
    unnamed x23, local copies, waits for them, and re-layouts  8.83 us
    all_to_all x1, starting transfers between devices, local(): lax.all_to_all(parts, ('y', 'xl', 'core'), split_axis=0, concat_axis=0, t...  8.66 us
    ppermute x2, waiting for transfers between devices, local(): lax.ppermute(tensor[2 * h:2 * h + 2], 'xh', SWAP)[None]  6.01 us
    all_to_all x1, waiting for transfers between devices, local(): lax.all_to_all(parts, ('y', 'xl', 'core'), split_axis=0, concat_axis=0, t...  4.16 us
  transfers between devices with their start and end apart: 24, of which 15 were waited for; matrix products, arithmetic and copies ran while one was open for 1% of the time, Pallas kernels for 9%

profile of v1, /device:TPU:1, one launch (start us, length us, event | category | flops | bytes accessed | tf_op | source)
XLA Modules:
  0.0 124.2 jit_solution(2552189626382039905)
XLA Ops:
  7.3 3.4 %copy-done = bf16[8,512,1024]{2,1,0:T(8,128)(2,1)S(1)} copy-done((bf16[8,512,1024]{2,1,0:T(8,128)(2,1)S(1)}, bf16[8,512,1024]{2,1,0:T(8,128)(2,1)}, u32[]{:S(2)}) %copy-start) | copy-done | bytes 8388632
  11.4 1.5 %prepare.1 = (bf16[2,512,1024]{2,1,0:T(8,128)(2,1)S(1)}, bf16[2,16,32,512]{3,2,1,0:T(8,128)(2,1)S(1)}, bf16[2,16,32,512]{3,2,1,0:T(8,128)(2,1)S(1)}) custom-call(s32[3]{0:T(128)S(1)} %pad_add_fusion.place, s32[2,2]{1,0:T(2,128)S(1)} %copy-done.4, bf16[8,512,1024]{2,1,0:T(8,128)(2,1)S(1)} %copy-done, bf16[8,512,1024]{2,1,0:T(8,128)(2,1)S(1)} %copy-done), custom_call_target="tpu_custom_call" | custom-call | tf_op jit(solution)/shard_map/prepare/pallas_call | solution.py:47
  12.9 3.3 %collective-permute-start = (bf16[2,512,1024]{2,1,0:T(8,128)(2,1)S(1)}, bf16[2,512,1024]{2,1,0:T(8,128)(2,1)S(1)}, u32[]{:S(2)}, u32[]{:S(2)}) collective-permute-start(bf16[2,512,1024]{2,1,0:T(8,128)(2,1)S(1)} %get-tuple-element.8.refs_10_.refs_6_.refs_1_), channel_id=1, source_target_pairs={{0,1},{1,0},{2,3},{3,2},{4,5},{5,4},{6,7},{7,6},{8,9},{9,8},{10,11... | collective-permute-start | bytes 6291464 | tf_op jit(solution)/shard_map/ppermute | solution.py:236
  16.4 1.1 collective-permute-start.2
  17.5 2.0 %collective-permute-start.7 = (bf16[2,32,1024]{2,1,0:T(8,128)(2,1)S(1)}, bf16[2,32,1024]{2,1,0:T(8,128)(2,1)S(1)}, u32[]{:S(2)}, u32[]{:S(2)}) collective-permute-start(bf16[2,32,1024]{2,1,0:T(8,128)(2,1)S(1)} %get-tuple-element.15), channel_id=1, source_target_pairs={{0,2},{2,0},{1,3},{3,1},{4,6},{6,4},{5,7},{7,5},{8,10},{10,8},{9,1... | collective-permute-start | bytes 393224 | tf_op jit(solution)/shard_map/ppermute | solution.py:234
  19.4 3.2 %collective-permute-done.2 = bf16[2,32,1024]{2,1,0:T(8,128)(2,1)S(1)} collective-permute-done((bf16[2,32,1024]{2,1,0:T(8,128)(2,1)S(1)}, bf16[2,32,1024]{2,1,0:T(8,128)(2,1)S(1)}, u32[]{:S(2)}, u32[]{:S(2)}) %collective-permute-start.2) | collective-permute-done | bytes 131104 | tf_op jit(solution)/shard_map/ppermute | solution.py:234
  22.6 2.8 %collective-permute-done.7 = bf16[2,32,1024]{2,1,0:T(8,128)(2,1)S(1)} collective-permute-done((bf16[2,32,1024]{2,1,0:T(8,128)(2,1)S(1)}, bf16[2,32,1024]{2,1,0:T(8,128)(2,1)S(1)}, u32[]{:S(2)}, u32[]{:S(2)}) %collective-permute-start.7) | collective-permute-done | bytes 131104 | tf_op jit(solution)/shard_map/ppermute | solution.py:234
  25.4 3.6 %collective-permute-start.10 = (bf16[1,2,32,1024]{3,2,1,0:T(8,128)(2,1)S(1)}, bf16[1,2,32,1024]{3,2,1,0:T(8,128)(2,1)S(1)}, u32[]{:S(2)}, u32[]{:S(2)}) collective-permute-start(bf16[1,2,32,1024]{3,2,1,0:T(8,128)(2,1)S(1)} %bitcast.41), channel_id=1, source_target_pairs={{4,0},{8,4},{12,8},{16,12},{20,16},{24,20},{28,24},{0,28},{5,1},{9... | collective-permute-start | bytes 393224 | tf_op jit(solution)/shard_map/ppermute | solution.py:248
  29.8 2.4 %collective-permute-done.3.refs_1_ = bf16[1,2,32,1024]{3,2,1,0:T(8,128)(2,1)S(1)} collective-permute-done((bf16[1,2,32,1024]{3,2,1,0:T(8,128)(2,1)S(1)}, bf16[1,2,32,1024]{3,2,1,0:T(8,128)(2,1)S(1)}, u32[]{:S(2)}, u32[]{:S(2)}) %collective-permute-start.3) | collective-permute-done | bytes 131104 | tf_op jit(solution)/shard_map/ppermute | solution.py:245
  32.8 5.4 %collective-permute-done.5.refs_3_ = bf16[1,2,32,1024]{3,2,1,0:T(8,128)(2,1)S(1)} collective-permute-done((bf16[1,2,32,1024]{3,2,1,0:T(8,128)(2,1)S(1)}, bf16[1,2,32,1024]{3,2,1,0:T(8,128)(2,1)S(1)}, u32[]{:S(2)}, u32[]{:S(2)}) %collective-permute-start.5) | collective-permute-done | bytes 131104 | tf_op jit(solution)/shard_map/ppermute | solution.py:248
  38.2 3.5 %collective-permute-start.11 = (bf16[1,2,32,1024]{3,2,1,0:T(8,128)(2,1)S(1)}, bf16[1,2,32,1024]{3,2,1,0:T(8,128)(2,1)S(1)}, u32[]{:S(2)}, u32[]{:S(2)}) collective-permute-start(bf16[1,2,32,1024]{3,2,1,0:T(8,128)(2,1)S(1)} %collective-permute-done.10.refs_8_), channel_id=1, source_target_pairs={{4,0},{8,4},{12,8},{16,12},{20,16},{24,20},{28,24},{0,28},{5,1},{9... | collective-permute-start | bytes 393224 | tf_op jit(solution)/shard_map/ppermute | solution.py:248
  41.8 5.2 %collective-permute-done.4.refs_2_ = bf16[1,2,32,1024]{3,2,1,0:T(8,128)(2,1)S(1)} collective-permute-done((bf16[1,2,32,1024]{3,2,1,0:T(8,128)(2,1)S(1)}, bf16[1,2,32,1024]{3,2,1,0:T(8,128)(2,1)S(1)}, u32[]{:S(2)}, u32[]{:S(2)}) %collective-permute-start.4) | collective-permute-done | bytes 131104 | tf_op jit(solution)/shard_map/ppermute | solution.py:245
  47.0 3.2 %collective-permute-done.6.refs_4_ = bf16[1,2,32,1024]{3,2,1,0:T(8,128)(2,1)S(1)} collective-permute-done((bf16[1,2,32,1024]{3,2,1,0:T(8,128)(2,1)S(1)}, bf16[1,2,32,1024]{3,2,1,0:T(8,128)(2,1)S(1)}, u32[]{:S(2)}, u32[]{:S(2)}) %collective-permute-start.6) | collective-permute-done | bytes 131104 | tf_op jit(solution)/shard_map/ppermute | solution.py:248
  50.2 3.5 %collective-permute-start.16 = (bf16[1,2,32,1024]{3,2,1,0:T(8,128)(2,1)S(1)}, bf16[1,2,32,1024]{3,2,1,0:T(8,128)(2,1)S(1)}, u32[]{:S(2)}, u32[]{:S(2)}) collective-permute-start(bf16[1,2,32,1024]{3,2,1,0:T(8,128)(2,1)S(1)} %collective-permute-done.11.refs_9_), channel_id=1, source_target_pairs={{4,0},{8,4},{12,8},{16,12},{20,16},{24,20},{28,24},{0,28},{5,1},{9... | collective-permute-start | bytes 393224 | tf_op jit(solution)/shard_map/ppermute | solution.py:248
  53.8 1.9 %collective-permute-done.9.refs_7_ = bf16[1,2,32,1024]{3,2,1,0:T(8,128)(2,1)S(1)} collective-permute-done((bf16[1,2,32,1024]{3,2,1,0:T(8,128)(2,1)S(1)}, bf16[1,2,32,1024]{3,2,1,0:T(8,128)(2,1)S(1)}, u32[]{:S(2)}, u32[]{:S(2)}) %collective-permute-start.9) | collective-permute-done | bytes 131104 | tf_op jit(solution)/shard_map/ppermute | solution.py:245
  55.7 5.6 %collective-permute-done.12.refs_0_ = bf16[1,2,32,1024]{3,2,1,0:T(8,128)(2,1)S(1)} collective-permute-done((bf16[1,2,32,1024]{3,2,1,0:T(8,128)(2,1)S(1)}, bf16[1,2,32,1024]{3,2,1,0:T(8,128)(2,1)S(1)}, u32[]{:S(2)}, u32[]{:S(2)}) %collective-permute-start.12) | collective-permute-done | bytes 131104 | tf_op jit(solution)/shard_map/ppermute | solution.py:245
  61.9 2.2 %collective-permute-start.17 = (bf16[1,2,32,1024]{3,2,1,0:T(8,128)(2,1)S(1)}, bf16[1,2,32,1024]{3,2,1,0:T(8,128)(2,1)S(1)}, u32[]{:S(2)}, u32[]{:S(2)}) collective-permute-start(bf16[1,2,32,1024]{3,2,1,0:T(8,128)(2,1)S(1)} %collective-permute-done.16.refs_4_), channel_id=1, source_target_pairs={{4,0},{8,4},{12,8},{16,12},{20,16},{24,20},{28,24},{0,28},{5,1},{9... | collective-permute-start | bytes 393224 | tf_op jit(solution)/shard_map/ppermute | solution.py:248
  64.0 2.3 %collective-permute-done.15.refs_3_ = bf16[1,2,32,1024]{3,2,1,0:T(8,128)(2,1)S(1)} collective-permute-done((bf16[1,2,32,1024]{3,2,1,0:T(8,128)(2,1)S(1)}, bf16[1,2,32,1024]{3,2,1,0:T(8,128)(2,1)S(1)}, u32[]{:S(2)}, u32[]{:S(2)}) %collective-permute-start.15) | collective-permute-done | bytes 131104 | tf_op jit(solution)/shard_map/ppermute | solution.py:245
  66.3 2.5 %collective-permute-done.13.refs_1_ = bf16[1,2,32,1024]{3,2,1,0:T(8,128)(2,1)S(1)} collective-permute-done((bf16[1,2,32,1024]{3,2,1,0:T(8,128)(2,1)S(1)}, bf16[1,2,32,1024]{3,2,1,0:T(8,128)(2,1)S(1)}, u32[]{:S(2)}, u32[]{:S(2)}) %collective-permute-start.13) | collective-permute-done | bytes 131104 | tf_op jit(solution)/shard_map/ppermute | solution.py:245
  68.8 1.4 %copy-done.8 = bf16[2,512,1024]{2,1,0:T(8,128)(2,1)} copy-done((bf16[2,512,1024]{2,1,0:T(8,128)(2,1)}, bf16[2,512,1024]{2,1,0:T(8,128)(2,1)S(1)}, u32[]{:S(2)}) %copy-start.8) | copy-done | bytes 2097176
  70.2 4.2 %collide.4.refs_6_ = f32[2,8,512]{2,1,0:T(8,128)S(1)} custom-call(s32[3]{0:T(128)S(1)} %pad_add_fusion.place, bf16[1,2,32,1024]{3,2,1,0:T(8,128)(2,1)S(1)} %collective-permute-done.12.refs_0_, bf16[1,2,32,1024]{3,2,1,0:T(8,128)(2,1)S(1)} %collective-permute-done.13.refs_1_, bf16[1,2,32,1024]{3,2,1,0:T(8,128)(2,1)S(1)} %collective-permute-done.14.refs_2_, ...), custom_call_target="tpu_custom_call" | custom-call | flops 1610612736 | bytes 4194304 | tf_op jit(solution)/shard_map/collide/pallas_call | solution.py:144
  74.5 5.3 %collide.3.refs_5_ = f32[2,8,512]{2,1,0:T(8,128)S(1)} custom-call(s32[3]{0:T(128)S(1)} %pad_add_fusion.place, bf16[1,2,32,1024]{3,2,1,0:T(8,128)(2,1)S(1)} %bitcast.40, bf16[1,2,32,1024]{3,2,1,0:T(8,128)(2,1)S(1)} %collective-permute-done.3.refs_1_, bf16[1,2,32,1024]{3,2,1,0:T(8,128)(2,1)S(1)} %collective-permute-done.4.refs_2_, ...), custom_call_target="tpu_custom_call" | custom-call | flops 2684354560 | bytes 4194304 | tf_op jit(solution)/shard_map/collide/pallas_call | solution.py:144
  79.9 1.2 copy-done.3
  81.1 1.6 %copy-done.7 = bf16[32,32,1024]{2,1,0:T(8,128)(2,1)S(1)} copy-done((bf16[32,32,1024]{2,1,0:T(8,128)(2,1)S(1)}, bf16[32,32,1024]{2,1,0:T(8,128)(2,1)}, u32[]{:S(2)}) %copy-start.7) | copy-done | bytes 2097176
  82.7 8.3 %collide.5 = f32[8,2,8,512]{3,2,1,0:T(8,128)} custom-call(s32[3]{0:T(128)S(1)} %pad_add_fusion.place, bf16[8,4,32,1024]{3,2,1,0:T(8,128)(2,1)S(1)} %bitcast.37, bf16[2,512,1024]{2,1,0:T(8,128)(2,1)} %copy-done.1, bf16[2,512,1024]{2,1,0:T(8,128)(2,1)} %copy-done.8, bf16[2,16,32,512]{3,2,1,0:T(8,128)(2,1)S(1)} %get-tuple-element.9.refs_12_.refs_8_.refs_3_, ...), custom_call_target="tpu_custom_call" | custom-call | flops 4294967296 | bytes 4194304 | tf_op jit(solution)/shard_map/collide/pallas_call | solution.py:144
  90.9 8.7 %all-to-all-start = ((f32[16,8,512]{2,1,0:T(8,128)}), f32[16,8,512]{2,1,0:T(8,128)S(1)}, u32[]{:S(2)}, u32[]{:S(2)}) async-start(f32[16,8,512]{2,1,0:T(8,128)} %bitcast.6), calls=%async_computation | async-start | bytes 524288 | tf_op jit(solution)/shard_map/all_to_all | solution.py:263
  100.2 2.7 %collective-permute-start.20 = (bf16[32,8,128]{2,1,0:T(8,128)(2,1)S(1)}, bf16[32,8,128]{2,1,0:T(8,128)(2,1)S(1)}, u32[]{:S(2)}, u32[]{:S(2)}) collective-permute-start(bf16[32,8,128]{2,1,0:T(8,128)(2,1)S(1)} %get-tuple-element.12), channel_id=1, source_target_pairs={{0,1},{1,2},{2,3},{3,4},{4,5},{5,6},{6,7},{7,8},{8,9},{9,10},{10,1... | collective-permute-start | bytes 196616 | tf_op jit(solution)/shard_map/ppermute | solution.py:252
  102.9 4.2 %all-to-all-done = f32[16,8,512]{2,1,0:T(8,128)S(1)} async-done(((f32[16,8,512]{2,1,0:T(8,128)}), f32[16,8,512]{2,1,0:T(8,128)S(1)}, u32[]{:S(2)}, u32[]{:S(2)}) %all-to-all-start) | async-done | bytes 262176 | tf_op jit(solution)/shard_map/all_to_all | solution.py:263
  107.1 3.3 %collective-permute-start.18 = (f32[8,8,128]{2,1,0:T(8,128)S(1)}, f32[8,8,128]{2,1,0:T(8,128)S(1)}, u32[]{:S(2)}, u32[]{:S(2)}) collective-permute-start(f32[8,8,128]{2,1,0:T(8,128)S(1)} %get-tuple-element.14), channel_id=1, source_target_pairs={{0,1},{1,2},{2,3},{3,4},{4,5},{5,6},{6,7},{7,8},{8,9},{9,10},{10,1... | collective-permute-start | bytes 98312 | tf_op jit(solution)/shard_map/ppermute | solution.py:267
  110.5 0.9 collective-permute-done.18.before
  111.4 3.8 %collective-permute-done.19.after = f32[8,8,128]{2,1,0:T(8,128)S(1)} collective-permute-done((f32[8,8,128]{2,1,0:T(8,128)S(1)}, f32[8,8,128]{2,1,0:T(8,128)S(1)}, u32[]{:S(2)}, u32[]{:S(2)}) %collective-permute-start.19) | collective-permute-done | bytes 32800 | tf_op jit(solution)/shard_map/ppermute | solution.py:268
  115.2 2.1 %finish.1 = f32[32,8,512]{2,1,0:T(8,128)} custom-call(s32[2,2]{1,0:T(2,128)S(1)} %copy-done.5, f32[8]{0:T(128)S(1)} %copy-done.6, f32[8,2,8,512]{3,2,1,0:T(8,128)S(1)} %bitcast.36, f32[8,8,128]{2,1,0:T(8,128)S(1)} %collective-permute-done.18.before, f32[8,8,128]{2,1,0:T(8,128)S(1)} %collective-permute-done.19.after, bf16[32,8,512]{2,1,0:T(8,128)(2,1)S(1)} %bitcast.34, ...), custom_call_target="tpu_custom_call" | custom-call | tf_op jit(solution)/shard_map/finish/pallas_call | solution.py:213
  (52 shorter events, 4.4 us)
Async XLA Ops:
  6.5 73.3 %all-gather.3.cloned.1.call-start = ((), (), s32[]{:S(2)}) async-start(), calls=%async_computation.1 | async-start | bytes 2359296 | tf_op jit(solution)/shard_map/all_gather | solution.py:232
  7.3 3.4 %copy-start = (bf16[8,512,1024]{2,1,0:T(8,128)(2,1)S(1)}, bf16[8,512,1024]{2,1,0:T(8,128)(2,1)}, u32[]{:S(2)}) copy-start(bf16[8,512,1024]{2,1,0:T(8,128)(2,1)} %right.1) | copy-start | bytes 25165828
  11.4 5.0 %copy-start.9 = (bf16[4,32,1024]{2,1,0:T(8,128)(2,1)S(1)}, bf16[4,32,1024]{2,1,0:T(8,128)(2,1)}, u32[]{:S(2)}) copy-start(bf16[4,32,1024]{2,1,0:T(8,128)(2,1)} %param.6) | copy-start | bytes 786436
  12.9 61.6 %copy-start.1 = (bf16[2,512,1024]{2,1,0:T(8,128)(2,1)}, bf16[2,512,1024]{2,1,0:T(8,128)(2,1)S(1)}, u32[]{:S(2)}) copy-start(bf16[2,512,1024]{2,1,0:T(8,128)(2,1)S(1)} %get-tuple-element.8.refs_10_.refs_6_.refs_1_) | copy-start | bytes 6291460
  12.9 55.9 %collective-permute-start = (bf16[2,512,1024]{2,1,0:T(8,128)(2,1)S(1)}, bf16[2,512,1024]{2,1,0:T(8,128)(2,1)S(1)}, u32[]{:S(2)}, u32[]{:S(2)}) collective-permute-start(bf16[2,512,1024]{2,1,0:T(8,128)(2,1)S(1)} %get-tuple-element.8.refs_10_.refs_6_.refs_1_), channel_id=1, source_target_pairs={{0,1},{1,0},{2,3},{3,2},{4,5},{5,4},{6,7},{7,6},{8,9},{9,8},{10,11... | collective-permute-start | bytes 6291464 | tf_op jit(solution)/shard_map/ppermute | solution.py:236
  16.3 52.6 %collective-permute-start.1 = (bf16[2,16,32,512]{3,2,1,0:T(8,128)(2,1)S(1)}, bf16[2,16,32,512]{3,2,1,0:T(8,128)(2,1)S(1)}, u32[]{:S(2)}, u32[]{:S(2)}) collective-permute-start(bf16[2,16,32,512]{3,2,1,0:T(8,128)(2,1)S(1)} %get-tuple-element.10), channel_id=1, source_target_pairs={{0,1},{1,0},{2,3},{3,2},{4,5},{5,4},{6,7},{7,6},{8,9},{9,8},{10,11... | collective-permute-start | bytes 3145736 | tf_op jit(solution)/shard_map/ppermute | solution.py:237
  16.4 6.3 %collective-permute-start.2 = (bf16[2,32,1024]{2,1,0:T(8,128)(2,1)S(1)}, bf16[2,32,1024]{2,1,0:T(8,128)(2,1)S(1)}, u32[]{:S(2)}, u32[]{:S(2)}) collective-permute-start(bf16[2,32,1024]{2,1,0:T(8,128)(2,1)S(1)} %get-tuple-element.16), channel_id=1, source_target_pairs={{0,2},{2,0},{1,3},{3,1},{4,6},{6,4},{5,7},{7,5},{8,10},{10,8},{9,1... | collective-permute-start | bytes 393224 | tf_op jit(solution)/shard_map/ppermute | solution.py:234
  17.5 8.0 %collective-permute-start.7 = (bf16[2,32,1024]{2,1,0:T(8,128)(2,1)S(1)}, bf16[2,32,1024]{2,1,0:T(8,128)(2,1)S(1)}, u32[]{:S(2)}, u32[]{:S(2)}) collective-permute-start(bf16[2,32,1024]{2,1,0:T(8,128)(2,1)S(1)} %get-tuple-element.15), channel_id=1, source_target_pairs={{0,2},{2,0},{1,3},{3,1},{4,6},{6,4},{5,7},{7,5},{8,10},{10,8},{9,1... | collective-permute-start | bytes 393224 | tf_op jit(solution)/shard_map/ppermute | solution.py:234
  22.6 9.6 %collective-permute-start.3 = (bf16[1,2,32,1024]{3,2,1,0:T(8,128)(2,1)S(1)}, bf16[1,2,32,1024]{3,2,1,0:T(8,128)(2,1)S(1)}, u32[]{:S(2)}, u32[]{:S(2)}) collective-permute-start(bf16[1,2,32,1024]{3,2,1,0:T(8,128)(2,1)S(1)} %bitcast.38), channel_id=1, source_target_pairs={{0,4},{4,8},{8,12},{12,16},{16,20},{20,24},{24,28},{28,0},{1,5},{5... | collective-permute-start | bytes 393224 | tf_op jit(solution)/shard_map/ppermute | solution.py:245
  25.4 6.9 %collective-permute-start.10 = (bf16[1,2,32,1024]{3,2,1,0:T(8,128)(2,1)S(1)}, bf16[1,2,32,1024]{3,2,1,0:T(8,128)(2,1)S(1)}, u32[]{:S(2)}, u32[]{:S(2)}) collective-permute-start(bf16[1,2,32,1024]{3,2,1,0:T(8,128)(2,1)S(1)} %bitcast.41), channel_id=1, source_target_pairs={{4,0},{8,4},{12,8},{16,12},{20,16},{24,20},{28,24},{0,28},{5,1},{9... | collective-permute-start | bytes 393224 | tf_op jit(solution)/shard_map/ppermute | solution.py:248
  29.0 9.2 %collective-permute-start.5 = (bf16[1,2,32,1024]{3,2,1,0:T(8,128)(2,1)S(1)}, bf16[1,2,32,1024]{3,2,1,0:T(8,128)(2,1)S(1)}, u32[]{:S(2)}, u32[]{:S(2)}) collective-permute-start(bf16[1,2,32,1024]{3,2,1,0:T(8,128)(2,1)S(1)} %bitcast.39), channel_id=1, source_target_pairs={{4,0},{8,4},{12,8},{16,12},{20,16},{24,20},{28,24},{0,28},{5,1},{9... | collective-permute-start | bytes 393224 | tf_op jit(solution)/shard_map/ppermute | solution.py:248
  32.2 9.6 %collective-permute-start.8 = (bf16[1,2,32,1024]{3,2,1,0:T(8,128)(2,1)S(1)}, bf16[1,2,32,1024]{3,2,1,0:T(8,128)(2,1)S(1)}, u32[]{:S(2)}, u32[]{:S(2)}) collective-permute-start(bf16[1,2,32,1024]{3,2,1,0:T(8,128)(2,1)S(1)} %bitcast.42), channel_id=1, source_target_pairs={{0,4},{4,8},{8,12},{12,16},{16,20},{20,24},{24,28},{28,0},{1,5},{5... | collective-permute-start | bytes 393224 | tf_op jit(solution)/shard_map/ppermute | solution.py:245
  32.3 14.7 %collective-permute-start.4 = (bf16[1,2,32,1024]{3,2,1,0:T(8,128)(2,1)S(1)}, bf16[1,2,32,1024]{3,2,1,0:T(8,128)(2,1)S(1)}, u32[]{:S(2)}, u32[]{:S(2)}) collective-permute-start(bf16[1,2,32,1024]{3,2,1,0:T(8,128)(2,1)S(1)} %collective-permute-done.3.refs_1_), channel_id=1, source_target_pairs={{0,4},{4,8},{8,12},{12,16},{16,20},{20,24},{24,28},{28,0},{1,5},{5... | collective-permute-start | bytes 393224 | tf_op jit(solution)/shard_map/ppermute | solution.py:245
  38.2 8.8 %collective-permute-start.11 = (bf16[1,2,32,1024]{3,2,1,0:T(8,128)(2,1)S(1)}, bf16[1,2,32,1024]{3,2,1,0:T(8,128)(2,1)S(1)}, u32[]{:S(2)}, u32[]{:S(2)}) collective-permute-start(bf16[1,2,32,1024]{3,2,1,0:T(8,128)(2,1)S(1)} %collective-permute-done.10.refs_8_), channel_id=1, source_target_pairs={{4,0},{8,4},{12,8},{16,12},{20,16},{24,20},{28,24},{0,28},{5,1},{9... | collective-permute-start | bytes 393224 | tf_op jit(solution)/shard_map/ppermute | solution.py:248
  41.8 8.5 %collective-permute-start.6 = (bf16[1,2,32,1024]{3,2,1,0:T(8,128)(2,1)S(1)}, bf16[1,2,32,1024]{3,2,1,0:T(8,128)(2,1)S(1)}, u32[]{:S(2)}, u32[]{:S(2)}) collective-permute-start(bf16[1,2,32,1024]{3,2,1,0:T(8,128)(2,1)S(1)} %collective-permute-done.5.refs_3_), channel_id=1, source_target_pairs={{4,0},{8,4},{12,8},{16,12},{20,16},{24,20},{28,24},{0,28},{5,1},{9... | collective-permute-start | bytes 393224 | tf_op jit(solution)/shard_map/ppermute | solution.py:248
  47.0 8.6 %collective-permute-start.9 = (bf16[1,2,32,1024]{3,2,1,0:T(8,128)(2,1)S(1)}, bf16[1,2,32,1024]{3,2,1,0:T(8,128)(2,1)S(1)}, u32[]{:S(2)}, u32[]{:S(2)}) collective-permute-start(bf16[1,2,32,1024]{3,2,1,0:T(8,128)(2,1)S(1)} %collective-permute-done.8.refs_6_), channel_id=1, source_target_pairs={{0,4},{4,8},{8,12},{12,16},{16,20},{20,24},{24,28},{28,0},{1,5},{5... | collective-permute-start | bytes 393224 | tf_op jit(solution)/shard_map/ppermute | solution.py:245
  47.0 14.2 %collective-permute-start.12 = (bf16[1,2,32,1024]{3,2,1,0:T(8,128)(2,1)S(1)}, bf16[1,2,32,1024]{3,2,1,0:T(8,128)(2,1)S(1)}, u32[]{:S(2)}, u32[]{:S(2)}) collective-permute-start(bf16[1,2,32,1024]{3,2,1,0:T(8,128)(2,1)S(1)} %collective-permute-done.4.refs_2_), channel_id=1, source_target_pairs={{0,4},{4,8},{8,12},{12,16},{16,20},{20,24},{24,28},{28,0},{1,5},{5... | collective-permute-start | bytes 393224 | tf_op jit(solution)/shard_map/ppermute | solution.py:245
  50.2 11.0 %collective-permute-start.16 = (bf16[1,2,32,1024]{3,2,1,0:T(8,128)(2,1)S(1)}, bf16[1,2,32,1024]{3,2,1,0:T(8,128)(2,1)S(1)}, u32[]{:S(2)}, u32[]{:S(2)}) collective-permute-start(bf16[1,2,32,1024]{3,2,1,0:T(8,128)(2,1)S(1)} %collective-permute-done.11.refs_9_), channel_id=1, source_target_pairs={{4,0},{8,4},{12,8},{16,12},{20,16},{24,20},{28,24},{0,28},{5,1},{9... | collective-permute-start | bytes 393224 | tf_op jit(solution)/shard_map/ppermute | solution.py:248
  55.6 6.2 %collective-permute-start.14 = (bf16[1,2,32,1024]{3,2,1,0:T(8,128)(2,1)S(1)}, bf16[1,2,32,1024]{3,2,1,0:T(8,128)(2,1)S(1)}, u32[]{:S(2)}, u32[]{:S(2)}) collective-permute-start(bf16[1,2,32,1024]{3,2,1,0:T(8,128)(2,1)S(1)} %collective-permute-done.6.refs_4_), channel_id=1, source_target_pairs={{4,0},{8,4},{12,8},{16,12},{20,16},{24,20},{28,24},{0,28},{5,1},{9... | collective-permute-start | bytes 393224 | tf_op jit(solution)/shard_map/ppermute | solution.py:248
  61.3 5.0 %collective-permute-start.15 = (bf16[1,2,32,1024]{3,2,1,0:T(8,128)(2,1)S(1)}, bf16[1,2,32,1024]{3,2,1,0:T(8,128)(2,1)S(1)}, u32[]{:S(2)}, u32[]{:S(2)}) collective-permute-start(bf16[1,2,32,1024]{3,2,1,0:T(8,128)(2,1)S(1)} %collective-permute-done.9.refs_7_), channel_id=1, source_target_pairs={{0,4},{4,8},{8,12},{12,16},{16,20},{20,24},{24,28},{28,0},{1,5},{5... | collective-permute-start | bytes 393224 | tf_op jit(solution)/shard_map/ppermute | solution.py:245
  61.3 7.5 %collective-permute-start.13 = (bf16[1,2,32,1024]{3,2,1,0:T(8,128)(2,1)S(1)}, bf16[1,2,32,1024]{3,2,1,0:T(8,128)(2,1)S(1)}, u32[]{:S(2)}, u32[]{:S(2)}) collective-permute-start(bf16[1,2,32,1024]{3,2,1,0:T(8,128)(2,1)S(1)} %collective-permute-done.12.refs_0_), channel_id=1, source_target_pairs={{0,4},{4,8},{8,12},{12,16},{16,20},{20,24},{24,28},{28,0},{1,5},{5... | collective-permute-start | bytes 393224 | tf_op jit(solution)/shard_map/ppermute | solution.py:245
  61.9 6.9 %collective-permute-start.17 = (bf16[1,2,32,1024]{3,2,1,0:T(8,128)(2,1)S(1)}, bf16[1,2,32,1024]{3,2,1,0:T(8,128)(2,1)S(1)}, u32[]{:S(2)}, u32[]{:S(2)}) collective-permute-start(bf16[1,2,32,1024]{3,2,1,0:T(8,128)(2,1)S(1)} %collective-permute-done.16.refs_4_), channel_id=1, source_target_pairs={{4,0},{8,4},{12,8},{16,12},{20,16},{24,20},{28,24},{0,28},{5,1},{9... | collective-permute-start | bytes 393224 | tf_op jit(solution)/shard_map/ppermute | solution.py:248
  68.8 5.7 %copy-start.2 = (bf16[2,16,32,512]{3,2,1,0:T(8,128)(2,1)}, bf16[2,16,32,512]{3,2,1,0:T(8,128)(2,1)S(1)}, u32[]{:S(2)}) copy-start(bf16[2,16,32,512]{3,2,1,0:T(8,128)(2,1)S(1)} %collective-permute-done.1.refs_13_.refs_9_.refs_4_) | copy-start | bytes 3145732
  90.9 8.7 %slice-start = ((bf16[8,512,1024]{2,1,0:T(8,128)(2,1)}), bf16[8,512,32]{2,1,0:T(8,128)(2,1)S(1)}, s32[]{:S(2)}) async-start(bf16[8,512,1024]{2,1,0:T(8,128)(2,1)} %right.1), calls=%async_computation.2 | async-start | bytes 2097152 | tf_op jit(solution)/shard_map/slice | solution.py:251
  90.9 19.4 %copy-start.10 = (s32[512]{0:T(512)S(1)}, s32[512]{0:T(512)}, u32[]{:S(2)}) copy-start(s32[512]{0:T(512)} %param.8) | copy-start | bytes 6148
  90.9 16.1 %all-to-all-start = ((f32[16,8,512]{2,1,0:T(8,128)}), f32[16,8,512]{2,1,0:T(8,128)S(1)}, u32[]{:S(2)}, u32[]{:S(2)}) async-start(f32[16,8,512]{2,1,0:T(8,128)} %bitcast.6), calls=%async_computation | async-start | bytes 524288 | tf_op jit(solution)/shard_map/all_to_all | solution.py:263
  99.6 15.6 %copy-start.5 = (s32[2,2]{1,0:T(2,128)S(1)}, s32[2,2]{1,0:T(2,128)}, u32[]{:S(2)}) copy-start(s32[2,2]{1,0:T(2,128)} %pairs.3) | copy-start | bytes 52
  99.6 15.6 %copy-start.6 = (f32[8]{0:T(128)S(1)}, f32[8]{0:T(128)}, u32[]{:S(2)}) copy-start(f32[8]{0:T(128)} %thermal.1) | copy-start | bytes 100
  100.2 10.3 %collective-permute-start.20 = (bf16[32,8,128]{2,1,0:T(8,128)(2,1)S(1)}, bf16[32,8,128]{2,1,0:T(8,128)(2,1)S(1)}, u32[]{:S(2)}, u32[]{:S(2)}) collective-permute-start(bf16[32,8,128]{2,1,0:T(8,128)(2,1)S(1)} %get-tuple-element.12), channel_id=1, source_target_pairs={{0,1},{1,2},{2,3},{3,4},{4,5},{5,6},{6,7},{7,8},{8,9},{9,10},{10,1... | collective-permute-start | bytes 196616 | tf_op jit(solution)/shard_map/ppermute | solution.py:252
  102.9 7.6 %collective-permute-start.21 = (bf16[32,8,128]{2,1,0:T(8,128)(2,1)S(1)}, bf16[32,8,128]{2,1,0:T(8,128)(2,1)S(1)}, u32[]{:S(2)}, u32[]{:S(2)}) collective-permute-start(bf16[32,8,128]{2,1,0:T(8,128)(2,1)S(1)} %get-tuple-element.11), channel_id=1, source_target_pairs={{1,0},{2,1},{3,2},{4,3},{5,4},{6,5},{7,6},{8,7},{9,8},{10,9},{11,1... | collective-permute-start | bytes 196616 | tf_op jit(solution)/shard_map/ppermute | solution.py:253
  107.1 4.3 %collective-permute-start.18 = (f32[8,8,128]{2,1,0:T(8,128)S(1)}, f32[8,8,128]{2,1,0:T(8,128)S(1)}, u32[]{:S(2)}, u32[]{:S(2)}) collective-permute-start(f32[8,8,128]{2,1,0:T(8,128)S(1)} %get-tuple-element.14), channel_id=1, source_target_pairs={{0,1},{1,2},{2,3},{3,4},{4,5},{5,6},{6,7},{7,8},{8,9},{9,10},{10,1... | collective-permute-start | bytes 98312 | tf_op jit(solution)/shard_map/ppermute | solution.py:267
  110.4 4.8 %collective-permute-start.19 = (f32[8,8,128]{2,1,0:T(8,128)S(1)}, f32[8,8,128]{2,1,0:T(8,128)S(1)}, u32[]{:S(2)}, u32[]{:S(2)}) collective-permute-start(f32[8,8,128]{2,1,0:T(8,128)S(1)} %get-tuple-element.13), channel_id=1, source_target_pairs={{1,0},{2,1},{3,2},{4,3},{5,4},{6,5},{7,6},{8,7},{9,8},{10,9},{11,1... | collective-permute-start | bytes 98312 | tf_op jit(solution)/shard_map/ppermute | solution.py:268
  (4 other events, 4.9 us)
Sparse Core Ops, SparseCore 0:
  9.1 52.5 all-gather.2

commit v2 on v0

v2 whole, which is shorter than its diff:
```python
import functools

import jax
import jax.numpy as jnp
from jax import lax
from jax.experimental import pallas as pl
from jax.experimental.pallas import tpu as pltpu
from jax.sharding import Mesh, PartitionSpec as P

PLANE = 128
Y, XL, Z, XH, CORE = 4, 2, 8, 2, 2
FINE = ("y", "xl", "z", "xh", "core")
BRICK = ("z", "xh", "core")
MODES_HERE = 4
ROWS = 32

collision_update = 0.5
courant = 0.08
max_speed = 11.0
mixing = 0.2

UP = [(i, (i + 1) % Z) for i in range(Z)]
DOWN = [((i + 1) % Z, i) for i in range(Z)]
SWAP = [(0, 1), (1, 0)]


def prepare_kernel(pairs, coeffs, right_out, left_out, left, sems):
    copies = []
    for p in range(2):
        copies.append(pltpu.make_async_copy(coeffs.at[pairs[p, 0]], left.at[p], sems.at[p]))
        copies.append(pltpu.make_async_copy(coeffs.at[pairs[p, 1]], right_out.at[p], sems.at[2 + p]))
    for c in copies:
        c.start()
    for p in range(2):
        copies[2 * p].wait()
        left_out[p] = jnp.transpose(left[p]).reshape(left_out.shape[1:])
    for p in range(2):
        copies[2 * p + 1].wait()


VMEM = pl.BlockSpec(memory_space=pltpu.VMEM)
SMEM = pl.BlockSpec(memory_space=pltpu.SMEM)


def prepare(pairs, coeffs):
    _, cells, width = coeffs.shape
    return pl.pallas_call(
        prepare_kernel,
        in_specs=[SMEM, pl.BlockSpec(memory_space=pltpu.HBM)],
        out_specs=[VMEM] * 2,
        out_shape=[
            jax.ShapeDtypeStruct((2, cells, width), coeffs.dtype),
            jax.ShapeDtypeStruct((2, width // ROWS, ROWS, cells), coeffs.dtype),
        ],
        scratch_shapes=[pltpu.VMEM((2, cells, width), coeffs.dtype), pltpu.SemaphoreType.DMA((4,))],
        compiler_params=pltpu.CompilerParams(vmem_limit_bytes=8 * 2**20),
        cost_estimate=pl.CostEstimate(flops=0, transcendentals=0, bytes_accessed=14 * 2**20),
        name="prepare",
    )(pairs, pltpu.with_memory_space_constraint(coeffs, pltpu.HBM))


def window_kernel(pairs, thermal, coeffs, window, gain, heat, rows, sems):
    modes, species, cells = window.shape
    copies = [
        pltpu.make_async_copy(coeffs.at[s, :, pl.ds(0, PLANE)], rows.at[s], sems.at[s]) for s in range(species)
    ]
    for c in copies:
        c.start()
    at = lax.broadcasted_iota(jnp.int32, (species, PLANE), 0)
    for p in range(2):
        gain[p] = jnp.where(at == pairs[p, 0], jnp.float32(collision_update), jnp.float32(0.0))
    speed = jnp.zeros((species, PLANE), jnp.float32)
    for s in range(species):
        speed = jnp.where(at == s, thermal[s], speed)
    heat[...] = speed
    for s in range(species):
        copies[s].wait()
        window[:, s, :] = jnp.transpose(rows[s].astype(jnp.float32))[:modes]


def make_window(pairs, thermal, coeffs, modes):
    species, cells, _ = coeffs.shape
    return pl.pallas_call(
        window_kernel,
        in_specs=[SMEM, SMEM, pl.BlockSpec(memory_space=pltpu.HBM)],
        out_specs=[VMEM] * 3,
        out_shape=[
            jax.ShapeDtypeStruct((modes, species, cells), jnp.float32),
            jax.ShapeDtypeStruct((2, species, PLANE), jnp.float32),
            jax.ShapeDtypeStruct((species, PLANE), jnp.float32),
        ],
        scratch_shapes=[pltpu.VMEM((species, cells, PLANE), coeffs.dtype), pltpu.SemaphoreType.DMA((species,))],
        compiler_params=pltpu.CompilerParams(vmem_limit_bytes=8 * 2**20),
        cost_estimate=pl.CostEstimate(flops=0, transcendentals=0, bytes_accessed=8 * 2**20),
        name="window",
    )(pairs, thermal, pltpu.with_memory_space_constraint(coeffs, pltpu.HBM))


TILE = 256


def collide_kernel(pieces, n_more, last, *refs):
    n = len(pieces)
    xs = refs[:n]
    rights, lefts = refs[n : n + 2], refs[n + 2 : n + 4]
    more = refs[n + 4 : n + 4 + n_more]
    out, stacked = refs[n + 4 + n_more :]
    z, xh, core = (lax.axis_index(a) for a in BRICK)
    block = MODES_HERE * ROWS
    spots = []
    row = 0
    for x, (column, steps) in zip(xs, pieces):
        rows = x.shape[0] * block
        stacked[row : row + rows, :] = x[...].reshape(rows, x.shape[-1])
        row += rows
        there = lax.rem(z + steps * (2 * core - 1) + Z, Z)
        at_column = 1 - xh if column else xh
        for e in range(x.shape[0]):
            spots.append((there * XH + at_column) * CORE + (core if e == 0 else 1 - core))
    cells = rights[0].shape[1]
    for source in range(2):
        right, left = rights[source], lefts[source]
        slot = core if source == 0 else 1 - core
        for p in range(2):
            for t in range(cells // TILE):
                at = pl.ds(t * TILE, TILE)
                inner = lax.dot_general(
                    stacked[...],
                    right[p, at, :],
                    (((1,), (1,)), ((), ())),
                    preferred_element_type=jnp.float32,
                )
                sums = [None] * MODES_HERE
                row = 0
                for spot in spots:
                    factor = left[p, spot, :, at].astype(jnp.float32)
                    for k in range(MODES_HERE):
                        term = inner[row : row + ROWS] * factor
                        row += ROWS
                        term = (term[0:8] + term[8:16]) + (term[16:24] + term[24:32])
                        sums[k] = term if sums[k] is None else sums[k] + term
                done = jnp.concatenate([jnp.sum(s, axis=0, keepdims=True) for s in sums], axis=0)
                kp = slice(p * MODES_HERE, (p + 1) * MODES_HERE)
                for m in more:
                    done = done + m[source, kp, at]
                if last:
                    for g in range(out.shape[0]):
                        out[g, slot, kp, at] = done
                else:
                    out[source, kp, at] = done


def collide_part(xs, pieces, sides, more=(), last=False):
    _, cells, width = sides[0].shape
    rows = sum(x.shape[0] for x in xs) * MODES_HERE * ROWS
    lead = (Y * XL, CORE) if last else (CORE,)
    return pl.pallas_call(
        functools.partial(collide_kernel, pieces, len(more), last),
        in_specs=[VMEM] * (len(xs) + 4 + len(more)),
        out_specs=VMEM,
        out_shape=jax.ShapeDtypeStruct((*lead, 2 * MODES_HERE, cells), jnp.float32),
        scratch_shapes=[pltpu.VMEM((rows, width), jnp.bfloat16)],
        compiler_params=pltpu.CompilerParams(vmem_limit_bytes=8 * 2**20),
        cost_estimate=pl.CostEstimate(
            flops=2 * rows * 4 * cells * width, transcendentals=0, bytes_accessed=8 * cells * width
        ),
        name="collide",
    )(*xs, *sides, *more)


def state_kernel(parts, window, gain, state, first, last):
    modes, species, cells = window.shape
    for g in range(Y * XL):
        own = parts[g, 0] + parts[g, 1]
        for k in range(MODES_HERE):
            m = g * MODES_HERE + k
            for t in range(cells // PLANE):
                at = slice(t * PLANE, (t + 1) * PLANE)
                value = window[m, :, at]
                for p in range(2):
                    r = p * MODES_HERE + k
                    value = value + gain[p] * own[r : r + 1, at]
                state[m, :, at] = value
                if t == 0:
                    first[m] = value
                if t == cells // PLANE - 1:
                    last[m] = value


def root(k):
    return float(k) ** 0.5


def inner_kernel(state, heat, onehot, out):
    modes, species, cells = state.shape
    flat = state[...].reshape(modes * species, cells)
    high = flat.astype(jnp.bfloat16)
    rest = flat - high.astype(jnp.float32)
    middle = rest.astype(jnp.bfloat16)
    low = (rest - middle.astype(jnp.float32)).astype(jnp.bfloat16)
    pick = onehot[...]
    beside = (
        jnp.dot(low, pick, preferred_element_type=jnp.float32)
        + jnp.dot(middle, pick, preferred_element_type=jnp.float32)
    ) + jnp.dot(high, pick, preferred_element_type=jnp.float32)
    out[...] = beside.reshape(modes, species, cells)
    layers = cells // PLANE
    scale = courant * heat[...]

    def drift(k, at):
        total = None
        for j, c in ((k - 1, k), (k + 1, k + 1)):
            if 0 <= j < modes:
                term = root(c) * state[j, :, at]
                total = term if total is None else total + term
        return total

    for k in range(modes):
        for t in range(layers):
            at = slice(t * PLANE, (t + 1) * PLANE)
            here = state[k, :, at]
            divergence = (max_speed * 1.0) * here
            if t + 1 < layers:
                ahead = slice((t + 1) * PLANE, (t + 2) * PLANE)
                divergence += 0.5 * drift(k, ahead) - (0.5 * max_speed) * state[k, :, ahead]
            if t > 0:
                behind = slice((t - 1) * PLANE, t * PLANE)
                divergence -= 0.5 * drift(k, behind) + (0.5 * max_speed) * state[k, :, behind]
            out[k, :, at] = here - scale * divergence + mixing * (out[k, :, at] - here)


def outer_kernel(inner, heat, before, behind, out):
    modes, species, cells = inner.shape
    scale = courant * heat[...]
    for k in range(modes):
        for side, at, sign in ((before, slice(0, PLANE), -1.0), (behind, slice(cells - PLANE, cells), 1.0)):
            divergence = -(0.5 * max_speed) * side[k]
            if k > 0:
                divergence += (sign * 0.5 * root(k)) * side[k - 1]
            if k < modes - 1:
                divergence += (sign * 0.5 * root(k + 1)) * side[k + 1]
            out[k, :, at] = inner[k, :, at] - scale * divergence
        middle = slice(PLANE, cells - PLANE)
        out[k, :, middle] = inner[k, :, middle]


def simple_call(kernel, name, shapes, *operands):
    return pl.pallas_call(
        kernel,
        in_specs=[VMEM] * len(operands),
        out_specs=[VMEM] * len(shapes),
        out_shape=[jax.ShapeDtypeStruct(s, jnp.float32) for s in shapes],
        compiler_params=pltpu.CompilerParams(vmem_limit_bytes=8 * 2**20),
        name=name,
    )(*operands)


def together(*values):
    return lax.optimization_barrier(values)


def local(coeffs, tensor, pairs, lateral, thermal):
    species, cells, width = coeffs.shape
    modes = tensor.shape[0] * Y * XL
    bricks = Z * XH * CORE
    onward = [(i, (i + 1) % bricks) for i in range(bricks)]
    backward = [((i + 1) % bricks, i) for i in range(bricks)]

    ring = [(CORE * i, CORE * ((i + 1) % Z)) for i in range(Z)] + [(CORE * ((i + 1) % Z) + 1, CORE * i + 1) for i in range(Z)]
    step = lambda a: lax.ppermute(a, ("z", "core"), ring)
    both = lambda a: jnp.concatenate([a, lax.ppermute(a, "core", SWAP)])

    tensor = tensor[None]
    other = lax.ppermute(tensor, "xh", SWAP)
    own0 = both(tensor)
    right_own, left_own = prepare(pairs, coeffs)
    own1 = step(own0)
    right_send, left_send = together(right_own, left_own, own0)[:2]
    right_sib = lax.ppermute(right_send, "core", SWAP)
    left_sib = lax.ppermute(left_send, "core", SWAP)
    sides = (right_own, right_sib, left_own, left_sib)
    own1, other = together(own1, other)
    alt1 = step(both(other))
    own2 = step(own1)
    parts = collide_part([tensor, other, own1], [(0, 0), (1, 0), (0, 1)], sides)
    alt1, parts, pairs_now, lateral = together(alt1, parts, pairs, lateral)
    alt2 = step(alt1)
    window, gain, heat = make_window(pairs_now, thermal, coeffs, modes)
    onehot = (lax.broadcasted_iota(jnp.int32, (cells, cells), 0) == lateral[None, :]).astype(jnp.bfloat16)
    own3 = step(own2)
    parts = collide_part([alt1, own2], [(1, 1), (0, 2)], sides, (parts,))
    alt2, parts, window, gain, heat, onehot = together(alt2, parts, window, gain, heat, onehot)
    alt3 = step(alt2)
    own4 = step(own3[:1])
    parts = collide_part([alt2, own3], [(1, 2), (0, 3)], sides, (parts,))
    alt3, parts = together(alt3, parts)
    alt4 = step(alt3[:1])
    parts = collide_part([alt3, own4], [(1, 3), (0, 4)], sides, (parts,))
    parts = collide_part([alt4], [(1, 4)], sides, (parts,), True)

    parts = parts.reshape(Y * XL * CORE, 2 * MODES_HERE, cells)
    parts = lax.all_to_all(parts, ("y", "xl", "core"), split_axis=0, concat_axis=0, tiled=True)
    parts = parts.reshape(Y * XL, CORE, 2 * MODES_HERE, cells)
    full, edge = (modes, species, cells), (modes, species, PLANE)
    state, first, last = simple_call(state_kernel, "state", (full, edge, edge), parts, window, gain)
    before = lax.ppermute(last, BRICK, onward)
    behind = lax.ppermute(first, BRICK, backward)
    inner = simple_call(inner_kernel, "inner", (full,), state, heat, onehot)[0]
    return simple_call(outer_kernel, "outer", (full,), inner, heat, before, behind)[0]


def solution(mesh):
    fine = Mesh(mesh.devices.reshape(Y, XL, Z, XH, CORE), FINE)
    in_specs = (P(None, BRICK, None), P(("y", "xl"), BRICK, None), P(), P(BRICK), P())
    out_specs = P(None, None, BRICK)
    return jax.shard_map(local, mesh=fine, in_specs=in_specs, out_specs=out_specs, check_vma=False)
```

time: 195 us -> 85.9 us (0.44)
  waiting for transfers between devices: 103 us -> 19.9 us
  local copies, waits for them, and re-layouts: 38.2 us -> 0.74 us
  starting transfers between devices: 7.19 us -> 32.2 us
  Pallas kernels: 0 us -> 17.2 us
  matrix products: 16.6 us -> 0 us
  other arithmetic: 15.5 us -> 0.24 us
  blocking collectives: 0 us -> 15.2 us
  between operations: 13.5 us -> 0.16 us
    all_gather x1 -> x0, waiting for transfers between devices: 94.9 us -> none  [local(): piece = lax.all_gather(tensor, 'brick', axis=1, tiled=True)]
    ppermute x2 -> x15, starting transfers between devices: 3.17 us -> 32.2 us  [the longest x8 21.4 us: local(): step = lambda a: lax.ppermute(a, ('z', 'core'), ring)]
    reshape x1 -> x0, local copies, waits for them, and re-layouts: 20.4 us -> none  [local(): inner = inner.reshape(local_modes, rows_here, pair_count, cells)]
    ppermute x2 -> x15, waiting for transfers between devices: 1.39 us -> 19.9 us  [the longest x8 9.14 us: local(): step = lambda a: lax.ppermute(a, ('z', 'core'), ring)]
    pallas_call x0 -> x10, Pallas kernels: none -> 17.2 us  [the longest x5 10.5 us: collide_part(): pl.pallas_call(functools.partial(collide_kernel, pieces, len(more), last)...]
    dot_general x2 -> x0, matrix products: 16.6 us -> none  [the longest x1 16 us: local(): lax.dot_general(piece.reshape(local_modes * rows_here, width), right_flat...]
    all_to_all x0 -> x1, blocking collectives: none -> 15.2 us  [local(): lax.all_to_all(parts, ('y', 'xl', 'core'), split_axis=0, concat_axis=0, t...]
    gather x4 -> x0, local copies, waits for them, and re-layouts: 14.7 us -> none  [the longest x1 5.5 us: local(): right_flat = coeffs[pairs[:, 1]].reshape(pair_count * cells, width)]
  transfers between devices with their start and end apart: 4 -> 15, of which waited for: 3 -> 8; matrix products, arithmetic and copies ran while one was open for 10% -> 0% of each run, Pallas kernels for 0% -> 17%
where the time goes in v2:
time: 85.9 us; the launch traced here: 85.8 us
  starting transfers between devices  32.2 us (37%)
  waiting for transfers between devices  19.9 us (23%)
  Pallas kernels  17.2 us (20%)
  blocking collectives  15.2 us (18%)
    ppermute x8, starting transfers between devices, local(): step = lambda a: lax.ppermute(a, ('z', 'core'), ring)  21.4 us
    all_to_all x1, blocking collectives, local(): lax.all_to_all(parts, ('y', 'xl', 'core'), split_axis=0, concat_axis=0, t...  15.2 us
    pallas_call x5, Pallas kernels, collide_part(): pl.pallas_call(functools.partial(collide_kernel, pieces, len(more), last)...  10.5 us
    ppermute x8, waiting for transfers between devices, local(): step = lambda a: lax.ppermute(a, ('z', 'core'), ring)  9.14 us
    ppermute x2, starting transfers between devices, local(): both = lambda a: jnp.concatenate([a, lax.ppermute(a, 'core', SWAP)])  4.05 us
    ppermute x1, waiting for transfers between devices, local(): other = lax.ppermute(tensor, 'xh', SWAP)  3.98 us
    ppermute x1, starting transfers between devices, local(): before = lax.ppermute(last, BRICK, onward)  3.4 us
    ppermute x1, waiting for transfers between devices, local(): behind = lax.ppermute(first, BRICK, backward)  3.06 us
  transfers between devices with their start and end apart: 15, of which 8 were waited for; matrix products, arithmetic and copies ran while one was open for 0% of the time, Pallas kernels for 17%

profile of v2, /device:TPU:1, one launch (start us, length us, event | category | flops | bytes accessed | tf_op | source)
XLA Modules:
  0.0 85.8 jit_solution(6265599614424996442)
XLA Ops:
  0.0 3.2 %collective-permute-start = (bf16[1,4,32,1024]{3,2,1,0:T(8,128)(2,1)}, bf16[1,4,32,1024]{3,2,1,0:T(8,128)(2,1)S(1)}, u32[]{:S(2)}, u32[]{:S(2)}) collective-permute-start(bf16[1,4,32,1024]{3,2,1,0:T(8,128)(2,1)} %bitcast.5), channel_id=1, source_target_pairs={{0,1},{1,0},{2,3},{3,2},{4,5},{5,4},{6,7},{7,6},{8,9},{9,8},{10,11... | collective-permute-start | bytes 786440 | tf_op jit(solution)/shard_map/ppermute | solution.py:271
  3.2 0.7 copy-done.1
  3.9 2.8 %prepare.1 = (bf16[2,512,1024]{2,1,0:T(8,128)(2,1)S(1)}, bf16[2,32,32,512]{3,2,1,0:T(8,128)(2,1)S(1)}) custom-call(s32[2,2]{1,0:T(2,128)S(1)} %copy-done.1, bf16[8,512,1024]{2,1,0:T(8,128)(2,1)} %coeffs.3), custom_call_target="tpu_custom_call" | custom-call | bytes 14680064 | tf_op jit(solution)/shard_map/prepare/pallas_call | solution.py:47
  6.9 0.5 collective-permute-start.6
  7.4 3.8 %collective-permute-start.1 = (bf16[2,4,32,1024]{3,2,1,0:T(8,128)(2,1)S(1)}, bf16[2,4,32,1024]{3,2,1,0:T(8,128)(2,1)S(1)}, u32[]{:S(2)}, u32[]{:S(2)}) collective-permute-start(bf16[2,4,32,1024]{3,2,1,0:T(8,128)(2,1)S(1)} %pad_maximum_fusion), channel_id=1, source_target_pairs={{0,4},{4,8},{8,12},{12,16},{16,20},{20,24},{24,28},{28,0},{5,1},{9... | collective-permute-start | bytes 1572872 | tf_op jit(solution)/shard_map/ppermute | solution.py:270
  11.2 2.7 %collective-permute-start.2 = (bf16[1,4,32,1024]{3,2,1,0:T(8,128)(2,1)S(1)}, bf16[1,4,32,1024]{3,2,1,0:T(8,128)(2,1)S(1)}, u32[]{:S(2)}, u32[]{:S(2)}) collective-permute-start(bf16[1,4,32,1024]{3,2,1,0:T(8,128)(2,1)S(1)} %bitcast.7), channel_id=1, source_target_pairs={{0,2},{2,0},{1,3},{3,1},{4,6},{6,4},{5,7},{7,5},{8,10},{10,8},{9,1... | collective-permute-start | bytes 786440 | tf_op jit(solution)/shard_map/ppermute | solution.py:274
  14.0 4.0 %collective-permute-done.2.refs_1_ = bf16[1,4,32,1024]{3,2,1,0:T(8,128)(2,1)S(1)} collective-permute-done((bf16[1,4,32,1024]{3,2,1,0:T(8,128)(2,1)S(1)}, bf16[1,4,32,1024]{3,2,1,0:T(8,128)(2,1)S(1)}, u32[]{:S(2)}, u32[]{:S(2)}) %collective-permute-start.2) | collective-permute-done | bytes 262176 | tf_op jit(solution)/shard_map/ppermute | solution.py:274
  17.9 0.8 collective-permute-start.3
  18.8 1.2 %collective-permute-done.3 = bf16[1,4,32,1024]{3,2,1,0:T(8,128)(2,1)S(1)} collective-permute-done((bf16[1,4,32,1024]{3,2,1,0:T(8,128)(2,1)S(1)}, bf16[1,4,32,1024]{3,2,1,0:T(8,128)(2,1)S(1)}, u32[]{:S(2)}, u32[]{:S(2)}) %collective-permute-start.3) | collective-permute-done | bytes 262176 | tf_op jit(solution)/shard_map/ppermute | solution.py:271
  20.0 3.2 %collective-permute-start.4 = (bf16[2,4,32,1024]{3,2,1,0:T(8,128)(2,1)S(1)}, bf16[2,4,32,1024]{3,2,1,0:T(8,128)(2,1)S(1)}, u32[]{:S(2)}, u32[]{:S(2)}) collective-permute-start(bf16[2,4,32,1024]{3,2,1,0:T(8,128)(2,1)S(1)} %pad_maximum_fusion.1), channel_id=1, source_target_pairs={{0,4},{4,8},{8,12},{12,16},{16,20},{20,24},{24,28},{28,0},{5,1},{9... | collective-permute-start | bytes 1572872 | tf_op jit(solution)/shard_map/ppermute | solution.py:270
  23.2 1.1 %collective-permute-start.8 = (bf16[2,4,32,1024]{3,2,1,0:T(8,128)(2,1)S(1)}, bf16[2,4,32,1024]{3,2,1,0:T(8,128)(2,1)S(1)}, u32[]{:S(2)}, u32[]{:S(2)}) collective-permute-start(bf16[2,4,32,1024]{3,2,1,0:T(8,128)(2,1)S(1)} %collective-permute-done.1.refs_2_), channel_id=1, source_target_pairs={{0,4},{4,8},{8,12},{12,16},{16,20},{20,24},{24,28},{28,0},{5,1},{9... | collective-permute-start | bytes 1572872 | tf_op jit(solution)/shard_map/ppermute | solution.py:270
  24.2 2.4 %collide.5.refs_6_ = f32[2,8,512]{2,1,0:T(8,128)S(1)} custom-call(bf16[1,4,32,1024]{3,2,1,0:T(8,128)(2,1)S(1)} %bitcast.8, bf16[1,4,32,1024]{3,2,1,0:T(8,128)(2,1)S(1)} %collective-permute-done.2.refs_1_, bf16[2,4,32,1024]{3,2,1,0:T(8,128)(2,1)S(1)} %collective-permute-done.1.refs_2_, bf16[2,512,1024]{2,1,0:T(8,128)(2,1)S(1)} %get-tuple-element.33.refs_3_.refs_2_.refs_1_, ...), custom_call_target="tpu_custom_call" | custom-call | flops 2147483648 | bytes 4194304 | tf_op jit(solution)/shard_map/collide/pallas_call | solution.py:157
  26.6 2.7 %collective-permute-done.4.refs_0_ = bf16[2,4,32,1024]{3,2,1,0:T(8,128)(2,1)S(1)} collective-permute-done((bf16[2,4,32,1024]{3,2,1,0:T(8,128)(2,1)S(1)}, bf16[2,4,32,1024]{3,2,1,0:T(8,128)(2,1)S(1)}, u32[]{:S(2)}, u32[]{:S(2)}) %collective-permute-start.4) | collective-permute-done | bytes 524320 | tf_op jit(solution)/shard_map/ppermute | solution.py:270
  29.3 3.1 %collective-permute-start.7 = (bf16[2,4,32,1024]{3,2,1,0:T(8,128)(2,1)S(1)}, bf16[2,4,32,1024]{3,2,1,0:T(8,128)(2,1)S(1)}, u32[]{:S(2)}, u32[]{:S(2)}) collective-permute-start(bf16[2,4,32,1024]{3,2,1,0:T(8,128)(2,1)S(1)} %collective-permute-done.4.refs_0_), channel_id=1, source_target_pairs={{0,4},{4,8},{8,12},{12,16},{16,20},{20,24},{24,28},{28,0},{5,1},{9... | collective-permute-start | bytes 1572872 | tf_op jit(solution)/shard_map/ppermute | solution.py:270
  32.4 2.5 %collective-permute-done.8.refs_1_ = bf16[2,4,32,1024]{3,2,1,0:T(8,128)(2,1)S(1)} collective-permute-done((bf16[2,4,32,1024]{3,2,1,0:T(8,128)(2,1)S(1)}, bf16[2,4,32,1024]{3,2,1,0:T(8,128)(2,1)S(1)}, u32[]{:S(2)}, u32[]{:S(2)}) %collective-permute-start.8) | collective-permute-done | bytes 524320 | tf_op jit(solution)/shard_map/ppermute | solution.py:270
  34.9 3.1 %collective-permute-start.10 = (bf16[2,4,32,1024]{3,2,1,0:T(8,128)(2,1)S(1)}, bf16[2,4,32,1024]{3,2,1,0:T(8,128)(2,1)S(1)}, u32[]{:S(2)}, u32[]{:S(2)}) collective-permute-start(bf16[2,4,32,1024]{3,2,1,0:T(8,128)(2,1)S(1)} %collective-permute-done.8.refs_1_), channel_id=1, source_target_pairs={{0,4},{4,8},{8,12},{12,16},{16,20},{20,24},{24,28},{28,0},{5,1},{9... | collective-permute-start | bytes 1572872 | tf_op jit(solution)/shard_map/ppermute | solution.py:270
  38.0 2.3 %window.1 = (f32[32,8,512]{2,1,0:T(8,128)S(1)}, f32[2,8,128]{2,1,0:T(8,128)S(1)}, f32[8,128]{1,0:T(8,128)S(1)}) custom-call(s32[2,2]{1,0:T(2,128)S(1)} %copy-done.2, f32[8]{0:T(128)S(1)} %copy-done.3, bf16[8,512,1024]{2,1,0:T(8,128)(2,1)} %coeffs.3), custom_call_target="tpu_custom_call" | custom-call | bytes 8388608 | tf_op jit(solution)/shard_map/window/pallas_call | solution.py:83
  40.5 2.4 %collide.6.refs_6_ = f32[2,8,512]{2,1,0:T(8,128)S(1)} custom-call(bf16[2,4,32,1024]{3,2,1,0:T(8,128)(2,1)S(1)} %collective-permute-done.4.refs_0_, bf16[2,4,32,1024]{3,2,1,0:T(8,128)(2,1)S(1)} %collective-permute-done.8.refs_1_, bf16[2,512,1024]{2,1,0:T(8,128)(2,1)S(1)} %get-tuple-element.33.refs_3_.refs_2_.refs_1_, ...), custom_call_target="tpu_custom_call" | custom-call | flops 2147483648 | bytes 4194304 | tf_op jit(solution)/shard_map/collide/pallas_call | solution.py:157
  42.9 0.8 collective-permute-start.9
  43.6 2.5 %collective-permute-done.10.refs_1_ = bf16[2,4,32,1024]{3,2,1,0:T(8,128)(2,1)S(1)} collective-permute-done((bf16[2,4,32,1024]{3,2,1,0:T(8,128)(2,1)S(1)}, bf16[2,4,32,1024]{3,2,1,0:T(8,128)(2,1)S(1)}, u32[]{:S(2)}, u32[]{:S(2)}) %collective-permute-start.10) | collective-permute-done | bytes 524320 | tf_op jit(solution)/shard_map/ppermute | solution.py:270
  46.2 3.2 %collective-permute-start.12 = (bf16[1,4,32,1024]{3,2,1,0:T(8,128)(2,1)S(1)}, bf16[1,4,32,1024]{3,2,1,0:T(8,128)(2,1)S(1)}, u32[]{:S(2)}, u32[]{:S(2)}) collective-permute-start(bf16[1,4,32,1024]{3,2,1,0:T(8,128)(2,1)S(1)} %slice.8), channel_id=1, source_target_pairs={{0,4},{4,8},{8,12},{12,16},{16,20},{20,24},{24,28},{28,0},{5,1},{9... | collective-permute-start | bytes 786440 | tf_op jit(solution)/shard_map/ppermute | solution.py:270
  49.4 2.4 %collide.7.refs_6_ = f32[2,8,512]{2,1,0:T(8,128)S(1)} custom-call(bf16[2,4,32,1024]{3,2,1,0:T(8,128)(2,1)S(1)} %collective-permute-done.7.refs_0_, bf16[2,4,32,1024]{3,2,1,0:T(8,128)(2,1)S(1)} %collective-permute-done.10.refs_1_, bf16[2,512,1024]{2,1,0:T(8,128)(2,1)S(1)} %get-tuple-element.33.refs_3_.refs_2_.refs_1_, ...), custom_call_target="tpu_custom_call" | custom-call | flops 2147483648 | bytes 4194304 | tf_op jit(solution)/shard_map/collide/pallas_call | solution.py:157
  51.8 3.2 %collective-permute-start.11 = (bf16[1,4,32,1024]{3,2,1,0:T(8,128)(2,1)S(1)}, bf16[1,4,32,1024]{3,2,1,0:T(8,128)(2,1)S(1)}, u32[]{:S(2)}, u32[]{:S(2)}) collective-permute-start(bf16[1,4,32,1024]{3,2,1,0:T(8,128)(2,1)S(1)} %slice.6), channel_id=1, source_target_pairs={{0,4},{4,8},{8,12},{12,16},{16,20},{20,24},{24,28},{28,0},{5,1},{9... | collective-permute-start | bytes 786440 | tf_op jit(solution)/shard_map/ppermute | solution.py:270
  55.0 1.8 %collide.8.refs_5_ = f32[2,8,512]{2,1,0:T(8,128)S(1)} custom-call(bf16[2,4,32,1024]{3,2,1,0:T(8,128)(2,1)S(1)} %collective-permute-done.9.refs_0_, bf16[1,4,32,1024]{3,2,1,0:T(8,128)(2,1)S(1)} %collective-permute-done.12.refs_1_, bf16[2,512,1024]{2,1,0:T(8,128)(2,1)S(1)} %get-tuple-element.33.refs_3_.refs_2_.refs_1_, ...), custom_call_target="tpu_custom_call" | custom-call | flops 1610612736 | bytes 4194304 | tf_op jit(solution)/shard_map/collide/pallas_call | solution.py:157
  56.8 1.5 %collective-permute-done.11.refs_0_ = bf16[1,4,32,1024]{3,2,1,0:T(8,128)(2,1)S(1)} collective-permute-done((bf16[1,4,32,1024]{3,2,1,0:T(8,128)(2,1)S(1)}, bf16[1,4,32,1024]{3,2,1,0:T(8,128)(2,1)S(1)}, u32[]{:S(2)}, u32[]{:S(2)}) %collective-permute-start.11) | collective-permute-done | bytes 262176 | tf_op jit(solution)/shard_map/ppermute | solution.py:270
  58.3 1.5 %collide.9 = f32[8,2,8,512]{3,2,1,0:T(8,128)S(1)} custom-call(bf16[1,4,32,1024]{3,2,1,0:T(8,128)(2,1)S(1)} %collective-permute-done.11.refs_0_, bf16[2,512,1024]{2,1,0:T(8,128)(2,1)S(1)} %get-tuple-element.33.refs_3_.refs_2_.refs_1_, bf16[2,512,1024]{2,1,0:T(8,128)(2,1)S(1)} %collective-permute-done.5.refs_4_.refs_3_.refs_2_, ...), custom_call_target="tpu_custom_call" | custom-call | flops 536870912 | bytes 4194304 | tf_op jit(solution)/shard_map/collide/pallas_call | solution.py:157
  59.8 15.2 %all_to_all.5 = f32[16,8,512]{2,1,0:T(8,128)S(1)} all-to-all(f32[16,8,512]{2,1,0:T(8,128)S(1)} %bitcast.3), channel_id=1, replica_groups=mesh['y'=4,'xl'=2,'z'=8,'xh'=2,'core'=2] {'y','xl','core'}, dimensions={0} | all-to-all | bytes 524288 | tf_op jit(solution)/shard_map/all_to_all | solution.py:302
  75.1 3.4 %collective-permute-start.13 = (f32[32,8,128]{2,1,0:T(8,128)S(1)}, f32[32,8,128]{2,1,0:T(8,128)S(1)}, u32[]{:S(2)}, u32[]{:S(2)}) collective-permute-start(f32[32,8,128]{2,1,0:T(8,128)S(1)} %get-tuple-element.51), channel_id=1, source_target_pairs={{0,1},{1,2},{2,3},{3,4},{4,5},{5,6},{6,7},{7,8},{8,9},{9,10},{10,1... | collective-permute-start | bytes 393224 | tf_op jit(solution)/shard_map/ppermute | solution.py:306
  78.6 0.7 inner.1
  79.3 2.6 %collective-permute-done.13.before = f32[32,8,128]{2,1,0:T(8,128)S(1)} collective-permute-done((f32[32,8,128]{2,1,0:T(8,128)S(1)}, f32[32,8,128]{2,1,0:T(8,128)S(1)}, u32[]{:S(2)}, u32[]{:S(2)}) %collective-permute-start.13) | collective-permute-done | bytes 131104 | tf_op jit(solution)/shard_map/ppermute | solution.py:306
  81.9 3.1 %collective-permute-done.14.behind = f32[32,8,128]{2,1,0:T(8,128)S(1)} collective-permute-done((f32[32,8,128]{2,1,0:T(8,128)S(1)}, f32[32,8,128]{2,1,0:T(8,128)S(1)}, u32[]{:S(2)}, u32[]{:S(2)}) %collective-permute-start.14) | collective-permute-done | bytes 131104 | tf_op jit(solution)/shard_map/ppermute | solution.py:307
  84.9 0.9 outer.1
  (24 shorter events, 0.6 us)
Async XLA Ops:
  0.0 6.7 %copy-start = (bf16[4,32,1024]{2,1,0:T(8,128)(2,1)S(1)}, bf16[4,32,1024]{2,1,0:T(8,128)(2,1)}, u32[]{:S(2)}) copy-start(bf16[4,32,1024]{2,1,0:T(8,128)(2,1)} %param.6) | copy-start | bytes 786436
  0.0 6.7 %collective-permute-start = (bf16[1,4,32,1024]{3,2,1,0:T(8,128)(2,1)}, bf16[1,4,32,1024]{3,2,1,0:T(8,128)(2,1)S(1)}, u32[]{:S(2)}, u32[]{:S(2)}) collective-permute-start(bf16[1,4,32,1024]{3,2,1,0:T(8,128)(2,1)} %bitcast.5), channel_id=1, source_target_pairs={{0,1},{1,0},{2,3},{3,2},{4,5},{5,4},{6,7},{7,6},{8,9},{9,8},{10,11... | collective-permute-start | bytes 786440 | tf_op jit(solution)/shard_map/ppermute | solution.py:271
  3.2 0.7 copy-start.1
  6.8 17.4 %collective-permute-start.5 = (bf16[2,512,1024]{2,1,0:T(8,128)(2,1)S(1)}, bf16[2,512,1024]{2,1,0:T(8,128)(2,1)S(1)}, u32[]{:S(2)}, u32[]{:S(2)}) collective-permute-start(bf16[2,512,1024]{2,1,0:T(8,128)(2,1)S(1)} %get-tuple-element.33.refs_3_.refs_2_.refs_1_), channel_id=1, source_target_pairs={{0,1},{1,0},{2,3},{3,2},{4,5},{5,4},{6,7},{7,6},{8,9},{9,8},{10,11... | collective-permute-start | bytes 6291464 | tf_op jit(solution)/shard_map/ppermute | solution.py:279
  6.9 17.3 %collective-permute-start.6 = (bf16[2,32,32,512]{3,2,1,0:T(8,128)(2,1)S(1)}, bf16[2,32,32,512]{3,2,1,0:T(8,128)(2,1)S(1)}, u32[]{:S(2)}, u32[]{:S(2)}) collective-permute-start(bf16[2,32,32,512]{3,2,1,0:T(8,128)(2,1)S(1)} %get-tuple-element.34.refs_5_.refs_4_.refs_3_), channel_id=1, source_target_pairs={{0,1},{1,0},{2,3},{3,2},{4,5},{5,4},{6,7},{7,6},{8,9},{9,8},{10,11... | collective-permute-start | bytes 6291464 | tf_op jit(solution)/shard_map/ppermute | solution.py:280
  7.4 10.6 %collective-permute-start.1 = (bf16[2,4,32,1024]{3,2,1,0:T(8,128)(2,1)S(1)}, bf16[2,4,32,1024]{3,2,1,0:T(8,128)(2,1)S(1)}, u32[]{:S(2)}, u32[]{:S(2)}) collective-permute-start(bf16[2,4,32,1024]{3,2,1,0:T(8,128)(2,1)S(1)} %pad_maximum_fusion), channel_id=1, source_target_pairs={{0,4},{4,8},{8,12},{12,16},{16,20},{20,24},{24,28},{28,0},{5,1},{9... | collective-permute-start | bytes 1572872 | tf_op jit(solution)/shard_map/ppermute | solution.py:270
  11.2 6.7 %collective-permute-start.2 = (bf16[1,4,32,1024]{3,2,1,0:T(8,128)(2,1)S(1)}, bf16[1,4,32,1024]{3,2,1,0:T(8,128)(2,1)S(1)}, u32[]{:S(2)}, u32[]{:S(2)}) collective-permute-start(bf16[1,4,32,1024]{3,2,1,0:T(8,128)(2,1)S(1)} %bitcast.7), channel_id=1, source_target_pairs={{0,2},{2,0},{1,3},{3,1},{4,6},{6,4},{5,7},{7,5},{8,10},{10,8},{9,1... | collective-permute-start | bytes 786440 | tf_op jit(solution)/shard_map/ppermute | solution.py:274
  17.9 2.0 %collective-permute-start.3 = (bf16[1,4,32,1024]{3,2,1,0:T(8,128)(2,1)S(1)}, bf16[1,4,32,1024]{3,2,1,0:T(8,128)(2,1)S(1)}, u32[]{:S(2)}, u32[]{:S(2)}) collective-permute-start(bf16[1,4,32,1024]{3,2,1,0:T(8,128)(2,1)S(1)} %collective-permute-done.2.refs_1_), channel_id=1, source_target_pairs={{0,1},{1,0},{2,3},{3,2},{4,5},{5,4},{6,7},{7,6},{8,9},{9,8},{10,11... | collective-permute-start | bytes 786440 | tf_op jit(solution)/shard_map/ppermute | solution.py:271
  20.0 18.0 %copy-start.2 = (s32[2,2]{1,0:T(2,128)S(1)}, s32[2,2]{1,0:T(2,128)}, u32[]{:S(2)}) copy-start(s32[2,2]{1,0:T(2,128)} %pairs.2) | copy-start | bytes 52
  20.0 18.0 %copy-start.3 = (f32[8]{0:T(128)S(1)}, f32[8]{0:T(128)}, u32[]{:S(2)}) copy-start(f32[8]{0:T(128)} %thermal.1) | copy-start | bytes 100
  20.0 9.3 %collective-permute-start.4 = (bf16[2,4,32,1024]{3,2,1,0:T(8,128)(2,1)S(1)}, bf16[2,4,32,1024]{3,2,1,0:T(8,128)(2,1)S(1)}, u32[]{:S(2)}, u32[]{:S(2)}) collective-permute-start(bf16[2,4,32,1024]{3,2,1,0:T(8,128)(2,1)S(1)} %pad_maximum_fusion.1), channel_id=1, source_target_pairs={{0,4},{4,8},{8,12},{12,16},{16,20},{20,24},{24,28},{28,0},{5,1},{9... | collective-permute-start | bytes 1572872 | tf_op jit(solution)/shard_map/ppermute | solution.py:270
  23.2 11.7 %collective-permute-start.8 = (bf16[2,4,32,1024]{3,2,1,0:T(8,128)(2,1)S(1)}, bf16[2,4,32,1024]{3,2,1,0:T(8,128)(2,1)S(1)}, u32[]{:S(2)}, u32[]{:S(2)}) collective-permute-start(bf16[2,4,32,1024]{3,2,1,0:T(8,128)(2,1)S(1)} %collective-permute-done.1.refs_2_), channel_id=1, source_target_pairs={{0,4},{4,8},{8,12},{12,16},{16,20},{20,24},{24,28},{28,0},{5,1},{9... | collective-permute-start | bytes 1572872 | tf_op jit(solution)/shard_map/ppermute | solution.py:270
  26.6 13.7 %copy-start.4 = (s32[512]{0:T(512)S(1)}, s32[512]{0:T(512)}, u32[]{:S(2)}) copy-start(s32[512]{0:T(512)} %param.8) | copy-start | bytes 6148
  29.3 13.6 %collective-permute-start.7 = (bf16[2,4,32,1024]{3,2,1,0:T(8,128)(2,1)S(1)}, bf16[2,4,32,1024]{3,2,1,0:T(8,128)(2,1)S(1)}, u32[]{:S(2)}, u32[]{:S(2)}) collective-permute-start(bf16[2,4,32,1024]{3,2,1,0:T(8,128)(2,1)S(1)} %collective-permute-done.4.refs_0_), channel_id=1, source_target_pairs={{0,4},{4,8},{8,12},{12,16},{16,20},{20,24},{24,28},{28,0},{5,1},{9... | collective-permute-start | bytes 1572872 | tf_op jit(solution)/shard_map/ppermute | solution.py:270
  34.9 11.2 %collective-permute-start.10 = (bf16[2,4,32,1024]{3,2,1,0:T(8,128)(2,1)S(1)}, bf16[2,4,32,1024]{3,2,1,0:T(8,128)(2,1)S(1)}, u32[]{:S(2)}, u32[]{:S(2)}) collective-permute-start(bf16[2,4,32,1024]{3,2,1,0:T(8,128)(2,1)S(1)} %collective-permute-done.8.refs_1_), channel_id=1, source_target_pairs={{0,4},{4,8},{8,12},{12,16},{16,20},{20,24},{24,28},{28,0},{5,1},{9... | collective-permute-start | bytes 1572872 | tf_op jit(solution)/shard_map/ppermute | solution.py:270
  42.9 8.9 %collective-permute-start.9 = (bf16[2,4,32,1024]{3,2,1,0:T(8,128)(2,1)S(1)}, bf16[2,4,32,1024]{3,2,1,0:T(8,128)(2,1)S(1)}, u32[]{:S(2)}, u32[]{:S(2)}) collective-permute-start(bf16[2,4,32,1024]{3,2,1,0:T(8,128)(2,1)S(1)} %collective-permute-done.7.refs_0_), channel_id=1, source_target_pairs={{0,4},{4,8},{8,12},{12,16},{16,20},{20,24},{24,28},{28,0},{5,1},{9... | collective-permute-start | bytes 1572872 | tf_op jit(solution)/shard_map/ppermute | solution.py:270
  46.2 8.8 %collective-permute-start.12 = (bf16[1,4,32,1024]{3,2,1,0:T(8,128)(2,1)S(1)}, bf16[1,4,32,1024]{3,2,1,0:T(8,128)(2,1)S(1)}, u32[]{:S(2)}, u32[]{:S(2)}) collective-permute-start(bf16[1,4,32,1024]{3,2,1,0:T(8,128)(2,1)S(1)} %slice.8), channel_id=1, source_target_pairs={{0,4},{4,8},{8,12},{12,16},{16,20},{20,24},{24,28},{28,0},{5,1},{9... | collective-permute-start | bytes 786440 | tf_op jit(solution)/shard_map/ppermute | solution.py:270
  51.8 6.5 %collective-permute-start.11 = (bf16[1,4,32,1024]{3,2,1,0:T(8,128)(2,1)S(1)}, bf16[1,4,32,1024]{3,2,1,0:T(8,128)(2,1)S(1)}, u32[]{:S(2)}, u32[]{:S(2)}) collective-permute-start(bf16[1,4,32,1024]{3,2,1,0:T(8,128)(2,1)S(1)} %slice.6), channel_id=1, source_target_pairs={{0,4},{4,8},{8,12},{12,16},{16,20},{20,24},{24,28},{28,0},{5,1},{9... | collective-permute-start | bytes 786440 | tf_op jit(solution)/shard_map/ppermute | solution.py:270
  75.1 6.7 %collective-permute-start.13 = (f32[32,8,128]{2,1,0:T(8,128)S(1)}, f32[32,8,128]{2,1,0:T(8,128)S(1)}, u32[]{:S(2)}, u32[]{:S(2)}) collective-permute-start(f32[32,8,128]{2,1,0:T(8,128)S(1)} %get-tuple-element.51), channel_id=1, source_target_pairs={{0,1},{1,2},{2,3},{3,4},{4,5},{5,6},{6,7},{7,8},{8,9},{9,10},{10,1... | collective-permute-start | bytes 393224 | tf_op jit(solution)/shard_map/ppermute | solution.py:306
  78.6 6.4 %collective-permute-start.14 = (f32[32,8,128]{2,1,0:T(8,128)S(1)}, f32[32,8,128]{2,1,0:T(8,128)S(1)}, u32[]{:S(2)}, u32[]{:S(2)}) collective-permute-start(f32[32,8,128]{2,1,0:T(8,128)S(1)} %get-tuple-element.52), channel_id=1, source_target_pairs={{1,0},{2,1},{3,2},{4,3},{5,4},{6,5},{7,6},{8,7},{9,8},{10,9},{11,1... | collective-permute-start | bytes 393224 | tf_op jit(solution)/shard_map/ppermute | solution.py:307

commit v3 on v2

--- a/solution.py
+++ b/solution.py
@@ -24,38 +24,69 @@
 SWAP = [(0, 1), (1, 0)]
 
 
-def prepare_kernel(pairs, coeffs, right_out, left_out, left, sems):
-    copies = []
-    for p in range(2):
-        copies.append(pltpu.make_async_copy(coeffs.at[pairs[p, 0]], left.at[p], sems.at[p]))
-        copies.append(pltpu.make_async_copy(coeffs.at[pairs[p, 1]], right_out.at[p], sems.at[2 + p]))
+BLOCKS = [(0, 0, 0), (1, 0, 0)]
+BLOCKS += [(column, swapped, steps) for steps in (1, 2, 3) for column in (0, 1) for swapped in (0, 1)]
+BLOCKS += [(0, 0, 4), (1, 0, 4)]
+
+
+def right_kernel(pairs, coeffs, right_out, sems):
+    copies = [pltpu.make_async_copy(coeffs.at[pairs[p, 1]], right_out.at[p], sems.at[p]) for p in range(2)]
     for c in copies:
         c.start()
+    for c in copies:
+        c.wait()
+
+
+def left_kernel(pairs, coeffs, keep, give, left, turned, sems):
+    copies = [pltpu.make_async_copy(coeffs.at[pairs[p, 0]], left.at[p], sems.at[p]) for p in range(2)]
+    for c in copies:
+        c.start()
+    z, xh, core = (lax.axis_index(a) for a in BRICK)
     for p in range(2):
-        copies[2 * p].wait()
-        left_out[p] = jnp.transpose(left[p]).reshape(left_out.shape[1:])
-    for p in range(2):
-        copies[2 * p + 1].wait()
+        copies[p].wait()
+        turned[...] = jnp.transpose(left[p]).reshape(turned.shape)
+        for out, mine in ((keep, core), (give, 1 - core)):
+            for n, (column, swapped, steps) in enumerate(BLOCKS):
+                there = lax.rem(z + steps * (2 * mine - 1) + Z, Z)
+                column_there = 1 - xh if column else xh
+                core_there = 1 - mine if swapped else mine
+                out[p, n] = turned[(there * XH + column_there) * CORE + core_there]
 
 
 VMEM = pl.BlockSpec(memory_space=pltpu.VMEM)
 SMEM = pl.BlockSpec(memory_space=pltpu.SMEM)
 
 
-def prepare(pairs, coeffs):
+def make_right(pairs, coeffs):
     _, cells, width = coeffs.shape
     return pl.pallas_call(
-        prepare_kernel,
+        right_kernel,
+        in_specs=[SMEM, pl.BlockSpec(memory_space=pltpu.HBM)],
+        out_specs=VMEM,
+        out_shape=jax.ShapeDtypeStruct((2, cells, width), coeffs.dtype),
+        scratch_shapes=[pltpu.SemaphoreType.DMA((2,))],
+        compiler_params=pltpu.CompilerParams(vmem_limit_bytes=8 * 2**20),
+        cost_estimate=pl.CostEstimate(flops=0, transcendentals=0, bytes_accessed=4 * 2**20),
+        name="right",
+    )(pairs, pltpu.with_memory_space_constraint(coeffs, pltpu.HBM))
+
+
+def make_left(pairs, coeffs):
+    _, cells, width = coeffs.shape
+    blocks = jax.ShapeDtypeStruct((2, len(BLOCKS), ROWS, cells), coeffs.dtype)
+    return pl.pallas_call(
+        left_kernel,
         in_specs=[SMEM, pl.BlockSpec(memory_space=pltpu.HBM)],
         out_specs=[VMEM] * 2,
-        out_shape=[
-            jax.ShapeDtypeStruct((2, cells, width), coeffs.dtype),
-            jax.ShapeDtypeStruct((2, width // ROWS, ROWS, cells), coeffs.dtype),
+        out_shape=[blocks, blocks],
+        scratch_shapes=[
+            pltpu.VMEM((2, cells, width), coeffs.dtype),
+            pltpu.VMEM((width // ROWS, ROWS, cells), coeffs.dtype),
+            pltpu.SemaphoreType.DMA((2,)),
         ],
-        scratch_shapes=[pltpu.VMEM((2, cells, width), coeffs.dtype), pltpu.SemaphoreType.DMA((4,))],
-        compiler_params=pltpu.CompilerParams(vmem_limit_bytes=8 * 2**20),
-        cost_estimate=pl.CostEstimate(flops=0, transcendentals=0, bytes_accessed=14 * 2**20),
-        name="prepare",
+        compiler_params=pltpu.CompilerParams(vmem_limit_bytes=10 * 2**20),
+        cost_estimate=pl.CostEstimate(flops=0, transcendentals=0, bytes_accessed=10 * 2**20),
+        name="left",
     )(pairs, pltpu.with_memory_space_constraint(coeffs, pltpu.HBM))
 
 
@@ -105,7 +136,7 @@
     rights, lefts = refs[n : n + 2], refs[n + 2 : n + 4]
     more = refs[n + 4 : n + 4 + n_more]
     out, stacked = refs[n + 4 + n_more :]
-    z, xh, core = (lax.axis_index(a) for a in BRICK)
+    core = lax.axis_index("core")
     block = MODES_HERE * ROWS
     spots = []
     row = 0
@@ -113,10 +144,7 @@
         rows = x.shape[0] * block
         stacked[row : row + rows, :] = x[...].reshape(rows, x.shape[-1])
         row += rows
-        there = lax.rem(z + steps * (2 * core - 1) + Z, Z)
-        at_column = 1 - xh if column else xh
-        for e in range(x.shape[0]):
-            spots.append((there * XH + at_column) * CORE + (core if e == 0 else 1 - core))
+        spots += [BLOCKS.index((column, e, steps)) for e in range(x.shape[0])]
     cells = rights[0].shape[1]
     for source in range(2):
         right, left = rights[source], lefts[source]
@@ -168,8 +196,9 @@
     )(*xs, *sides, *more)
 
 
-def state_kernel(parts, window, gain, state, first, last):
+def state_kernel(parts, window, gain, state, inward, outward):
     modes, species, cells = window.shape
+    core = lax.axis_index("core")
     for g in range(Y * XL):
         own = parts[g, 0] + parts[g, 1]
         for k in range(MODES_HERE):
@@ -181,10 +210,17 @@
                     r = p * MODES_HERE + k
                     value = value + gain[p] * own[r : r + 1, at]
                 state[m, :, at] = value
-                if t == 0:
-                    first[m] = value
-                if t == cells // PLANE - 1:
-                    last[m] = value
+    first, last = slice(0, PLANE), slice(cells - PLANE, cells)
+
+    @pl.when(core == 0)
+    def _():
+        inward[...] = state[:, :, last]
+        outward[...] = state[:, :, first]
+
+    @pl.when(core == 1)
+    def _():
+        inward[...] = state[:, :, first]
+        outward[...] = state[:, :, last]
 
 
 def root(k):
@@ -229,19 +265,30 @@
             out[k, :, at] = here - scale * divergence + mixing * (out[k, :, at] - here)
 
 
-def outer_kernel(inner, heat, before, behind, out):
+def outer_kernel(inner, heat, inward, outward, out):
     modes, species, cells = inner.shape
+    core = lax.axis_index("core")
     scale = courant * heat[...]
-    for k in range(modes):
-        for side, at, sign in ((before, slice(0, PLANE), -1.0), (behind, slice(cells - PLANE, cells), 1.0)):
-            divergence = -(0.5 * max_speed) * side[k]
-            if k > 0:
-                divergence += (sign * 0.5 * root(k)) * side[k - 1]
-            if k < modes - 1:
-                divergence += (sign * 0.5 * root(k + 1)) * side[k + 1]
-            out[k, :, at] = inner[k, :, at] - scale * divergence
-        middle = slice(PLANE, cells - PLANE)
-        out[k, :, middle] = inner[k, :, middle]
+
+    def work(before, behind):
+        for k in range(modes):
+            for side, at, sign in ((before, slice(0, PLANE), -1.0), (behind, slice(cells - PLANE, cells), 1.0)):
+                divergence = -(0.5 * max_speed) * side[k]
+                if k > 0:
+                    divergence += (sign * 0.5 * root(k)) * side[k - 1]
+                if k < modes - 1:
+                    divergence += (sign * 0.5 * root(k + 1)) * side[k + 1]
+                out[k, :, at] = inner[k, :, at] - scale * divergence
+            middle = slice(PLANE, cells - PLANE)
+            out[k, :, middle] = inner[k, :, middle]
+
+    @pl.when(core == 0)
+    def _():
+        work(outward, inward)
+
+    @pl.when(core == 1)
+    def _():
+        work(inward, outward)
 
 
 def simple_call(kernel, name, shapes, *operands):
@@ -263,8 +310,6 @@
     species, cells, width = coeffs.shape
     modes = tensor.shape[0] * Y * XL
     bricks = Z * XH * CORE
-    onward = [(i, (i + 1) % bricks) for i in range(bricks)]
-    backward = [((i + 1) % bricks, i) for i in range(bricks)]
 
     ring = [(CORE * i, CORE * ((i + 1) % Z)) for i in range(Z)] + [(CORE * ((i + 1) % Z) + 1, CORE * i + 1) for i in range(Z)]
     step = lambda a: lax.ppermute(a, ("z", "core"), ring)
@@ -273,28 +318,35 @@
     tensor = tensor[None]
     other = lax.ppermute(tensor, "xh", SWAP)
     own0 = both(tensor)
-    right_own, left_own = prepare(pairs, coeffs)
+    pairs_now = together(pairs, own0)[0]
+    right_own = make_right(pairs_now, coeffs)
+    left_own, left_send = make_left(pairs_now, coeffs)
     own1 = step(own0)
-    right_send, left_send = together(right_own, left_own, own0)[:2]
+    own1, other, right_own, left_own, left_send = together(own1, other, right_own, left_own, left_send)
+    alt0 = both(other)
+    alt1 = step(alt0)
+    own2 = step(own1)
+    right_send, left_send = together(right_own, left_send, alt0)[:2]
     right_sib = lax.ppermute(right_send, "core", SWAP)
     left_sib = lax.ppermute(left_send, "core", SWAP)
     sides = (right_own, right_sib, left_own, left_sib)
-    own1, other = together(own1, other)
-    alt1 = step(both(other))
-    own2 = step(own1)
-    parts = collide_part([tensor, other, own1], [(0, 0), (1, 0), (0, 1)], sides)
-    alt1, parts, pairs_now, lateral = together(alt1, parts, pairs, lateral)
-    alt2 = step(alt1)
+    pairs_now, lateral = together(pairs, lateral, alt0)[:2]
     window, gain, heat = make_window(pairs_now, thermal, coeffs, modes)
     onehot = (lax.broadcasted_iota(jnp.int32, (cells, cells), 0) == lateral[None, :]).astype(jnp.bfloat16)
+    alt1, right_sib, left_sib, window, gain, heat, onehot = together(
+        alt1, right_sib, left_sib, window, gain, heat, onehot
+    )
+    sides = (right_own, right_sib, left_own, left_sib)
+    alt2 = step(alt1)
     own3 = step(own2)
-    parts = collide_part([alt1, own2], [(1, 1), (0, 2)], sides, (parts,))
-    alt2, parts, window, gain, heat, onehot = together(alt2, parts, window, gain, heat, onehot)
+    parts = collide_part([tensor, other, own1], [(0, 0), (1, 0), (0, 1)], sides)
+    alt2, parts = together(alt2, parts)
     alt3 = step(alt2)
     own4 = step(own3[:1])
-    parts = collide_part([alt2, own3], [(1, 2), (0, 3)], sides, (parts,))
+    parts = collide_part([alt1, own2], [(1, 1), (0, 2)], sides, (parts,))
     alt3, parts = together(alt3, parts)
     alt4 = step(alt3[:1])
+    parts = collide_part([alt2, own3], [(1, 2), (0, 3)], sides, (parts,))
     parts = collide_part([alt3, own4], [(1, 3), (0, 4)], sides, (parts,))
     parts = collide_part([alt4], [(1, 4)], sides, (parts,), True)
 
@@ -302,11 +354,12 @@
     parts = lax.all_to_all(parts, ("y", "xl", "core"), split_axis=0, concat_axis=0, tiled=True)
     parts = parts.reshape(Y * XL, CORE, 2 * MODES_HERE, cells)
     full, edge = (modes, species, cells), (modes, species, PLANE)
-    state, first, last = simple_call(state_kernel, "state", (full, edge, edge), parts, window, gain)
-    before = lax.ppermute(last, BRICK, onward)
-    behind = lax.ppermute(first, BRICK, backward)
+    state, inward, outward = simple_call(state_kernel, "state", (full, edge, edge), parts, window, gain)
+    facing = [(i, (i + 1 if i % 2 else i - 1) % bricks) for i in range(bricks)]
+    outward = lax.ppermute(outward, BRICK, facing)
+    inward = lax.ppermute(inward, "core", SWAP)
     inner = simple_call(inner_kernel, "inner", (full,), state, heat, onehot)[0]
-    return simple_call(outer_kernel, "outer", (full,), inner, heat, before, behind)[0]
+    return simple_call(outer_kernel, "outer", (full,), inner, heat, inward, outward)[0]
 
 
 def solution(mesh):

time: 85.9 us -> 82.6 us (0.962)
  waiting for transfers between devices: 19.9 us -> 13.6 us
  Pallas kernels: 17.2 us -> 19.3 us
  blocking collectives: 15.2 us -> 14.2 us
  starting transfers between devices: 32.2 us -> 33.1 us
  other arithmetic: 0.24 us -> 1.13 us
    ppermute x1, waiting for transfers between devices: 3.98 us -> 0.01 us  [local(): other = lax.ppermute(tensor, 'xh', SWAP)]
    ppermute x2, waiting for transfers between devices: 5.64 us -> 2.73 us  [the longest x1 2.72 us: local(): outward = lax.ppermute(outward, BRICK, facing)]
    pallas_call x1 -> x2, Pallas kernels: 2.77 us -> 4.69 us  [the longest x1 2.58 us: make_left(): pl.pallas_call(left_kernel, in_specs=[SMEM, pl.BlockSpec(memory_space=plt...]
    ppermute x2, waiting for transfers between devices: 1.16 us -> 2.87 us  [local(): both = lambda a: jnp.concatenate([a, lax.ppermute(a, 'core', SWAP)])]
    ppermute x8, starting transfers between devices: 21.4 us -> 22.9 us  [local(): step = lambda a: lax.ppermute(a, ('z', 'core'), ring)]
    ppermute x8, waiting for transfers between devices: 9.14 us -> 8.05 us  [local(): step = lambda a: lax.ppermute(a, ('z', 'core'), ring)]
    all_to_all x1, blocking collectives: 15.2 us -> 14.2 us  [local(): lax.all_to_all(parts, ('y', 'xl', 'core'), split_axis=0, concat_axis=0, t...]
    concatenate x2 -> x1, other arithmetic: 0.1 us -> 1 us  [local(): both = lambda a: jnp.concatenate([a, lax.ppermute(a, 'core', SWAP)])]
  transfers between devices with their start and end apart: 15 -> 15, of which waited for: 8 -> 7; matrix products, arithmetic and copies ran while one was open for 0% -> 0% of each run, Pallas kernels for 17% -> 20%
where the time goes in v3:
time: 82.6 us; the launch traced here: 82.3 us
  starting transfers between devices  33.1 us (40%)
  Pallas kernels  19.3 us (23%)
  blocking collectives  14.2 us (17%)
  waiting for transfers between devices  13.6 us (16%)
  other arithmetic  1.13 us (1%)
    ppermute x8, starting transfers between devices, local(): step = lambda a: lax.ppermute(a, ('z', 'core'), ring)  22.9 us
    all_to_all x1, blocking collectives, local(): lax.all_to_all(parts, ('y', 'xl', 'core'), split_axis=0, concat_axis=0, t...  14.2 us
    pallas_call x5, Pallas kernels, collide_part(): pl.pallas_call(functools.partial(collide_kernel, pieces, len(more), last)...  10.6 us
    ppermute x8, waiting for transfers between devices, local(): step = lambda a: lax.ppermute(a, ('z', 'core'), ring)  8.05 us
    ppermute x2, starting transfers between devices, local(): both = lambda a: jnp.concatenate([a, lax.ppermute(a, 'core', SWAP)])  3.33 us
    ppermute x2, waiting for transfers between devices, local(): both = lambda a: jnp.concatenate([a, lax.ppermute(a, 'core', SWAP)])  2.87 us
    ppermute x1, starting transfers between devices, local(): other = lax.ppermute(tensor, 'xh', SWAP)  2.74 us
    ppermute x1, waiting for transfers between devices, local(): outward = lax.ppermute(outward, BRICK, facing)  2.72 us
  transfers between devices with their start and end apart: 15, of which 7 were waited for; matrix products, arithmetic and copies ran while one was open for 0% of the time, Pallas kernels for 20%

profile of v3, /device:TPU:1, one launch (start us, length us, event | category | flops | bytes accessed | tf_op | source)
XLA Modules:
  0.0 82.3 jit_solution(16082022207031531039)
XLA Ops:
  0.0 3.2 %collective-permute-start = (bf16[1,4,32,1024]{3,2,1,0:T(8,128)(2,1)}, bf16[1,4,32,1024]{3,2,1,0:T(8,128)(2,1)S(1)}, u32[]{:S(2)}, u32[]{:S(2)}) collective-permute-start(bf16[1,4,32,1024]{3,2,1,0:T(8,128)(2,1)} %bitcast.5), channel_id=1, source_target_pairs={{0,1},{1,0},{2,3},{3,2},{4,5},{5,4},{6,7},{7,6},{8,9},{9,8},{10,11... | collective-permute-start | bytes 786440 | tf_op jit(solution)/shard_map/ppermute | solution.py:316
  3.2 1.4 %collective-permute-done = bf16[1,4,32,1024]{3,2,1,0:T(8,128)(2,1)S(1)} collective-permute-done((bf16[1,4,32,1024]{3,2,1,0:T(8,128)(2,1)}, bf16[1,4,32,1024]{3,2,1,0:T(8,128)(2,1)S(1)}, u32[]{:S(2)}, u32[]{:S(2)}) %collective-permute-start) | collective-permute-done | bytes 262176 | tf_op jit(solution)/shard_map/ppermute | solution.py:316
  4.6 1.0 %pad_maximum_fusion = bf16[2,4,32,1024]{3,2,1,0:T(8,128)(2,1)S(1)} fusion(bf16[1,4,32,1024]{3,2,1,0:T(8,128)(2,1)S(1)} %collective-permute-done, bf16[1,4,32,1024]{3,2,1,0:T(8,128)(2,1)} %bitcast.6), kind=kLoop, calls=%fused_computation.2 | loop fusion | flops 262144 | bytes 1048576 | tf_op jit(solution)/shard_map/concatenate | solution.py:316
  5.6 3.9 %collective-permute-start.1 = (bf16[2,4,32,1024]{3,2,1,0:T(8,128)(2,1)S(1)}, bf16[2,4,32,1024]{3,2,1,0:T(8,128)(2,1)S(1)}, u32[]{:S(2)}, u32[]{:S(2)}) collective-permute-start(bf16[2,4,32,1024]{3,2,1,0:T(8,128)(2,1)S(1)} %pad_maximum_fusion), channel_id=1, source_target_pairs={{0,4},{4,8},{8,12},{12,16},{16,20},{20,24},{24,28},{28,0},{5,1},{9... | collective-permute-start | bytes 1572872 | tf_op jit(solution)/shard_map/ppermute | solution.py:315
  9.5 2.7 %collective-permute-start.2 = (bf16[1,4,32,1024]{3,2,1,0:T(8,128)(2,1)}, bf16[1,4,32,1024]{3,2,1,0:T(8,128)(2,1)S(1)}, u32[]{:S(2)}, u32[]{:S(2)}) collective-permute-start(bf16[1,4,32,1024]{3,2,1,0:T(8,128)(2,1)} %bitcast.7), channel_id=1, source_target_pairs={{0,2},{2,0},{1,3},{3,1},{4,6},{6,4},{5,7},{7,5},{8,10},{10,8},{9,1... | collective-permute-start | bytes 786440 | tf_op jit(solution)/shard_map/ppermute | solution.py:319
  12.3 0.7 copy-done.1
  13.0 2.6 %left.1 = (bf16[2,16,32,512]{3,2,1,0:T(8,128)(2,1)S(1)}, bf16[2,16,32,512]{3,2,1,0:T(8,128)(2,1)S(1)}) custom-call(s32[2,2]{1,0:T(2,128)S(1)} %copy-done.1, bf16[8,512,1024]{2,1,0:T(8,128)(2,1)} %coeffs.5), custom_call_target="tpu_custom_call" | custom-call | bytes 10485760 | tf_op jit(solution)/shard_map/left/pallas_call | solution.py:77
  15.6 2.1 %right.1.refs_3_.refs_2_.refs_1_ = bf16[2,512,1024]{2,1,0:T(8,128)(2,1)S(1)} custom-call(s32[2,2]{1,0:T(2,128)S(1)} %copy-done.1, bf16[8,512,1024]{2,1,0:T(8,128)(2,1)} %coeffs.5), custom_call_target="tpu_custom_call" | custom-call | bytes 4194304 | tf_op jit(solution)/shard_map/right/pallas_call | solution.py:62
  17.8 1.5 %collective-permute-done.3 = bf16[1,4,32,1024]{3,2,1,0:T(8,128)(2,1)S(1)} collective-permute-done((bf16[1,4,32,1024]{3,2,1,0:T(8,128)(2,1)S(1)}, bf16[1,4,32,1024]{3,2,1,0:T(8,128)(2,1)S(1)}, u32[]{:S(2)}, u32[]{:S(2)}) %collective-permute-start.3) | collective-permute-done | bytes 262176 | tf_op jit(solution)/shard_map/ppermute | solution.py:316
  19.6 0.4 collective-permute-start.6
  20.0 2.5 %collective-permute-start.4 = (bf16[2,4,32,1024]{3,2,1,0:T(8,128)(2,1)S(1)}, bf16[2,4,32,1024]{3,2,1,0:T(8,128)(2,1)S(1)}, u32[]{:S(2)}, u32[]{:S(2)}) collective-permute-start(bf16[2,4,32,1024]{3,2,1,0:T(8,128)(2,1)S(1)} %constant_dynamic-update-slice_fusion), channel_id=1, source_target_pairs={{0,4},{4,8},{8,12},{12,16},{16,20},{20,24},{24,28},{28,0},{5,1},{9... | collective-permute-start | bytes 1572872 | tf_op jit(solution)/shard_map/ppermute | solution.py:315
  22.5 0.7 collective-permute-start.9
  23.2 2.3 %window.1 = (f32[32,8,512]{2,1,0:T(8,128)S(1)}, f32[2,8,128]{2,1,0:T(8,128)S(1)}, f32[8,128]{1,0:T(8,128)S(1)}) custom-call(s32[2,2]{1,0:T(2,128)S(1)} %copy-done.1, f32[8]{0:T(128)S(1)} %copy-done.2, bf16[8,512,1024]{2,1,0:T(8,128)(2,1)} %coeffs.5), custom_call_target="tpu_custom_call" | custom-call | bytes 8388608 | tf_op jit(solution)/shard_map/window/pallas_call | solution.py:114
  25.7 2.9 %collective-permute-done.4.refs_0_ = bf16[2,4,32,1024]{3,2,1,0:T(8,128)(2,1)S(1)} collective-permute-done((bf16[2,4,32,1024]{3,2,1,0:T(8,128)(2,1)S(1)}, bf16[2,4,32,1024]{3,2,1,0:T(8,128)(2,1)S(1)}, u32[]{:S(2)}, u32[]{:S(2)}) %collective-permute-start.4) | collective-permute-done | bytes 524320 | tf_op jit(solution)/shard_map/ppermute | solution.py:315
  28.6 3.1 %collective-permute-start.7 = (bf16[2,4,32,1024]{3,2,1,0:T(8,128)(2,1)S(1)}, bf16[2,4,32,1024]{3,2,1,0:T(8,128)(2,1)S(1)}, u32[]{:S(2)}, u32[]{:S(2)}) collective-permute-start(bf16[2,4,32,1024]{3,2,1,0:T(8,128)(2,1)S(1)} %collective-permute-done.4.refs_0_), channel_id=1, source_target_pairs={{0,4},{4,8},{8,12},{12,16},{16,20},{20,24},{24,28},{28,0},{5,1},{9... | collective-permute-start | bytes 1572872 | tf_op jit(solution)/shard_map/ppermute | solution.py:315
  31.8 2.5 %collective-permute-done.9.refs_1_ = bf16[2,4,32,1024]{3,2,1,0:T(8,128)(2,1)S(1)} collective-permute-done((bf16[2,4,32,1024]{3,2,1,0:T(8,128)(2,1)S(1)}, bf16[2,4,32,1024]{3,2,1,0:T(8,128)(2,1)S(1)}, u32[]{:S(2)}, u32[]{:S(2)}) %collective-permute-start.9) | collective-permute-done | bytes 524320 | tf_op jit(solution)/shard_map/ppermute | solution.py:315
  34.3 3.1 %collective-permute-start.11 = (bf16[2,4,32,1024]{3,2,1,0:T(8,128)(2,1)S(1)}, bf16[2,4,32,1024]{3,2,1,0:T(8,128)(2,1)S(1)}, u32[]{:S(2)}, u32[]{:S(2)}) collective-permute-start(bf16[2,4,32,1024]{3,2,1,0:T(8,128)(2,1)S(1)} %collective-permute-done.9.refs_1_), channel_id=1, source_target_pairs={{0,4},{4,8},{8,12},{12,16},{16,20},{20,24},{24,28},{28,0},{5,1},{9... | collective-permute-start | bytes 1572872 | tf_op jit(solution)/shard_map/ppermute | solution.py:315
  37.4 2.4 %collide.5.refs_6_ = f32[2,8,512]{2,1,0:T(8,128)S(1)} custom-call(bf16[1,4,32,1024]{3,2,1,0:T(8,128)(2,1)S(1)} %bitcast.8, bf16[1,4,32,1024]{3,2,1,0:T(8,128)(2,1)S(1)} %collective-permute-done.2.refs_1_, bf16[2,4,32,1024]{3,2,1,0:T(8,128)(2,1)S(1)} %collective-permute-done.1.refs_2_, bf16[2,512,1024]{2,1,0:T(8,128)(2,1)S(1)} %right.1.refs_3_.refs_2_.refs_1_, ...), custom_call_target="tpu_custom_call" | custom-call | flops 2147483648 | bytes 4194304 | tf_op jit(solution)/shard_map/collide/pallas_call | solution.py:185
  39.9 3.1 %collective-permute-start.8 = (bf16[2,4,32,1024]{3,2,1,0:T(8,128)(2,1)S(1)}, bf16[2,4,32,1024]{3,2,1,0:T(8,128)(2,1)S(1)}, u32[]{:S(2)}, u32[]{:S(2)}) collective-permute-start(bf16[2,4,32,1024]{3,2,1,0:T(8,128)(2,1)S(1)} %collective-permute-done.7.refs_0_), channel_id=1, source_target_pairs={{0,4},{4,8},{8,12},{12,16},{16,20},{20,24},{24,28},{28,0},{5,1},{9... | collective-permute-start | bytes 1572872 | tf_op jit(solution)/shard_map/ppermute | solution.py:315
  43.0 2.5 %collective-permute-done.11.refs_1_ = bf16[2,4,32,1024]{3,2,1,0:T(8,128)(2,1)S(1)} collective-permute-done((bf16[2,4,32,1024]{3,2,1,0:T(8,128)(2,1)S(1)}, bf16[2,4,32,1024]{3,2,1,0:T(8,128)(2,1)S(1)}, u32[]{:S(2)}, u32[]{:S(2)}) %collective-permute-start.11) | collective-permute-done | bytes 524320 | tf_op jit(solution)/shard_map/ppermute | solution.py:315
  45.5 3.4 %collective-permute-start.12 = (bf16[1,4,32,1024]{3,2,1,0:T(8,128)(2,1)S(1)}, bf16[1,4,32,1024]{3,2,1,0:T(8,128)(2,1)S(1)}, u32[]{:S(2)}, u32[]{:S(2)}) collective-permute-start(bf16[1,4,32,1024]{3,2,1,0:T(8,128)(2,1)S(1)} %slice.8), channel_id=1, source_target_pairs={{0,4},{4,8},{8,12},{12,16},{16,20},{20,24},{24,28},{28,0},{5,1},{9... | collective-permute-start | bytes 786440 | tf_op jit(solution)/shard_map/ppermute | solution.py:315
  48.9 2.4 %collide.6.refs_6_ = f32[2,8,512]{2,1,0:T(8,128)S(1)} custom-call(bf16[2,4,32,1024]{3,2,1,0:T(8,128)(2,1)S(1)} %collective-permute-done.4.refs_0_, bf16[2,4,32,1024]{3,2,1,0:T(8,128)(2,1)S(1)} %collective-permute-done.9.refs_1_, bf16[2,512,1024]{2,1,0:T(8,128)(2,1)S(1)} %right.1.refs_3_.refs_2_.refs_1_, ...), custom_call_target="tpu_custom_call" | custom-call | flops 2147483648 | bytes 4194304 | tf_op jit(solution)/shard_map/collide/pallas_call | solution.py:185
  51.3 3.0 %collective-permute-start.10 = (bf16[1,4,32,1024]{3,2,1,0:T(8,128)(2,1)S(1)}, bf16[1,4,32,1024]{3,2,1,0:T(8,128)(2,1)S(1)}, u32[]{:S(2)}, u32[]{:S(2)}) collective-permute-start(bf16[1,4,32,1024]{3,2,1,0:T(8,128)(2,1)S(1)} %slice.6), channel_id=1, source_target_pairs={{0,4},{4,8},{8,12},{12,16},{16,20},{20,24},{24,28},{28,0},{5,1},{9... | collective-permute-start | bytes 786440 | tf_op jit(solution)/shard_map/ppermute | solution.py:315
  54.3 2.4 %collide.7.refs_6_ = f32[2,8,512]{2,1,0:T(8,128)S(1)} custom-call(bf16[2,4,32,1024]{3,2,1,0:T(8,128)(2,1)S(1)} %collective-permute-done.7.refs_0_, bf16[2,4,32,1024]{3,2,1,0:T(8,128)(2,1)S(1)} %collective-permute-done.11.refs_1_, bf16[2,512,1024]{2,1,0:T(8,128)(2,1)S(1)} %right.1.refs_3_.refs_2_.refs_1_, ...), custom_call_target="tpu_custom_call" | custom-call | flops 2147483648 | bytes 4194304 | tf_op jit(solution)/shard_map/collide/pallas_call | solution.py:185
  56.7 1.9 %collide.8.refs_5_ = f32[2,8,512]{2,1,0:T(8,128)S(1)} custom-call(bf16[2,4,32,1024]{3,2,1,0:T(8,128)(2,1)S(1)} %collective-permute-done.8.refs_0_, bf16[1,4,32,1024]{3,2,1,0:T(8,128)(2,1)S(1)} %collective-permute-done.12.refs_1_, bf16[2,512,1024]{2,1,0:T(8,128)(2,1)S(1)} %right.1.refs_3_.refs_2_.refs_1_, ...), custom_call_target="tpu_custom_call" | custom-call | flops 1610612736 | bytes 4194304 | tf_op jit(solution)/shard_map/collide/pallas_call | solution.py:185
  58.6 1.5 %collide.9 = f32[8,2,8,512]{3,2,1,0:T(8,128)S(1)} custom-call(bf16[1,4,32,1024]{3,2,1,0:T(8,128)(2,1)S(1)} %collective-permute-done.10.refs_0_, bf16[2,512,1024]{2,1,0:T(8,128)(2,1)S(1)} %right.1.refs_3_.refs_2_.refs_1_, bf16[2,512,1024]{2,1,0:T(8,128)(2,1)S(1)} %collective-permute-done.5.refs_4_.refs_3_.refs_2_, ...), custom_call_target="tpu_custom_call" | custom-call | flops 536870912 | bytes 4194304 | tf_op jit(solution)/shard_map/collide/pallas_call | solution.py:185
  60.2 14.2 %all_to_all.5 = f32[16,8,512]{2,1,0:T(8,128)S(1)} all-to-all(f32[16,8,512]{2,1,0:T(8,128)S(1)} %bitcast.4), channel_id=1, replica_groups=mesh['y'=4,'xl'=2,'z'=8,'xh'=2,'core'=2] {'y','xl','core'}, dimensions={0} | all-to-all | bytes 524288 | tf_op jit(solution)/shard_map/all_to_all | solution.py:354
  74.5 1.1 %collective-permute-start.13 = (f32[32,8,128]{2,1,0:T(8,128)S(1)}, f32[32,8,128]{2,1,0:T(8,128)S(1)}, u32[]{:S(2)}, u32[]{:S(2)}) collective-permute-start(f32[32,8,128]{2,1,0:T(8,128)S(1)} %get-tuple-element.61), channel_id=1, source_target_pairs={{0,1},{1,0},{2,3},{3,2},{4,5},{5,4},{6,7},{7,6},{8,9},{9,8},{10,11... | collective-permute-start | bytes 393224 | tf_op jit(solution)/shard_map/ppermute | solution.py:360
  75.6 2.4 %collective-permute-start.14 = (f32[32,8,128]{2,1,0:T(8,128)S(1)}, f32[32,8,128]{2,1,0:T(8,128)S(1)}, u32[]{:S(2)}, u32[]{:S(2)}) collective-permute-start(f32[32,8,128]{2,1,0:T(8,128)S(1)} %get-tuple-element.62), channel_id=1, source_target_pairs={{0,31},{1,2},{2,1},{3,4},{4,3},{5,6},{6,5},{7,8},{8,7},{9,10},{10,... | collective-permute-start | bytes 393224 | tf_op jit(solution)/shard_map/ppermute | solution.py:359
  78.0 0.7 inner.1
  78.8 2.7 %collective-permute-done.14.outward = f32[32,8,128]{2,1,0:T(8,128)S(1)} collective-permute-done((f32[32,8,128]{2,1,0:T(8,128)S(1)}, f32[32,8,128]{2,1,0:T(8,128)S(1)}, u32[]{:S(2)}, u32[]{:S(2)}) %collective-permute-start.14) | collective-permute-done | bytes 131104 | tf_op jit(solution)/shard_map/ppermute | solution.py:359
  81.5 0.9 %outer.1 = f32[32,8,512]{2,1,0:T(8,128)} custom-call(f32[32,8,512]{2,1,0:T(8,128)S(1)} %inner.1, f32[8,128]{1,0:T(8,128)S(1)} %get-tuple-element.59.heat, f32[32,8,128]{2,1,0:T(8,128)S(1)} %collective-permute-done.13.inward, f32[32,8,128]{2,1,0:T(8,128)S(1)} %collective-permute-done.14.outward), custom_call_target="tpu_custom_call" | custom-call | tf_op jit(solution)/shard_map/outer/pallas_call | solution.py:295
  (24 shorter events, 0.8 us)
Async XLA Ops:
  0.0 4.6 %collective-permute-start = (bf16[1,4,32,1024]{3,2,1,0:T(8,128)(2,1)}, bf16[1,4,32,1024]{3,2,1,0:T(8,128)(2,1)S(1)}, u32[]{:S(2)}, u32[]{:S(2)}) collective-permute-start(bf16[1,4,32,1024]{3,2,1,0:T(8,128)(2,1)} %bitcast.5), channel_id=1, source_target_pairs={{0,1},{1,0},{2,3},{3,2},{4,5},{5,4},{6,7},{7,6},{8,9},{9,8},{10,11... | collective-permute-start | bytes 786440 | tf_op jit(solution)/shard_map/ppermute | solution.py:316
  5.6 12.1 %collective-permute-start.1 = (bf16[2,4,32,1024]{3,2,1,0:T(8,128)(2,1)S(1)}, bf16[2,4,32,1024]{3,2,1,0:T(8,128)(2,1)S(1)}, u32[]{:S(2)}, u32[]{:S(2)}) collective-permute-start(bf16[2,4,32,1024]{3,2,1,0:T(8,128)(2,1)S(1)} %pad_maximum_fusion), channel_id=1, source_target_pairs={{0,4},{4,8},{8,12},{12,16},{16,20},{20,24},{24,28},{28,0},{5,1},{9... | collective-permute-start | bytes 1572872 | tf_op jit(solution)/shard_map/ppermute | solution.py:315
  9.5 8.1 %collective-permute-start.2 = (bf16[1,4,32,1024]{3,2,1,0:T(8,128)(2,1)}, bf16[1,4,32,1024]{3,2,1,0:T(8,128)(2,1)S(1)}, u32[]{:S(2)}, u32[]{:S(2)}) collective-permute-start(bf16[1,4,32,1024]{3,2,1,0:T(8,128)(2,1)} %bitcast.7), channel_id=1, source_target_pairs={{0,2},{2,0},{1,3},{3,1},{4,6},{6,4},{5,7},{7,5},{8,10},{10,8},{9,1... | collective-permute-start | bytes 786440 | tf_op jit(solution)/shard_map/ppermute | solution.py:319
  12.3 0.7 copy-start.1
  15.5 7.7 %copy-start.2 = (f32[8]{0:T(128)S(1)}, f32[8]{0:T(128)}, u32[]{:S(2)}) copy-start(f32[8]{0:T(128)} %thermal.1) | copy-start | bytes 100
  17.7 1.6 %collective-permute-start.3 = (bf16[1,4,32,1024]{3,2,1,0:T(8,128)(2,1)S(1)}, bf16[1,4,32,1024]{3,2,1,0:T(8,128)(2,1)S(1)}, u32[]{:S(2)}, u32[]{:S(2)}) collective-permute-start(bf16[1,4,32,1024]{3,2,1,0:T(8,128)(2,1)S(1)} %collective-permute-done.2.refs_1_), channel_id=1, source_target_pairs={{0,1},{1,0},{2,3},{3,2},{4,5},{5,4},{6,7},{7,6},{8,9},{9,8},{10,11... | collective-permute-start | bytes 786440 | tf_op jit(solution)/shard_map/ppermute | solution.py:316
  19.3 6.2 %copy-start.3 = (s32[512]{0:T(512)S(1)}, s32[512]{0:T(512)}, u32[]{:S(2)}) copy-start(s32[512]{0:T(512)} %param.8) | copy-start | bytes 6148
  19.4 18.0 %copy-start = (bf16[4,32,1024]{2,1,0:T(8,128)(2,1)S(1)}, bf16[4,32,1024]{2,1,0:T(8,128)(2,1)}, u32[]{:S(2)}) copy-start(bf16[4,32,1024]{2,1,0:T(8,128)(2,1)} %param.6) | copy-start | bytes 786436
  19.4 9.3 %collective-permute-start.5 = (bf16[2,512,1024]{2,1,0:T(8,128)(2,1)S(1)}, bf16[2,512,1024]{2,1,0:T(8,128)(2,1)S(1)}, u32[]{:S(2)}, u32[]{:S(2)}) collective-permute-start(bf16[2,512,1024]{2,1,0:T(8,128)(2,1)S(1)} %right.1.refs_3_.refs_2_.refs_1_), channel_id=1, source_target_pairs={{0,1},{1,0},{2,3},{3,2},{4,5},{5,4},{6,7},{7,6},{8,9},{9,8},{10,11... | collective-permute-start | bytes 6291464 | tf_op jit(solution)/shard_map/ppermute | solution.py:330
  19.6 9.0 %collective-permute-start.6 = (bf16[2,16,32,512]{3,2,1,0:T(8,128)(2,1)S(1)}, bf16[2,16,32,512]{3,2,1,0:T(8,128)(2,1)S(1)}, u32[]{:S(2)}, u32[]{:S(2)}) collective-permute-start(bf16[2,16,32,512]{3,2,1,0:T(8,128)(2,1)S(1)} %get-tuple-element.41), channel_id=1, source_target_pairs={{0,1},{1,0},{2,3},{3,2},{4,5},{5,4},{6,7},{7,6},{8,9},{9,8},{10,11... | collective-permute-start | bytes 3145736 | tf_op jit(solution)/shard_map/ppermute | solution.py:331
  20.0 8.7 %collective-permute-start.4 = (bf16[2,4,32,1024]{3,2,1,0:T(8,128)(2,1)S(1)}, bf16[2,4,32,1024]{3,2,1,0:T(8,128)(2,1)S(1)}, u32[]{:S(2)}, u32[]{:S(2)}) collective-permute-start(bf16[2,4,32,1024]{3,2,1,0:T(8,128)(2,1)S(1)} %constant_dynamic-update-slice_fusion), channel_id=1, source_target_pairs={{0,4},{4,8},{8,12},{12,16},{16,20},{20,24},{24,28},{28,0},{5,1},{9... | collective-permute-start | bytes 1572872 | tf_op jit(solution)/shard_map/ppermute | solution.py:315
  22.5 11.7 %collective-permute-start.9 = (bf16[2,4,32,1024]{3,2,1,0:T(8,128)(2,1)S(1)}, bf16[2,4,32,1024]{3,2,1,0:T(8,128)(2,1)S(1)}, u32[]{:S(2)}, u32[]{:S(2)}) collective-permute-start(bf16[2,4,32,1024]{3,2,1,0:T(8,128)(2,1)S(1)} %collective-permute-done.1.refs_2_), channel_id=1, source_target_pairs={{0,4},{4,8},{8,12},{12,16},{16,20},{20,24},{24,28},{28,0},{5,1},{9... | collective-permute-start | bytes 1572872 | tf_op jit(solution)/shard_map/ppermute | solution.py:315
  28.6 11.2 %collective-permute-start.7 = (bf16[2,4,32,1024]{3,2,1,0:T(8,128)(2,1)S(1)}, bf16[2,4,32,1024]{3,2,1,0:T(8,128)(2,1)S(1)}, u32[]{:S(2)}, u32[]{:S(2)}) collective-permute-start(bf16[2,4,32,1024]{3,2,1,0:T(8,128)(2,1)S(1)} %collective-permute-done.4.refs_0_), channel_id=1, source_target_pairs={{0,4},{4,8},{8,12},{12,16},{16,20},{20,24},{24,28},{28,0},{5,1},{9... | collective-permute-start | bytes 1572872 | tf_op jit(solution)/shard_map/ppermute | solution.py:315
  34.3 11.2 %collective-permute-start.11 = (bf16[2,4,32,1024]{3,2,1,0:T(8,128)(2,1)S(1)}, bf16[2,4,32,1024]{3,2,1,0:T(8,128)(2,1)S(1)}, u32[]{:S(2)}, u32[]{:S(2)}) collective-permute-start(bf16[2,4,32,1024]{3,2,1,0:T(8,128)(2,1)S(1)} %collective-permute-done.9.refs_1_), channel_id=1, source_target_pairs={{0,4},{4,8},{8,12},{12,16},{16,20},{20,24},{24,28},{28,0},{5,1},{9... | collective-permute-start | bytes 1572872 | tf_op jit(solution)/shard_map/ppermute | solution.py:315
  39.9 11.4 %collective-permute-start.8 = (bf16[2,4,32,1024]{3,2,1,0:T(8,128)(2,1)S(1)}, bf16[2,4,32,1024]{3,2,1,0:T(8,128)(2,1)S(1)}, u32[]{:S(2)}, u32[]{:S(2)}) collective-permute-start(bf16[2,4,32,1024]{3,2,1,0:T(8,128)(2,1)S(1)} %collective-permute-done.7.refs_0_), channel_id=1, source_target_pairs={{0,4},{4,8},{8,12},{12,16},{16,20},{20,24},{24,28},{28,0},{5,1},{9... | collective-permute-start | bytes 1572872 | tf_op jit(solution)/shard_map/ppermute | solution.py:315
  45.5 11.2 %collective-permute-start.12 = (bf16[1,4,32,1024]{3,2,1,0:T(8,128)(2,1)S(1)}, bf16[1,4,32,1024]{3,2,1,0:T(8,128)(2,1)S(1)}, u32[]{:S(2)}, u32[]{:S(2)}) collective-permute-start(bf16[1,4,32,1024]{3,2,1,0:T(8,128)(2,1)S(1)} %slice.8), channel_id=1, source_target_pairs={{0,4},{4,8},{8,12},{12,16},{16,20},{20,24},{24,28},{28,0},{5,1},{9... | collective-permute-start | bytes 786440 | tf_op jit(solution)/shard_map/ppermute | solution.py:315
  51.3 7.3 %collective-permute-start.10 = (bf16[1,4,32,1024]{3,2,1,0:T(8,128)(2,1)S(1)}, bf16[1,4,32,1024]{3,2,1,0:T(8,128)(2,1)S(1)}, u32[]{:S(2)}, u32[]{:S(2)}) collective-permute-start(bf16[1,4,32,1024]{3,2,1,0:T(8,128)(2,1)S(1)} %slice.6), channel_id=1, source_target_pairs={{0,4},{4,8},{8,12},{12,16},{16,20},{20,24},{24,28},{28,0},{5,1},{9... | collective-permute-start | bytes 786440 | tf_op jit(solution)/shard_map/ppermute | solution.py:315
  74.5 4.2 %collective-permute-start.13 = (f32[32,8,128]{2,1,0:T(8,128)S(1)}, f32[32,8,128]{2,1,0:T(8,128)S(1)}, u32[]{:S(2)}, u32[]{:S(2)}) collective-permute-start(f32[32,8,128]{2,1,0:T(8,128)S(1)} %get-tuple-element.61), channel_id=1, source_target_pairs={{0,1},{1,0},{2,3},{3,2},{4,5},{5,4},{6,7},{7,6},{8,9},{9,8},{10,11... | collective-permute-start | bytes 393224 | tf_op jit(solution)/shard_map/ppermute | solution.py:360
  75.6 5.9 %collective-permute-start.14 = (f32[32,8,128]{2,1,0:T(8,128)S(1)}, f32[32,8,128]{2,1,0:T(8,128)S(1)}, u32[]{:S(2)}, u32[]{:S(2)}) collective-permute-start(f32[32,8,128]{2,1,0:T(8,128)S(1)} %get-tuple-element.62), channel_id=1, source_target_pairs={{0,31},{1,2},{2,1},{3,4},{4,3},{5,6},{6,5},{7,8},{8,7},{9,10},{10,... | collective-permute-start | bytes 393224 | tf_op jit(solution)/shard_map/ppermute | solution.py:359

commit v4 on v3

--- a/solution.py
+++ b/solution.py
@@ -138,13 +138,9 @@
     out, stacked = refs[n + 4 + n_more :]
     core = lax.axis_index("core")
     block = MODES_HERE * ROWS
-    spots = []
-    row = 0
-    for x, (column, steps) in zip(xs, pieces):
-        rows = x.shape[0] * block
-        stacked[row : row + rows, :] = x[...].reshape(rows, x.shape[-1])
-        row += rows
-        spots += [BLOCKS.index((column, e, steps)) for e in range(x.shape[0])]
+    for n, x in enumerate(xs):
+        stacked[n * block : (n + 1) * block, :] = x[...].reshape(block, x.shape[-1])
+    spots = [BLOCKS.index(piece) for piece in pieces]
     cells = rights[0].shape[1]
     for source in range(2):
         right, left = rights[source], lefts[source]
@@ -180,7 +176,7 @@
 
 def collide_part(xs, pieces, sides, more=(), last=False):
     _, cells, width = sides[0].shape
-    rows = sum(x.shape[0] for x in xs) * MODES_HERE * ROWS
+    rows = len(xs) * MODES_HERE * ROWS
     lead = (Y * XL, CORE) if last else (CORE,)
     return pl.pallas_call(
         functools.partial(collide_kernel, pieces, len(more), last),
@@ -313,42 +309,55 @@
 
     ring = [(CORE * i, CORE * ((i + 1) % Z)) for i in range(Z)] + [(CORE * ((i + 1) % Z) + 1, CORE * i + 1) for i in range(Z)]
     step = lambda a: lax.ppermute(a, ("z", "core"), ring)
-    both = lambda a: jnp.concatenate([a, lax.ppermute(a, "core", SWAP)])
-
-    tensor = tensor[None]
-    other = lax.ppermute(tensor, "xh", SWAP)
-    own0 = both(tensor)
-    pairs_now = together(pairs, own0)[0]
+    swap = lambda a: lax.ppermute(a, "core", SWAP)
+
+    got = {}
+
+    def part(keys, more=(), last=False):
+        return collide_part([got[key] for key in keys], keys, sides, more, last)
+
+    def send(column, swapped, steps):
+        got[column, swapped, steps] = step(got[column, swapped, steps - 1])
+
+    got[0, 0, 0] = tensor
+    got[1, 0, 0] = lax.ppermute(tensor, "xh", SWAP)
+    got[0, 1, 0] = swap(tensor)
+    send(0, 0, 1)
+    send(0, 1, 1)
+    pairs_now = together(pairs, got[0, 1, 0])[0]
     right_own = make_right(pairs_now, coeffs)
     left_own, left_send = make_left(pairs_now, coeffs)
-    own1 = step(own0)
-    own1, other, right_own, left_own, left_send = together(own1, other, right_own, left_own, left_send)
-    alt0 = both(other)
-    alt1 = step(alt0)
-    own2 = step(own1)
-    right_send, left_send = together(right_own, left_send, alt0)[:2]
-    right_sib = lax.ppermute(right_send, "core", SWAP)
-    left_sib = lax.ppermute(left_send, "core", SWAP)
-    sides = (right_own, right_sib, left_own, left_sib)
-    pairs_now, lateral = together(pairs, lateral, alt0)[:2]
+    got[0, 0, 1], got[0, 1, 1], got[1, 0, 0], right_own, left_own, left_send = together(
+        got[0, 0, 1], got[0, 1, 1], got[1, 0, 0], right_own, left_own, left_send
+    )
+    got[1, 1, 0] = swap(got[1, 0, 0])
+    send(0, 0, 2)
+    send(1, 0, 1)
+    send(0, 1, 2)
+    send(1, 1, 1)
+    right_send, left_send, pairs_now, lateral = together(right_own, left_send, pairs, lateral, got[1, 1, 0])[:4]
+    right_sib, left_sib = swap(right_send), swap(left_send)
     window, gain, heat = make_window(pairs_now, thermal, coeffs, modes)
     onehot = (lax.broadcasted_iota(jnp.int32, (cells, cells), 0) == lateral[None, :]).astype(jnp.bfloat16)
-    alt1, right_sib, left_sib, window, gain, heat, onehot = together(
-        alt1, right_sib, left_sib, window, gain, heat, onehot
+    got[1, 1, 1], right_sib, left_sib, window, gain, heat, onehot = together(
+        got[1, 1, 1], right_sib, left_sib, window, gain, heat, onehot
     )
     sides = (right_own, right_sib, left_own, left_sib)
-    alt2 = step(alt1)
-    own3 = step(own2)
-    parts = collide_part([tensor, other, own1], [(0, 0), (1, 0), (0, 1)], sides)
-    alt2, parts = together(alt2, parts)
-    alt3 = step(alt2)
-    own4 = step(own3[:1])
-    parts = collide_part([alt1, own2], [(1, 1), (0, 2)], sides, (parts,))
-    alt3, parts = together(alt3, parts)
-    alt4 = step(alt3[:1])
-    parts = collide_part([alt2, own3], [(1, 2), (0, 3)], sides, (parts,))
-    parts = collide_part([alt3, own4], [(1, 3), (0, 4)], sides, (parts,))
-    parts = collide_part([alt4], [(1, 4)], sides, (parts,), True)
+    send(0, 0, 3)
+    send(1, 0, 2)
+    send(0, 1, 3)
+    send(1, 1, 2)
+    parts = part([(0, 0, 0), (1, 0, 0), (0, 0, 1), (0, 1, 1)])
+    got[1, 1, 2], parts = together(got[1, 1, 2], parts)
+    send(1, 0, 3)
+    send(1, 1, 3)
+    send(0, 0, 4)
+    parts = part([(1, 0, 1), (1, 1, 1), (0, 0, 2), (0, 1, 2)], (parts,))
+    got[1, 0, 3], parts = together(got[1, 0, 3], parts)
+    send(1, 0, 4)
+    parts = part([(1, 0, 2), (1, 1, 2), (0, 0, 3), (0, 1, 3)], (parts,))
+    parts = part([(1, 0, 3), (1, 1, 3), (0, 0, 4)], (parts,))
+    parts = part([(1, 0, 4)], (parts,), True)
 
     parts = parts.reshape(Y * XL * CORE, 2 * MODES_HERE, cells)
     parts = lax.all_to_all(parts, ("y", "xl", "core"), split_axis=0, concat_axis=0, tiled=True)

time: 82.6 us -> 77.9 us (0.943)
  waiting for transfers between devices: 13.6 us -> 8.72 us
  starting transfers between devices: 33.1 us -> 35.1 us
  other arithmetic: 1.13 us -> 0.14 us
    ppermute x8 -> x14, waiting for transfers between devices: 8.05 us -> 4.14 us  [local(): step = lambda a: lax.ppermute(a, ('z', 'core'), ring)]
    ppermute x8 -> x14, starting transfers between devices: 22.9 us -> 25.3 us  [local(): step = lambda a: lax.ppermute(a, ('z', 'core'), ring)]
    ppermute x5, waiting for transfers between devices: 2.88 us -> 1.53 us  [the longest x4 1.53 us: local(): swap = lambda a: lax.ppermute(a, 'core', SWAP)]
    concatenate x1 -> x0, other arithmetic: 1 us -> none  [local(): both = lambda a: jnp.concatenate([a, lax.ppermute(a, 'core', SWAP)])]
  transfers between devices with their start and end apart: 15 -> 21, of which waited for: 7 -> 9; matrix products, arithmetic and copies ran while one was open for 0% -> 0% of each run, Pallas kernels for 20% -> 22%
where the time goes in v4:
time: 77.9 us; the launch traced here: 77.7 us
  starting transfers between devices  35.1 us (45%)
  Pallas kernels  19.2 us (25%)
  blocking collectives  13.7 us (18%)
  waiting for transfers between devices  8.72 us (11%)
    ppermute x14, starting transfers between devices, local(): step = lambda a: lax.ppermute(a, ('z', 'core'), ring)  25.3 us
    all_to_all x1, blocking collectives, local(): lax.all_to_all(parts, ('y', 'xl', 'core'), split_axis=0, concat_axis=0, t...  13.7 us
    pallas_call x5, Pallas kernels, collide_part(): pl.pallas_call(functools.partial(collide_kernel, pieces, len(more), last)...  10.5 us
    ppermute x14, waiting for transfers between devices, local(): step = lambda a: lax.ppermute(a, ('z', 'core'), ring)  4.14 us
    ppermute x4, starting transfers between devices, local(): swap = lambda a: lax.ppermute(a, 'core', SWAP)  3.84 us
    ppermute x1, waiting for transfers between devices, local(): outward = lax.ppermute(outward, BRICK, facing)  3.04 us
    ppermute x1, starting transfers between devices, local(): got[1, 0, 0] = lax.ppermute(tensor, 'xh', SWAP)  2.74 us
    pallas_call x1, Pallas kernels, make_left(): pl.pallas_call(left_kernel, in_specs=[SMEM, pl.BlockSpec(memory_space=plt...  2.58 us
  transfers between devices with their start and end apart: 21, of which 9 were waited for; matrix products, arithmetic and copies ran while one was open for 0% of the time, Pallas kernels for 22%

profile of v4, /device:TPU:1, one launch (start us, length us, event | category | flops | bytes accessed | tf_op | source)
XLA Modules:
  0.0 77.7 jit_solution(9199187325378219332)
XLA Ops:
  0.0 3.2 %collective-permute-start.1 = (bf16[4,32,1024]{2,1,0:T(8,128)(2,1)}, bf16[4,32,1024]{2,1,0:T(8,128)(2,1)S(1)}, u32[]{:S(2)}, u32[]{:S(2)}) collective-permute-start(bf16[4,32,1024]{2,1,0:T(8,128)(2,1)} %refs_0_.1), channel_id=1, source_target_pairs={{0,1},{1,0},{2,3},{3,2},{4,5},{5,4},{6,7},{7,6},{8,9},{9,8},{10,11... | collective-permute-start | bytes 786440 | tf_op jit(solution)/shard_map/ppermute | solution.py:312
  3.2 3.8 %collective-permute-start = (bf16[4,32,1024]{2,1,0:T(8,128)(2,1)}, bf16[4,32,1024]{2,1,0:T(8,128)(2,1)S(1)}, u32[]{:S(2)}, u32[]{:S(2)}) collective-permute-start(bf16[4,32,1024]{2,1,0:T(8,128)(2,1)} %refs_0_.1), channel_id=1, source_target_pairs={{0,4},{4,8},{8,12},{12,16},{16,20},{20,24},{24,28},{28,0},{5,1},{9... | collective-permute-start | bytes 786440 | tf_op jit(solution)/shard_map/ppermute | solution.py:311
  7.1 2.7 %collective-permute-start.3 = (bf16[4,32,1024]{2,1,0:T(8,128)(2,1)}, bf16[4,32,1024]{2,1,0:T(8,128)(2,1)S(1)}, u32[]{:S(2)}, u32[]{:S(2)}) collective-permute-start(bf16[4,32,1024]{2,1,0:T(8,128)(2,1)} %refs_0_.1), channel_id=1, source_target_pairs={{0,2},{2,0},{1,3},{3,1},{4,6},{6,4},{5,7},{7,5},{8,10},{10,8},{9,1... | collective-permute-start | bytes 786440 | tf_op jit(solution)/shard_map/ppermute | solution.py:323
  9.8 0.7 collective-permute-start.2
  11.2 2.6 %left.1 = (bf16[2,16,32,512]{3,2,1,0:T(8,128)(2,1)S(1)}, bf16[2,16,32,512]{3,2,1,0:T(8,128)(2,1)S(1)}) custom-call(s32[2,2]{1,0:T(2,128)S(1)} %copy-done, bf16[8,512,1024]{2,1,0:T(8,128)(2,1)} %coeffs.5), custom_call_target="tpu_custom_call" | custom-call | bytes 10485760 | tf_op jit(solution)/shard_map/left/pallas_call | solution.py:77
  13.8 2.1 %right.1.refs_4_.refs_3_.refs_1_ = bf16[2,512,1024]{2,1,0:T(8,128)(2,1)S(1)} custom-call(s32[2,2]{1,0:T(2,128)S(1)} %copy-done, bf16[8,512,1024]{2,1,0:T(8,128)(2,1)} %coeffs.5), custom_call_target="tpu_custom_call" | custom-call | bytes 4194304 | tf_op jit(solution)/shard_map/right/pallas_call | solution.py:62
  16.1 1.5 %collective-permute-done.7 = bf16[4,32,1024]{2,1,0:T(8,128)(2,1)S(1)} collective-permute-done((bf16[4,32,1024]{2,1,0:T(8,128)(2,1)S(1)}, bf16[4,32,1024]{2,1,0:T(8,128)(2,1)S(1)}, u32[]{:S(2)}, u32[]{:S(2)}) %collective-permute-start.7) | collective-permute-done | bytes 262176 | tf_op jit(solution)/shard_map/ppermute | solution.py:312
  18.2 1.5 %collective-permute-start.4 = (bf16[4,32,1024]{2,1,0:T(8,128)(2,1)S(1)}, bf16[4,32,1024]{2,1,0:T(8,128)(2,1)S(1)}, u32[]{:S(2)}, u32[]{:S(2)}) collective-permute-start(bf16[4,32,1024]{2,1,0:T(8,128)(2,1)S(1)} %collective-permute-done.3.refs_1_), channel_id=1, source_target_pairs={{0,4},{4,8},{8,12},{12,16},{16,20},{20,24},{24,28},{28,0},{5,1},{9... | collective-permute-start | bytes 786440 | tf_op jit(solution)/shard_map/ppermute | solution.py:311
  19.7 1.1 %collective-permute-start.11 = (bf16[4,32,1024]{2,1,0:T(8,128)(2,1)S(1)}, bf16[4,32,1024]{2,1,0:T(8,128)(2,1)S(1)}, u32[]{:S(2)}, u32[]{:S(2)}) collective-permute-start(bf16[4,32,1024]{2,1,0:T(8,128)(2,1)S(1)} %collective-permute-done.refs_2_), channel_id=1, source_target_pairs={{0,4},{4,8},{8,12},{12,16},{16,20},{20,24},{24,28},{28,0},{5,1},{9... | collective-permute-start | bytes 786440 | tf_op jit(solution)/shard_map/ppermute | solution.py:311
  20.7 0.7 collective-permute-start.8
  21.5 2.3 %window.1 = (f32[32,8,512]{2,1,0:T(8,128)S(1)}, f32[2,8,128]{2,1,0:T(8,128)S(1)}, f32[8,128]{1,0:T(8,128)S(1)}) custom-call(s32[2,2]{1,0:T(2,128)S(1)} %copy-done, f32[8]{0:T(128)S(1)} %copy-done.1, bf16[8,512,1024]{2,1,0:T(8,128)(2,1)} %coeffs.5), custom_call_target="tpu_custom_call" | custom-call | bytes 8388608 | tf_op jit(solution)/shard_map/window/pallas_call | solution.py:114
  23.8 2.3 %collective-permute-start.12 = (bf16[4,32,1024]{2,1,0:T(8,128)(2,1)S(1)}, bf16[4,32,1024]{2,1,0:T(8,128)(2,1)S(1)}, u32[]{:S(2)}, u32[]{:S(2)}) collective-permute-start(bf16[4,32,1024]{2,1,0:T(8,128)(2,1)S(1)} %collective-permute-done.2.refs_3_), channel_id=1, source_target_pairs={{0,4},{4,8},{8,12},{12,16},{16,20},{20,24},{24,28},{28,0},{5,1},{9... | collective-permute-start | bytes 786440 | tf_op jit(solution)/shard_map/ppermute | solution.py:311
  26.5 2.4 %collective-permute-start.5 = (bf16[4,32,1024]{2,1,0:T(8,128)(2,1)S(1)}, bf16[4,32,1024]{2,1,0:T(8,128)(2,1)S(1)}, u32[]{:S(2)}, u32[]{:S(2)}) collective-permute-start(bf16[4,32,1024]{2,1,0:T(8,128)(2,1)S(1)} %collective-permute-done.4.refs_0_), channel_id=1, source_target_pairs={{0,4},{4,8},{8,12},{12,16},{16,20},{20,24},{24,28},{28,0},{5,1},{9... | collective-permute-start | bytes 786440 | tf_op jit(solution)/shard_map/ppermute | solution.py:311
  29.3 2.4 %collective-permute-start.16 = (bf16[4,32,1024]{2,1,0:T(8,128)(2,1)S(1)}, bf16[4,32,1024]{2,1,0:T(8,128)(2,1)S(1)}, u32[]{:S(2)}, u32[]{:S(2)}) collective-permute-start(bf16[4,32,1024]{2,1,0:T(8,128)(2,1)S(1)} %collective-permute-done.11.refs_2_), channel_id=1, source_target_pairs={{0,4},{4,8},{8,12},{12,16},{16,20},{20,24},{24,28},{28,0},{5,1},{9... | collective-permute-start | bytes 786440 | tf_op jit(solution)/shard_map/ppermute | solution.py:311
  32.1 2.4 %collective-permute-start.18 = (bf16[4,32,1024]{2,1,0:T(8,128)(2,1)S(1)}, bf16[4,32,1024]{2,1,0:T(8,128)(2,1)S(1)}, u32[]{:S(2)}, u32[]{:S(2)}) collective-permute-start(bf16[4,32,1024]{2,1,0:T(8,128)(2,1)S(1)} %collective-permute-done.12.refs_3_), channel_id=1, source_target_pairs={{0,4},{4,8},{8,12},{12,16},{16,20},{20,24},{24,28},{28,0},{5,1},{9... | collective-permute-start | bytes 786440 | tf_op jit(solution)/shard_map/ppermute | solution.py:311
  34.9 2.4 %collective-permute-start.6 = (bf16[4,32,1024]{2,1,0:T(8,128)(2,1)S(1)}, bf16[4,32,1024]{2,1,0:T(8,128)(2,1)S(1)}, u32[]{:S(2)}, u32[]{:S(2)}) collective-permute-start(bf16[4,32,1024]{2,1,0:T(8,128)(2,1)S(1)} %collective-permute-done.5.refs_0_), channel_id=1, source_target_pairs={{0,4},{4,8},{8,12},{12,16},{16,20},{20,24},{24,28},{28,0},{5,1},{9... | collective-permute-start | bytes 786440 | tf_op jit(solution)/shard_map/ppermute | solution.py:311
  37.7 2.4 %collective-permute-start.17 = (bf16[4,32,1024]{2,1,0:T(8,128)(2,1)S(1)}, bf16[4,32,1024]{2,1,0:T(8,128)(2,1)S(1)}, u32[]{:S(2)}, u32[]{:S(2)}) collective-permute-start(bf16[4,32,1024]{2,1,0:T(8,128)(2,1)S(1)} %collective-permute-done.16.refs_2_), channel_id=1, source_target_pairs={{0,4},{4,8},{8,12},{12,16},{16,20},{20,24},{24,28},{28,0},{5,1},{9... | collective-permute-start | bytes 786440 | tf_op jit(solution)/shard_map/ppermute | solution.py:311
  40.1 2.4 %collide.5.refs_8_ = f32[2,8,512]{2,1,0:T(8,128)S(1)} custom-call(bf16[4,32,1024]{2,1,0:T(8,128)(2,1)S(1)} %copy-done.2, bf16[4,32,1024]{2,1,0:T(8,128)(2,1)S(1)} %collective-permute-done.3.refs_1_, bf16[4,32,1024]{2,1,0:T(8,128)(2,1)S(1)} %collective-permute-done.refs_2_, bf16[4,32,1024]{2,1,0:T(8,128)(2,1)S(1)} %collective-permute-done.2.refs_3_, ...), custom_call_target="tpu_custom_call" | custom-call | flops 2147483648 | bytes 4194304 | tf_op jit(solution)/shard_map/collide/pallas_call | solution.py:181
  42.9 2.4 %collide.6.refs_8_ = f32[2,8,512]{2,1,0:T(8,128)S(1)} custom-call(bf16[4,32,1024]{2,1,0:T(8,128)(2,1)S(1)} %collective-permute-done.4.refs_0_, bf16[4,32,1024]{2,1,0:T(8,128)(2,1)S(1)} %collective-permute-done.8.refs_1_, bf16[4,32,1024]{2,1,0:T(8,128)(2,1)S(1)} %collective-permute-done.11.refs_2_, bf16[4,32,1024]{2,1,0:T(8,128)(2,1)S(1)} %collective-permute-done.12.refs_3_, ...), custom_call_target="tpu_custom_call" | custom-call | flops 2147483648 | bytes 4194304 | tf_op jit(solution)/shard_map/collide/pallas_call | solution.py:181
  45.3 0.8 %collective-permute-done.6.refs_0_ = bf16[4,32,1024]{2,1,0:T(8,128)(2,1)S(1)} collective-permute-done((bf16[4,32,1024]{2,1,0:T(8,128)(2,1)S(1)}, bf16[4,32,1024]{2,1,0:T(8,128)(2,1)S(1)}, u32[]{:S(2)}, u32[]{:S(2)}) %collective-permute-start.6) | collective-permute-done | bytes 262176 | tf_op jit(solution)/shard_map/ppermute | solution.py:311
  46.1 2.4 %collective-permute-start.14 = (bf16[4,32,1024]{2,1,0:T(8,128)(2,1)S(1)}, bf16[4,32,1024]{2,1,0:T(8,128)(2,1)S(1)}, u32[]{:S(2)}, u32[]{:S(2)}) collective-permute-start(bf16[4,32,1024]{2,1,0:T(8,128)(2,1)S(1)} %collective-permute-done.6.refs_0_), channel_id=1, source_target_pairs={{0,4},{4,8},{8,12},{12,16},{16,20},{20,24},{24,28},{28,0},{5,1},{9... | collective-permute-start | bytes 786440 | tf_op jit(solution)/shard_map/ppermute | solution.py:311
  48.6 2.4 %collide.7.refs_7_ = f32[2,8,512]{2,1,0:T(8,128)S(1)} custom-call(bf16[4,32,1024]{2,1,0:T(8,128)(2,1)S(1)} %collective-permute-done.5.refs_0_, bf16[4,32,1024]{2,1,0:T(8,128)(2,1)S(1)} %collective-permute-done.13.refs_1_, bf16[4,32,1024]{2,1,0:T(8,128)(2,1)S(1)} %collective-permute-done.16.refs_2_, bf16[4,32,1024]{2,1,0:T(8,128)(2,1)S(1)} %collective-permute-done.18.refs_3_, ...), custom_call_target="tpu_custom_call" | custom-call | flops 2147483648 | bytes 4194304 | tf_op jit(solution)/shard_map/collide/pallas_call | solution.py:181
  51.0 0.8 %collective-permute-done.15.refs_1_ = bf16[4,32,1024]{2,1,0:T(8,128)(2,1)S(1)} collective-permute-done((bf16[4,32,1024]{2,1,0:T(8,128)(2,1)S(1)}, bf16[4,32,1024]{2,1,0:T(8,128)(2,1)S(1)}, u32[]{:S(2)}, u32[]{:S(2)}) %collective-permute-start.15) | collective-permute-done | bytes 262176 | tf_op jit(solution)/shard_map/ppermute | solution.py:311
  51.8 1.9 %collide.8.refs_5_ = f32[2,8,512]{2,1,0:T(8,128)S(1)} custom-call(bf16[4,32,1024]{2,1,0:T(8,128)(2,1)S(1)} %collective-permute-done.6.refs_0_, bf16[4,32,1024]{2,1,0:T(8,128)(2,1)S(1)} %collective-permute-done.15.refs_1_, bf16[4,32,1024]{2,1,0:T(8,128)(2,1)S(1)} %collective-permute-done.17.refs_2_, bf16[2,512,1024]{2,1,0:T(8,128)(2,1)S(1)} %right.1.refs_4_.refs_3_.refs_1_, ...), custom_call_target="tpu_custom_call" | custom-call | flops 1610612736 | bytes 4194304 | tf_op jit(solution)/shard_map/collide/pallas_call | solution.py:181
  53.6 0.9 %collective-permute-done.14.refs_0_ = bf16[4,32,1024]{2,1,0:T(8,128)(2,1)S(1)} collective-permute-done((bf16[4,32,1024]{2,1,0:T(8,128)(2,1)S(1)}, bf16[4,32,1024]{2,1,0:T(8,128)(2,1)S(1)}, u32[]{:S(2)}, u32[]{:S(2)}) %collective-permute-start.14) | collective-permute-done | bytes 262176 | tf_op jit(solution)/shard_map/ppermute | solution.py:311
  54.6 1.5 %collide.9 = f32[8,2,8,512]{3,2,1,0:T(8,128)S(1)} custom-call(bf16[4,32,1024]{2,1,0:T(8,128)(2,1)S(1)} %collective-permute-done.14.refs_0_, bf16[2,512,1024]{2,1,0:T(8,128)(2,1)S(1)} %right.1.refs_4_.refs_3_.refs_1_, bf16[2,512,1024]{2,1,0:T(8,128)(2,1)S(1)} %collective-permute-done.9.refs_5_.refs_4_.refs_2_, ...), custom_call_target="tpu_custom_call" | custom-call | flops 536870912 | bytes 4194304 | tf_op jit(solution)/shard_map/collide/pallas_call | solution.py:181
  56.1 13.7 %all_to_all.5 = f32[16,8,512]{2,1,0:T(8,128)S(1)} all-to-all(f32[16,8,512]{2,1,0:T(8,128)S(1)} %bitcast.3), channel_id=1, replica_groups=mesh['y'=4,'xl'=2,'z'=8,'xh'=2,'core'=2] {'y','xl','core'}, dimensions={0} | all-to-all | bytes 524288 | tf_op jit(solution)/shard_map/all_to_all | solution.py:363
  69.9 1.1 %collective-permute-start.19 = (f32[32,8,128]{2,1,0:T(8,128)S(1)}, f32[32,8,128]{2,1,0:T(8,128)S(1)}, u32[]{:S(2)}, u32[]{:S(2)}) collective-permute-start(f32[32,8,128]{2,1,0:T(8,128)S(1)} %get-tuple-element.63), channel_id=1, source_target_pairs={{0,1},{1,0},{2,3},{3,2},{4,5},{5,4},{6,7},{7,6},{8,9},{9,8},{10,11... | collective-permute-start | bytes 393224 | tf_op jit(solution)/shard_map/ppermute | solution.py:369
  71.0 2.1 %collective-permute-start.20 = (f32[32,8,128]{2,1,0:T(8,128)S(1)}, f32[32,8,128]{2,1,0:T(8,128)S(1)}, u32[]{:S(2)}, u32[]{:S(2)}) collective-permute-start(f32[32,8,128]{2,1,0:T(8,128)S(1)} %get-tuple-element.64), channel_id=1, source_target_pairs={{0,31},{1,2},{2,1},{3,4},{4,3},{5,6},{6,5},{7,8},{8,7},{9,10},{10,... | collective-permute-start | bytes 393224 | tf_op jit(solution)/shard_map/ppermute | solution.py:368
  73.1 0.7 inner.1
  73.8 3.0 %collective-permute-done.20.outward = f32[32,8,128]{2,1,0:T(8,128)S(1)} collective-permute-done((f32[32,8,128]{2,1,0:T(8,128)S(1)}, f32[32,8,128]{2,1,0:T(8,128)S(1)}, u32[]{:S(2)}, u32[]{:S(2)}) %collective-permute-start.20) | collective-permute-done | bytes 131104 | tf_op jit(solution)/shard_map/ppermute | solution.py:368
  76.9 0.9 %outer.1 = f32[32,8,512]{2,1,0:T(8,128)} custom-call(f32[32,8,512]{2,1,0:T(8,128)S(1)} %inner.1, f32[8,128]{1,0:T(8,128)S(1)} %get-tuple-element.61.heat, f32[32,8,128]{2,1,0:T(8,128)S(1)} %collective-permute-done.19.inward, f32[32,8,128]{2,1,0:T(8,128)S(1)} %collective-permute-done.20.outward), custom_call_target="tpu_custom_call" | custom-call | tf_op jit(solution)/shard_map/outer/pallas_call | solution.py:291
  (31 shorter events, 3.8 us)
Async XLA Ops:
  0.0 9.8 %collective-permute-start.1 = (bf16[4,32,1024]{2,1,0:T(8,128)(2,1)}, bf16[4,32,1024]{2,1,0:T(8,128)(2,1)S(1)}, u32[]{:S(2)}, u32[]{:S(2)}) collective-permute-start(bf16[4,32,1024]{2,1,0:T(8,128)(2,1)} %refs_0_.1), channel_id=1, source_target_pairs={{0,1},{1,0},{2,3},{3,2},{4,5},{5,4},{6,7},{7,6},{8,9},{9,8},{10,11... | collective-permute-start | bytes 786440 | tf_op jit(solution)/shard_map/ppermute | solution.py:312
  3.2 12.7 %collective-permute-start = (bf16[4,32,1024]{2,1,0:T(8,128)(2,1)}, bf16[4,32,1024]{2,1,0:T(8,128)(2,1)S(1)}, u32[]{:S(2)}, u32[]{:S(2)}) collective-permute-start(bf16[4,32,1024]{2,1,0:T(8,128)(2,1)} %refs_0_.1), channel_id=1, source_target_pairs={{0,4},{4,8},{8,12},{12,16},{16,20},{20,24},{24,28},{28,0},{5,1},{9... | collective-permute-start | bytes 786440 | tf_op jit(solution)/shard_map/ppermute | solution.py:311
  7.1 8.9 %collective-permute-start.3 = (bf16[4,32,1024]{2,1,0:T(8,128)(2,1)}, bf16[4,32,1024]{2,1,0:T(8,128)(2,1)S(1)}, u32[]{:S(2)}, u32[]{:S(2)}) collective-permute-start(bf16[4,32,1024]{2,1,0:T(8,128)(2,1)} %refs_0_.1), channel_id=1, source_target_pairs={{0,2},{2,0},{1,3},{3,1},{4,6},{6,4},{5,7},{7,5},{8,10},{10,8},{9,1... | collective-permute-start | bytes 786440 | tf_op jit(solution)/shard_map/ppermute | solution.py:323
  9.8 6.2 %collective-permute-start.2 = (bf16[4,32,1024]{2,1,0:T(8,128)(2,1)S(1)}, bf16[4,32,1024]{2,1,0:T(8,128)(2,1)S(1)}, u32[]{:S(2)}, u32[]{:S(2)}) collective-permute-start(bf16[4,32,1024]{2,1,0:T(8,128)(2,1)S(1)} %collective-permute-done.1), channel_id=1, source_target_pairs={{0,4},{4,8},{8,12},{12,16},{16,20},{20,24},{24,28},{28,0},{5,1},{9... | collective-permute-start | bytes 786440 | tf_op jit(solution)/shard_map/ppermute | solution.py:311
  10.6 0.7 copy-start
  13.8 7.6 %copy-start.1 = (f32[8]{0:T(128)S(1)}, f32[8]{0:T(128)}, u32[]{:S(2)}) copy-start(f32[8]{0:T(128)} %thermal.1) | copy-start | bytes 100
  16.0 15.7 %copy-start.3 = (s32[512]{0:T(512)S(1)}, s32[512]{0:T(512)}, u32[]{:S(2)}) copy-start(s32[512]{0:T(512)} %param.8) | copy-start | bytes 6148
  16.0 24.1 %copy-start.2 = (bf16[4,32,1024]{2,1,0:T(8,128)(2,1)S(1)}, bf16[4,32,1024]{2,1,0:T(8,128)(2,1)}, u32[]{:S(2)}) copy-start(bf16[4,32,1024]{2,1,0:T(8,128)(2,1)} %refs_0_.1) | copy-start | bytes 786436
  16.0 1.6 %collective-permute-start.7 = (bf16[4,32,1024]{2,1,0:T(8,128)(2,1)S(1)}, bf16[4,32,1024]{2,1,0:T(8,128)(2,1)S(1)}, u32[]{:S(2)}, u32[]{:S(2)}) collective-permute-start(bf16[4,32,1024]{2,1,0:T(8,128)(2,1)S(1)} %collective-permute-done.3.refs_1_), channel_id=1, source_target_pairs={{0,1},{1,0},{2,3},{3,2},{4,5},{5,4},{6,7},{7,6},{8,9},{9,8},{10,11... | collective-permute-start | bytes 786440 | tf_op jit(solution)/shard_map/ppermute | solution.py:312
  17.6 14.2 %collective-permute-start.9 = (bf16[2,512,1024]{2,1,0:T(8,128)(2,1)S(1)}, bf16[2,512,1024]{2,1,0:T(8,128)(2,1)S(1)}, u32[]{:S(2)}, u32[]{:S(2)}) collective-permute-start(bf16[2,512,1024]{2,1,0:T(8,128)(2,1)S(1)} %right.1.refs_4_.refs_3_.refs_1_), channel_id=1, source_target_pairs={{0,1},{1,0},{2,3},{3,2},{4,5},{5,4},{6,7},{7,6},{8,9},{9,8},{10,11... | collective-permute-start | bytes 6291464 | tf_op jit(solution)/shard_map/ppermute | solution.py:312
  17.8 14.1 %collective-permute-start.10 = (bf16[2,16,32,512]{3,2,1,0:T(8,128)(2,1)S(1)}, bf16[2,16,32,512]{3,2,1,0:T(8,128)(2,1)S(1)}, u32[]{:S(2)}, u32[]{:S(2)}) collective-permute-start(bf16[2,16,32,512]{3,2,1,0:T(8,128)(2,1)S(1)} %get-tuple-element.42), channel_id=1, source_target_pairs={{0,1},{1,0},{2,3},{3,2},{4,5},{5,4},{6,7},{7,6},{8,9},{9,8},{10,11... | collective-permute-start | bytes 3145736 | tf_op jit(solution)/shard_map/ppermute | solution.py:312
  18.2 5.6 %collective-permute-start.4 = (bf16[4,32,1024]{2,1,0:T(8,128)(2,1)S(1)}, bf16[4,32,1024]{2,1,0:T(8,128)(2,1)S(1)}, u32[]{:S(2)}, u32[]{:S(2)}) collective-permute-start(bf16[4,32,1024]{2,1,0:T(8,128)(2,1)S(1)} %collective-permute-done.3.refs_1_), channel_id=1, source_target_pairs={{0,4},{4,8},{8,12},{12,16},{16,20},{20,24},{24,28},{28,0},{5,1},{9... | collective-permute-start | bytes 786440 | tf_op jit(solution)/shard_map/ppermute | solution.py:311
  19.7 6.8 %collective-permute-start.11 = (bf16[4,32,1024]{2,1,0:T(8,128)(2,1)S(1)}, bf16[4,32,1024]{2,1,0:T(8,128)(2,1)S(1)}, u32[]{:S(2)}, u32[]{:S(2)}) collective-permute-start(bf16[4,32,1024]{2,1,0:T(8,128)(2,1)S(1)} %collective-permute-done.refs_2_), channel_id=1, source_target_pairs={{0,4},{4,8},{8,12},{12,16},{16,20},{20,24},{24,28},{28,0},{5,1},{9... | collective-permute-start | bytes 786440 | tf_op jit(solution)/shard_map/ppermute | solution.py:311
  20.7 8.6 %collective-permute-start.8 = (bf16[4,32,1024]{2,1,0:T(8,128)(2,1)S(1)}, bf16[4,32,1024]{2,1,0:T(8,128)(2,1)S(1)}, u32[]{:S(2)}, u32[]{:S(2)}) collective-permute-start(bf16[4,32,1024]{2,1,0:T(8,128)(2,1)S(1)} %collective-permute-done.7), channel_id=1, source_target_pairs={{0,4},{4,8},{8,12},{12,16},{16,20},{20,24},{24,28},{28,0},{5,1},{9... | collective-permute-start | bytes 786440 | tf_op jit(solution)/shard_map/ppermute | solution.py:311
  23.8 8.3 %collective-permute-start.12 = (bf16[4,32,1024]{2,1,0:T(8,128)(2,1)S(1)}, bf16[4,32,1024]{2,1,0:T(8,128)(2,1)S(1)}, u32[]{:S(2)}, u32[]{:S(2)}) collective-permute-start(bf16[4,32,1024]{2,1,0:T(8,128)(2,1)S(1)} %collective-permute-done.2.refs_3_), channel_id=1, source_target_pairs={{0,4},{4,8},{8,12},{12,16},{16,20},{20,24},{24,28},{28,0},{5,1},{9... | collective-permute-start | bytes 786440 | tf_op jit(solution)/shard_map/ppermute | solution.py:311
  26.5 8.4 %collective-permute-start.5 = (bf16[4,32,1024]{2,1,0:T(8,128)(2,1)S(1)}, bf16[4,32,1024]{2,1,0:T(8,128)(2,1)S(1)}, u32[]{:S(2)}, u32[]{:S(2)}) collective-permute-start(bf16[4,32,1024]{2,1,0:T(8,128)(2,1)S(1)} %collective-permute-done.4.refs_0_), channel_id=1, source_target_pairs={{0,4},{4,8},{8,12},{12,16},{16,20},{20,24},{24,28},{28,0},{5,1},{9... | collective-permute-start | bytes 786440 | tf_op jit(solution)/shard_map/ppermute | solution.py:311
  29.3 8.4 %collective-permute-start.16 = (bf16[4,32,1024]{2,1,0:T(8,128)(2,1)S(1)}, bf16[4,32,1024]{2,1,0:T(8,128)(2,1)S(1)}, u32[]{:S(2)}, u32[]{:S(2)}) collective-permute-start(bf16[4,32,1024]{2,1,0:T(8,128)(2,1)S(1)} %collective-permute-done.11.refs_2_), channel_id=1, source_target_pairs={{0,4},{4,8},{8,12},{12,16},{16,20},{20,24},{24,28},{28,0},{5,1},{9... | collective-permute-start | bytes 786440 | tf_op jit(solution)/shard_map/ppermute | solution.py:311
  31.9 10.7 %collective-permute-start.13 = (bf16[4,32,1024]{2,1,0:T(8,128)(2,1)S(1)}, bf16[4,32,1024]{2,1,0:T(8,128)(2,1)S(1)}, u32[]{:S(2)}, u32[]{:S(2)}) collective-permute-start(bf16[4,32,1024]{2,1,0:T(8,128)(2,1)S(1)} %collective-permute-done.8.refs_1_), channel_id=1, source_target_pairs={{0,4},{4,8},{8,12},{12,16},{16,20},{20,24},{24,28},{28,0},{5,1},{9... | collective-permute-start | bytes 786440 | tf_op jit(solution)/shard_map/ppermute | solution.py:311
  32.1 16.5 %collective-permute-start.18 = (bf16[4,32,1024]{2,1,0:T(8,128)(2,1)S(1)}, bf16[4,32,1024]{2,1,0:T(8,128)(2,1)S(1)}, u32[]{:S(2)}, u32[]{:S(2)}) collective-permute-start(bf16[4,32,1024]{2,1,0:T(8,128)(2,1)S(1)} %collective-permute-done.12.refs_3_), channel_id=1, source_target_pairs={{0,4},{4,8},{8,12},{12,16},{16,20},{20,24},{24,28},{28,0},{5,1},{9... | collective-permute-start | bytes 786440 | tf_op jit(solution)/shard_map/ppermute | solution.py:311
  34.9 11.2 %collective-permute-start.6 = (bf16[4,32,1024]{2,1,0:T(8,128)(2,1)S(1)}, bf16[4,32,1024]{2,1,0:T(8,128)(2,1)S(1)}, u32[]{:S(2)}, u32[]{:S(2)}) collective-permute-start(bf16[4,32,1024]{2,1,0:T(8,128)(2,1)S(1)} %collective-permute-done.5.refs_0_), channel_id=1, source_target_pairs={{0,4},{4,8},{8,12},{12,16},{16,20},{20,24},{24,28},{28,0},{5,1},{9... | collective-permute-start | bytes 786440 | tf_op jit(solution)/shard_map/ppermute | solution.py:311
  37.7 13.2 %collective-permute-start.17 = (bf16[4,32,1024]{2,1,0:T(8,128)(2,1)S(1)}, bf16[4,32,1024]{2,1,0:T(8,128)(2,1)S(1)}, u32[]{:S(2)}, u32[]{:S(2)}) collective-permute-start(bf16[4,32,1024]{2,1,0:T(8,128)(2,1)S(1)} %collective-permute-done.16.refs_2_), channel_id=1, source_target_pairs={{0,4},{4,8},{8,12},{12,16},{16,20},{20,24},{24,28},{28,0},{5,1},{9... | collective-permute-start | bytes 786440 | tf_op jit(solution)/shard_map/ppermute | solution.py:311
  42.5 9.2 %collective-permute-start.15 = (bf16[4,32,1024]{2,1,0:T(8,128)(2,1)S(1)}, bf16[4,32,1024]{2,1,0:T(8,128)(2,1)S(1)}, u32[]{:S(2)}, u32[]{:S(2)}) collective-permute-start(bf16[4,32,1024]{2,1,0:T(8,128)(2,1)S(1)} %collective-permute-done.13.refs_1_), channel_id=1, source_target_pairs={{0,4},{4,8},{8,12},{12,16},{16,20},{20,24},{24,28},{28,0},{5,1},{9... | collective-permute-start | bytes 786440 | tf_op jit(solution)/shard_map/ppermute | solution.py:311
  46.1 8.4 %collective-permute-start.14 = (bf16[4,32,1024]{2,1,0:T(8,128)(2,1)S(1)}, bf16[4,32,1024]{2,1,0:T(8,128)(2,1)S(1)}, u32[]{:S(2)}, u32[]{:S(2)}) collective-permute-start(bf16[4,32,1024]{2,1,0:T(8,128)(2,1)S(1)} %collective-permute-done.6.refs_0_), channel_id=1, source_target_pairs={{0,4},{4,8},{8,12},{12,16},{16,20},{20,24},{24,28},{28,0},{5,1},{9... | collective-permute-start | bytes 786440 | tf_op jit(solution)/shard_map/ppermute | solution.py:311
  69.9 3.9 %collective-permute-start.19 = (f32[32,8,128]{2,1,0:T(8,128)S(1)}, f32[32,8,128]{2,1,0:T(8,128)S(1)}, u32[]{:S(2)}, u32[]{:S(2)}) collective-permute-start(f32[32,8,128]{2,1,0:T(8,128)S(1)} %get-tuple-element.63), channel_id=1, source_target_pairs={{0,1},{1,0},{2,3},{3,2},{4,5},{5,4},{6,7},{7,6},{8,9},{9,8},{10,11... | collective-permute-start | bytes 393224 | tf_op jit(solution)/shard_map/ppermute | solution.py:369
  71.0 5.9 %collective-permute-start.20 = (f32[32,8,128]{2,1,0:T(8,128)S(1)}, f32[32,8,128]{2,1,0:T(8,128)S(1)}, u32[]{:S(2)}, u32[]{:S(2)}) collective-permute-start(f32[32,8,128]{2,1,0:T(8,128)S(1)} %get-tuple-element.64), channel_id=1, source_target_pairs={{0,31},{1,2},{2,1},{3,4},{4,3},{5,6},{6,5},{7,8},{8,7},{9,10},{10,... | collective-permute-start | bytes 393224 | tf_op jit(solution)/shard_map/ppermute | solution.py:368
